TPU v7x, 32 devices: a whole 2x2x4 slice. The times are simulated.
32 devices in a mesh: tile: 8 (over z, x), mem: 4 (over y, core).
Axes of the slice: x: 2, y: 2, z: 4, core: 2. Of those that a mesh axis runs over, the one named last changes fastest.
Arguments:
- alpha: float32 [4, 16, 64, 1024], P('mem', None, None, 'tile'), may hold values from -6 to 6
- members: bfloat16 [4, 16, 64, 1024], P('mem', None, None, 'tile'), may hold values from -6 to 6
- mem_weight: float32 [4], P('mem'), may hold values from 0.5 to 2
- kappa: float32 [64, 1024], P(None, 'tile'), may hold values from 0.04 to 0.24
- norm_scale: float32 [64, 1024], P(None, 'tile'), may hold values from 0.8 to 1.25
- land_sea: int32 [64, 1024], P(None, 'tile'), may hold values 0 or 1
- obs_cell: int32 [16384], P('tile'), may hold values from 0 to 131071
- obs_weight: float32 [16384], P('tile'), may hold values from 0.5 to 4
Outputs:
- product: float32 [4, 16, 64, 1024], P('mem', None, None, 'tile')
Inputs may be any that keep to these rules, and one draw needn't show every extreme that they name: `obs_cell`: observations o of tile t = o // 2048 index a cell of that tile; several may share a cell.
All inputs are finite; a program needn't handle non-finite values. No bound on the sum of `land_sea` on one device may be relied on, other than what follows from the above.
Results may differ from a plain program's by a relative error of at most 0.0003.
Values sent between devices are 32-bit elements; how exact they have to be, the bound alone decides.
No kernel may reach another device: no remote copies, remote signals or barrier semaphores. Data moves between devices by JAX's collectives and lax.ppermute only.
A program may use at most 64 MiB of HBM per device.

v0:
```python
import jax
import jax.numpy as jnp
from jax import lax
from jax.sharding import PartitionSpec as P

STEPS = 8


def extended_2(value, sides, width):
    for axis, dim in sides:
        count, length = (lax.axis_size(axis), value.shape[dim])
        up = [(i, (i + 1) % count) for i in range(count)]
        down = [(j, i) for i, j in up]
        last = lax.slice_in_dim(value, length - width, length, axis=dim)
        first = lax.slice_in_dim(value, 0, width, axis=dim)
        before = lax.ppermute(last, axis, up)
        after = lax.ppermute(first, axis, down)
        value = jnp.concatenate([before, value, after], axis=dim)
    return value


def section(field, coeffs, forward):
    scaling, east, west, north, north_below = (
        coeffs[0],
        coeffs[1],
        coeffs[2],
        coeffs[3],
        coeffs[4],
    )
    if forward:
        field = scaling * field
    east_value = jnp.roll(field, -1, -1)
    west_value = jnp.roll(field, 1, -1)
    across = east * (east_value - field) - west * (field - west_value)
    along = north * (jnp.roll(field, -1, -2) - field) - north_below * (
        field - jnp.roll(field, 1, -2)
    )
    result = field + across + along
    if not forward:
        result = scaling * result
    return result


def sweep(field, coeffs, forward):
    strips = jnp.concatenate([field[..., :STEPS], field[..., -STEPS:]], -1)
    beside = extended_2(strips, (("tile", 3),), STEPS)
    extended = jnp.concatenate([beside[..., :STEPS], field, beside[..., -STEPS:]], -1)
    for step in range(STEPS):
        extended = section(extended, coeffs, forward)
    return extended[..., STEPS : extended.shape[-1] - STEPS]


def local(alpha, members, mem_weight, kappa, norm_scale, land_sea, obs_cell, obs_weight):
    margin = STEPS
    fields = jnp.stack([kappa, norm_scale, land_sea.astype(jnp.float32)])
    widened = extended_2(fields, (("tile", 2),), margin)
    diffusive, scaling, ocean = (widened[0], widened[1], widened[2])
    columns = alpha.shape[3]
    north = 0.5 * (diffusive + jnp.roll(diffusive, -1, 0)) * ocean * jnp.roll(ocean, -1, 0)
    row_index = lax.broadcasted_iota(jnp.int32, north.shape, 0)
    north = jnp.where(row_index == north.shape[0] - 1, 0.0, north)
    east = 0.5 * (diffusive + jnp.roll(diffusive, -1, 1)) * ocean * jnp.roll(ocean, -1, 1)
    west = jnp.roll(east, 1, 1)
    coeffs = (scaling, east, west, north, jnp.roll(north, 1, 0), None, None)
    levels, rows = (alpha.shape[1], alpha.shape[2])
    weights = mem_weight[:, None, None, None]
    smoothed = sweep(alpha, coeffs, True)
    partial_sum = jnp.sum(weights * members.astype(jnp.float32) * smoothed, axis=0)
    obs_field = (
        jnp.zeros((levels * rows * columns,), jnp.float32)
        .at[obs_cell]
        .add(obs_weight)
        .reshape(levels, rows, columns)
    )
    share = lax.psum_scatter(partial_sum, "mem", scatter_dimension=0, tiled=True)
    per_device = levels // lax.axis_size("mem")
    first = lax.axis_index("mem") * per_device
    weighted = lax.dynamic_slice_in_dim(obs_field, first, per_device, 0) * share
    gradient = lax.all_gather(weighted, "mem", axis=0, tiled=True)
    back = weights * members.astype(jnp.float32) * gradient[None]
    return alpha + sweep(back, coeffs, False)


def solution(mesh):
    placed = (
        P("mem", None, None, "tile"),
        P("mem", None, None, "tile"),
        P("mem"),
        P(None, "tile"),
        P(None, "tile"),
        P(None, "tile"),
        P("tile"),
        P("tile"),
    )
    return jax.shard_map(
        local, mesh=mesh, in_specs=placed, out_specs=P("mem", None, None, "tile"), check_vma=False
    )
```

profile of v0, /device:TPU:0, one launch (start us, length us, event | category | flops | bytes accessed | tf_op | source)
XLA Modules:
  0.0 133.2 jit_solution(15796390251148431253)
XLA Ops:
  6.5 0.8 convert_bitcast_fusion
  7.5 3.0 %collective-permute-start = (f32[3,64,8]{2,1,0:T(8,128)S(1)}, f32[3,64,8]{2,1,0:T(8,128)S(1)}, u32[]{:S(2)}, u32[]{:S(2)}) collective-permute-start(f32[3,64,8]{2,1,0:T(8,128)S(1)} %get-tuple-element.144), channel_id=1, source_target_pairs={{0,4},{4,8},{8,12},{12,16},{16,20},{20,24},{24,28},{28,0},{1,5},{5... | collective-permute-start | bytes 18440 | tf_op jit(solution)/shard_map/ppermute | solution.py:16
  10.5 3.1 %collective-permute-start.1 = (f32[3,64,8]{2,1,0:T(8,128)S(1)}, f32[3,64,8]{2,1,0:T(8,128)S(1)}, u32[]{:S(2)}, u32[]{:S(2)}) collective-permute-start(f32[3,64,8]{2,1,0:T(8,128)S(1)} %get-tuple-element.145), channel_id=1, source_target_pairs={{4,0},{8,4},{12,8},{16,12},{20,16},{24,20},{28,24},{0,28},{5,1},{9... | collective-permute-start | bytes 18440 | tf_op jit(solution)/shard_map/ppermute | solution.py:17
  13.9 4.7 %collective-permute-start.3 = (f32[1,16,64,8]{3,2,1,0:T(8,128)S(1)}, f32[1,16,64,8]{3,2,1,0:T(8,128)S(1)}, u32[]{:S(2)}, u32[]{:S(2)}) collective-permute-start(f32[1,16,64,8]{3,2,1,0:T(8,128)S(1)} %get-tuple-element.134), channel_id=1, source_target_pairs={{4,0},{8,4},{12,8},{16,12},{20,16},{24,20},{28,24},{0,28},{5,1},{9... | collective-permute-start | bytes 98312 | tf_op jit(solution)/shard_map/ppermute | solution.py:17
  20.3 17.0 %collective-permute-done.2 = f32[1,16,64,8]{3,2,1,0:T(8,128)S(1)} collective-permute-done((f32[1,16,64,8]{3,2,1,0:T(8,128)S(1)}, f32[1,16,64,8]{3,2,1,0:T(8,128)S(1)}, u32[]{:S(2)}, u32[]{:S(2)}) %collective-permute-start.2) | collective-permute-done | bytes 32800 | tf_op jit(solution)/shard_map/ppermute | solution.py:16
  37.3 2.4 %collective-permute-done.3 = f32[1,16,64,8]{3,2,1,0:T(8,128)S(1)} collective-permute-done((f32[1,16,64,8]{3,2,1,0:T(8,128)S(1)}, f32[1,16,64,8]{3,2,1,0:T(8,128)S(1)}, u32[]{:S(2)}, u32[]{:S(2)}) %collective-permute-start.3) | collective-permute-done | bytes 32800 | tf_op jit(solution)/shard_map/ppermute | solution.py:17
  39.7 0.5 maximum_multiply_fusion
  40.4 0.4 fusion.227
  40.7 0.2 fusion.226
  41.0 0.9 fusion.4
  42.1 0.4 fusion.223
  42.4 0.2 fusion.222
  42.7 0.9 fusion.13
  43.7 0.4 fusion.219
  44.1 0.2 fusion.218
  44.3 0.9 fusion.22
  45.4 0.4 fusion.215
  45.8 0.2 fusion.214
  46.0 0.9 fusion.31
  47.1 0.4 fusion.211
  47.5 0.2 fusion.210
  47.7 0.9 fusion.40
  48.8 0.4 fusion.207
  49.1 0.2 fusion.206
  49.4 0.9 fusion.49
  50.5 0.4 fusion.203
  50.8 0.2 fusion.202
  51.1 0.9 fusion.58
  51.9 0.5 fusion.197
  52.9 0.7 copy-done.1
  53.6 1.8 %fusion.147 = f32[16,64,128]{2,1,0:T(8,128)} fusion(f32[1,16,1,144]{3,2,1,0:T(1,128)S(1)} %get-tuple-element.72, f32[1,16,63,144]{3,2,1,0:T(8,128)S(1)} %get-tuple-element.74, f32[1,16,63,144]{3,2,1,0:T(8,128)S(1)} %get-tuple-element.73, f32[1,16,1,144]{3,2,1,0:T(1,128)S(1)} %get-tuple-element.71, f32[1,16,64,1]{3,2,1,0:T(8,128)S(1)} %get-tuple-element.68, ...), kind=kLoop, calls=%fused_computation.213 | loop fusion | flops 2490368 | bytes 3801092 | tf_op jit(solution)/shard_map/reduce_sum | solution.py:68
  55.4 0.7 copy-done.4
  56.1 11.5 %scatter_custom_fusion = f32[131072]{0:T(1024)S(1)} fusion(s32[2048]{0:T(1024)S(1)} %compare_select_fusion, f32[2048]{0:T(1024)} %param.15, f32[]{:T(128)} %constant.8.clone.1), kind=kCustom, calls=%fused_computation.227 | custom fusion | flops 2048 | bytes 524800 | tf_op jit(solution)/shard_map/scatter-add | solution.py:72
  67.7 9.3 %reduce-scatter.2.cloned.1.call-done = f32[4,64,128]{2,1,0:T(8,128)} async-done(((f32[16,64,128]{2,1,0:T(8,128)}), f32[4,64,128]{2,1,0:T(8,128)}) %reduce-scatter.2.cloned.1.call-update) | async-done | bytes 131088 | tf_op jit(solution)/shard_map/reduce_scatter | solution.py:75
  77.0 0.9 dynamic-slice_multiply_fusion
  77.9 6.6 %all_gather.3 = f32[16,64,128]{2,1,0:T(8,128)S(1)} all-gather(f32[4,64,128]{2,1,0:T(8,128)S(1)} %dynamic-slice_multiply_fusion), channel_id=1, replica_groups=mesh['tile'=8,'mem'=4] {'mem'}, dimensions={0}, use_global_device_ids=true | all-gather | bytes 655360 | tf_op jit(solution)/shard_map/all_gather | solution.py:79
  84.6 0.2 fusion.228
  84.8 1.5 %collective-permute-start.4 = (f32[1,16,64,8]{3,2,1,0:T(8,128)S(1)}, f32[1,16,64,8]{3,2,1,0:T(8,128)S(1)}, u32[]{:S(2)}, u32[]{:S(2)}) collective-permute-start(f32[1,16,64,8]{3,2,1,0:T(8,128)S(1)} %get-tuple-element.131), channel_id=1, source_target_pairs={{0,4},{4,8},{8,12},{12,16},{16,20},{20,24},{24,28},{28,0},{1,5},{5... | collective-permute-start | bytes 98312 | tf_op jit(solution)/shard_map/ppermute | solution.py:16
  86.3 3.3 %collective-permute-start.5 = (f32[1,16,64,8]{3,2,1,0:T(8,128)S(1)}, f32[1,16,64,8]{3,2,1,0:T(8,128)S(1)}, u32[]{:S(2)}, u32[]{:S(2)}) collective-permute-start(f32[1,16,64,8]{3,2,1,0:T(8,128)S(1)} %get-tuple-element.132), channel_id=1, source_target_pairs={{4,0},{8,4},{12,8},{16,12},{20,16},{24,20},{28,24},{0,28},{5,1},{9... | collective-permute-start | bytes 98312 | tf_op jit(solution)/shard_map/ppermute | solution.py:17
  89.7 19.6 %collective-permute-done.4 = f32[1,16,64,8]{3,2,1,0:T(8,128)S(1)} collective-permute-done((f32[1,16,64,8]{3,2,1,0:T(8,128)S(1)}, f32[1,16,64,8]{3,2,1,0:T(8,128)S(1)}, u32[]{:S(2)}, u32[]{:S(2)}) %collective-permute-start.4) | collective-permute-done | bytes 32800 | tf_op jit(solution)/shard_map/ppermute | solution.py:16
  109.2 2.2 %collective-permute-done.5 = f32[1,16,64,8]{3,2,1,0:T(8,128)S(1)} collective-permute-done((f32[1,16,64,8]{3,2,1,0:T(8,128)S(1)}, f32[1,16,64,8]{3,2,1,0:T(8,128)S(1)}, u32[]{:S(2)}, u32[]{:S(2)}) %collective-permute-start.5) | collective-permute-done | bytes 32800 | tf_op jit(solution)/shard_map/ppermute | solution.py:17
  111.4 0.5 pad_maximum_fusion
  112.1 0.4 fusion.195
  112.7 1.0 fusion.67
  113.9 0.4 fusion.192
  114.3 0.2 fusion.191
  114.6 0.8 fusion.76
  115.6 0.4 fusion.188
  116.0 0.2 fusion.187
  116.2 0.9 fusion.85
  117.3 0.4 fusion.184
  117.7 0.2 fusion.183
  117.9 0.9 fusion.94
  119.0 0.4 fusion.180
  119.3 0.2 fusion.179
  119.6 0.9 fusion.103
  120.7 0.4 fusion.176
  121.0 0.2 fusion.175
  121.3 0.9 fusion.112
  122.3 0.4 fusion.172
  122.7 0.2 fusion.171
  122.9 0.9 fusion.121
  123.8 0.4 fusion.168
  124.6 1.7 %fusion.133 = f32[1,16,64,128]{3,2,1,0:T(8,128)} fusion(f32[1,16,64,128]{3,2,1,0:T(8,128)S(1)} %copy-done, f32[1,16,64,1]{3,2,1,0:T(8,128)S(1)} %get-tuple-element.10, f32[1,16,64,143]{3,2,1,0:T(8,128)S(1)} %get-tuple-element.12, f32[1,16,64,143]{3,2,1,0:T(8,128)S(1)} %get-tuple-element.11, f32[1,16,64,1]{3,2,1,0:T(8,128)S(1)} %get-tuple-element.9, ...), kind=kLoop, calls=%fused_computation.196 | loop fusion | flops 2359296 | bytes 4096000 | tf_op jit(solution)/shard_map/add | solution.py:81
  (71 shorter events, 5.8 us)
Async XLA Ops:
  6.5 0.8 copy-start.3
  6.5 0.8 copy-start.2
  6.5 7.1 %copy-start = (f32[1,16,64,128]{3,2,1,0:T(8,128)S(1)}, f32[1,16,64,128]{3,2,1,0:T(8,128)}, u32[]{:S(2)}) copy-start(f32[1,16,64,128]{3,2,1,0:T(8,128)} %param.8) | copy-start | bytes 1572868
  6.5 70.4 %reduce-scatter.2.cloned.1.call-start = ((), (), s32[]{:S(2)}) async-start(), calls=%async_computation.1 | async-start | bytes 655360 | tf_op jit(solution)/shard_map/reduce_scatter | solution.py:75
  7.5 11.8 %collective-permute-start = (f32[3,64,8]{2,1,0:T(8,128)S(1)}, f32[3,64,8]{2,1,0:T(8,128)S(1)}, u32[]{:S(2)}, u32[]{:S(2)}) collective-permute-start(f32[3,64,8]{2,1,0:T(8,128)S(1)} %get-tuple-element.144), channel_id=1, source_target_pairs={{0,4},{4,8},{8,12},{12,16},{16,20},{20,24},{24,28},{28,0},{1,5},{5... | collective-permute-start | bytes 18440 | tf_op jit(solution)/shard_map/ppermute | solution.py:16
  10.5 8.8 %collective-permute-start.1 = (f32[3,64,8]{2,1,0:T(8,128)S(1)}, f32[3,64,8]{2,1,0:T(8,128)S(1)}, u32[]{:S(2)}, u32[]{:S(2)}) collective-permute-start(f32[3,64,8]{2,1,0:T(8,128)S(1)} %get-tuple-element.145), channel_id=1, source_target_pairs={{4,0},{8,4},{12,8},{16,12},{20,16},{24,20},{28,24},{0,28},{5,1},{9... | collective-permute-start | bytes 18440 | tf_op jit(solution)/shard_map/ppermute | solution.py:17
  13.8 23.5 %collective-permute-start.2 = (f32[1,16,64,8]{3,2,1,0:T(8,128)S(1)}, f32[1,16,64,8]{3,2,1,0:T(8,128)S(1)}, u32[]{:S(2)}, u32[]{:S(2)}) collective-permute-start(f32[1,16,64,8]{3,2,1,0:T(8,128)S(1)} %get-tuple-element.133), channel_id=1, source_target_pairs={{0,4},{4,8},{8,12},{12,16},{16,20},{20,24},{24,28},{28,0},{1,5},{5... | collective-permute-start | bytes 98312 | tf_op jit(solution)/shard_map/ppermute | solution.py:16
  13.9 25.8 %collective-permute-start.3 = (f32[1,16,64,8]{3,2,1,0:T(8,128)S(1)}, f32[1,16,64,8]{3,2,1,0:T(8,128)S(1)}, u32[]{:S(2)}, u32[]{:S(2)}) collective-permute-start(f32[1,16,64,8]{3,2,1,0:T(8,128)S(1)} %get-tuple-element.134), channel_id=1, source_target_pairs={{4,0},{8,4},{12,8},{16,12},{20,16},{24,20},{28,24},{0,28},{5,1},{9... | collective-permute-start | bytes 98312 | tf_op jit(solution)/shard_map/ppermute | solution.py:17
  52.7 1.0 copy-start.1
  55.4 0.7 copy-start.4
  84.8 24.4 %collective-permute-start.4 = (f32[1,16,64,8]{3,2,1,0:T(8,128)S(1)}, f32[1,16,64,8]{3,2,1,0:T(8,128)S(1)}, u32[]{:S(2)}, u32[]{:S(2)}) collective-permute-start(f32[1,16,64,8]{3,2,1,0:T(8,128)S(1)} %get-tuple-element.131), channel_id=1, source_target_pairs={{0,4},{4,8},{8,12},{12,16},{16,20},{20,24},{24,28},{28,0},{1,5},{5... | collective-permute-start | bytes 98312 | tf_op jit(solution)/shard_map/ppermute | solution.py:16
  86.3 25.1 %collective-permute-start.5 = (f32[1,16,64,8]{3,2,1,0:T(8,128)S(1)}, f32[1,16,64,8]{3,2,1,0:T(8,128)S(1)}, u32[]{:S(2)}, u32[]{:S(2)}) collective-permute-start(f32[1,16,64,8]{3,2,1,0:T(8,128)S(1)} %get-tuple-element.132), channel_id=1, source_target_pairs={{4,0},{8,4},{12,8},{16,12},{20,16},{24,20},{28,24},{0,28},{5,1},{9... | collective-permute-start | bytes 98312 | tf_op jit(solution)/shard_map/ppermute | solution.py:17
Sparse Core Ops, SparseCore 0:
  55.5 21.3 reduce-scatter.1
where the time goes:
time: 133 us
  waiting for transfers between devices  50.5 us (38%)
  other arithmetic  30.3 us (23%)
  starting transfers between devices  15.7 us (12%)
  local copies, waits for them, and re-layouts  15.5 us (12%)
  between operations  14.6 us (11%)
  blocking collectives  6.61 us (5%)
    ppermute x3, waiting for transfers between devices, extended_2(): before = lax.ppermute(last, axis, up)  36.6 us
    scatter-add x1, other arithmetic, local(): obs_field = jnp.zeros((levels * rows * columns,), jnp.float32).at[obs_cel...  11.5 us
    ppermute x3, starting transfers between devices, extended_2(): after = lax.ppermute(first, axis, down)  11.1 us
    reduce_scatter x1, waiting for transfers between devices, local(): lax.psum_scatter(partial_sum, 'mem', scatter_dimension=0, tiled=True)  9.3 us
    slice x30, local copies, waits for them, and re-layouts, section(): west_value = jnp.roll(field, 1, -1)  8.72 us
    all_gather x1, blocking collectives, local(): gradient = lax.all_gather(weighted, 'mem', axis=0, tiled=True)  6.61 us
    mul x8, other arithmetic, section(): field = scaling * field  6.44 us
    mul x7, other arithmetic, section(): result = scaling * result  6.13 us
  transfers between devices with their start and end apart: 7, of which 5 were waited for; matrix products, arithmetic and copies ran while one was open for 10% of the time, Pallas kernels for 0%

commit v1 on v0

v1 whole, which is shorter than its diff:
```python
import functools

import jax
import jax.numpy as jnp
from jax import lax
from jax.experimental import pallas as pl
from jax.experimental.pallas import tpu as pltpu
from jax.sharding import PartitionSpec as P

STEPS = 8
SUB = 8
EDGE = 2 * STEPS
F32 = jnp.float32
BF16 = jnp.bfloat16


def div_mod(value, size):
    if size & (size - 1) == 0:
        return value >> (size.bit_length() - 1), value & (size - 1)
    return lax.div(value, size), lax.rem(value, size)


def roll(value, shift, axis=1):
    shift %= value.shape[axis]
    return pltpu.roll(value, shift, axis) if shift else value


def lanes(shape=(SUB, 128)):
    return lax.broadcasted_iota(jnp.int32, shape, len(shape) - 1)


def split(value):
    high = value.astype(BF16)
    return high, (value - high.astype(F32)).astype(BF16)


class Sizes:
    def __init__(self, levels, rows, columns, obs):
        self.levels, self.rows, self.columns, self.obs = levels, rows, columns, obs
        self.groups = levels // SUB
        self.half = rows // 2
        assert columns == 128 and self.groups == 2 and rows % 16 == 0
        assert levels % SUB == 0 and obs % 256 == 0 and STEPS == 8
        self.tall = rows * SUB
        self.at_coeff = self.half * SUB
        self.at_obs = self.at_coeff + self.half
        self.obs_rows = obs // 128
        self.payload = self.at_obs + 2 * self.obs_rows
        self.quarter = rows // 4
        self.short = self.quarter * SUB


def level_rows(z, group, row):
    return pl.ds(group * SUB * z.rows + row, SUB, stride=z.rows)


def pack_kernel(z, alpha, members, kappa, scale, ocean, cell, weight, out_a, out_b, wide):
    even = lax.rem(lax.axis_index("tile"), 2) == 0
    wide[...] = members[...].astype(F32)
    lane = lanes()

    def put(where, right, left):
        out_a[where, :] = jnp.where(even, right, left)
        out_b[where, :] = jnp.where(even, left, right)

    for q in range(z.half):
        right = left = None
        for h in range(2):
            for g in range(2):
                rows = level_rows(z, g, q + h * z.half)
                a, m = alpha[rows, :], wide[rows, :]
                base = 64 * g + 32 * h
                r_part = roll(jnp.where(lane >= 128 - EDGE, a, roll(m, -EDGE)), base - (128 - 2 * EDGE))
                l_part = roll(jnp.where(lane < EDGE, m, roll(a, EDGE)), base)
                if right is None:
                    right, left = r_part, l_part
                else:
                    here = (lane >= base) & (lane < base + 32)
                    right, left = jnp.where(here, r_part, right), jnp.where(here, l_part, left)
        put(pl.ds(q * SUB, SUB), right, left)
    lane = lanes((z.half, 128))
    right = left = None
    for h in range(2):
        rows = pl.ds(h * z.half, z.half)
        for k, ref in enumerate((kappa, scale, ocean)):
            value = ref[rows, :].astype(F32)
            base = 64 * h + EDGE * k
            r_part, l_part = roll(value, base - (128 - EDGE)), roll(value, base)
            if right is None:
                right, left = r_part, l_part
            else:
                here = (lane >= base) & (lane < base + EDGE)
                right, left = jnp.where(here, r_part, right), jnp.where(here, l_part, left)
    put(pl.ds(z.at_coeff, z.half), right, left)
    n = z.obs_rows
    for at, value in ((z.at_obs, cell[...].astype(F32)), (z.at_obs + n, weight[...])):
        out_a[pl.ds(at, n), :] = value
        out_b[pl.ds(at, n), :] = value


def up(value):
    return roll(value, -1, 0)


def down(value):
    return roll(value, 1, 0)


def coefficients(kappa, scale, ocean, forward):
    row = lax.broadcasted_iota(jnp.int32, kappa.shape, 0)
    north = 0.5 * (kappa + up(kappa)) * ocean * up(ocean)
    north = jnp.where(row == kappa.shape[0] - 1, 0.0, north)
    east = 0.5 * (kappa + roll(kappa, -1)) * ocean * roll(ocean, -1)
    west, south = roll(east, 1), down(north)
    centre = 1.0 - (east + west) - (north + south)
    if forward:
        return (
            centre * scale,
            east * roll(scale, -1),
            west * roll(scale, 1),
            north * up(scale),
            south * down(scale),
        )
    return tuple(scale * c for c in (centre, east, west, north, south))


def put_coefficients(ref, values):
    rows = values[0].shape[0]
    for k, value in enumerate(values):
        for r in range(rows):
            ref[k, pl.ds(r * SUB, SUB), :] = jnp.broadcast_to(value[r : r + 1, :], (SUB, value.shape[1]))


def step_rows(x, coeff, rows, blocks):
    at = lambda r, b: (pl.ds(r * SUB, SUB), pl.ds(b * 128, 128))
    before = [None] * blocks
    here = [x[at(0, b)] for b in range(blocks)]
    for r in range(rows):
        c = [coeff[k, pl.ds(r * SUB, SUB), :] for k in range(5)]
        for b in range(blocks):
            u = here[b]
            new = c[0] * u + (c[1] * roll(u, -1) + c[2] * roll(u, 1))
            after = x[at(r + 1, b)] if r + 1 < rows else None
            if after is not None:
                new = new + c[3] * after
            if before[b] is not None:
                new = new + c[4] * before[b]
            x[at(r, b)] = new
            before[b], here[b] = u, after


def main_kernel(z, alpha, members, weight, kappa, scale, ocean, out, coeff, wide):
    wide[...] = members[...].astype(F32) * weight[0]
    put_coefficients(coeff, coefficients(kappa[...], scale[...], ocean[...].astype(F32), True))
    for r in range(z.rows):
        for g in range(2):
            out[pl.ds(r * SUB, SUB), pl.ds(128 * g, 128)] = alpha[level_rows(z, g, r), :]

    def step(_, carry):
        step_rows(out, coeff, z.rows, 2)
        return carry

    lax.fori_loop(0, STEPS, step, 0)
    for r in range(z.rows):
        for g in range(2):
            at = (pl.ds(r * SUB, SUB), pl.ds(128 * g, 128))
            out[at] = out[at] * wide[level_rows(z, g, r), :]


def own_index(z, cell):
    level, rest = div_mod(cell, z.rows * z.columns)
    row, column = div_mod(rest, z.columns)
    return row * SUB + (level & (SUB - 1)), (level >> 3) * 128 + column


def beside_index(z, cell, left):
    level, rest = div_mod(cell, z.rows * z.columns)
    row, column = div_mod(rest, z.columns)
    quarter, row = div_mod(row, z.quarter)
    first = z.columns - STEPS if left else 0
    inside = (column >= first) & (column < first + STEPS)
    lane = (40 if left else 16) + (column - first) + 64 * (level >> 3) + 16 * quarter
    return jnp.where(inside, row * SUB + (level & (SUB - 1)), -1), lane & 127


def quarter_mask(lane, k):
    unit = lane >> 3
    return (((unit & 1) == 0) & ((((unit - 2) >> 1) & 3) == k)) | (
        ((unit & 1) == 1) & ((((unit - 5) >> 1) & 3) == k)
    )


def one_hot(index, size):
    rows = lax.broadcasted_iota(jnp.int32, (size, index.shape[1]), 0)
    return jnp.where(rows == index, 1.0, 0.0).astype(BF16)


def read_off(field_high, field_low, i, j):
    hot = one_hot(i, field_high.shape[0])
    dims = (((0,), (0,)), ((), ()))
    value = lax.dot_general(field_high, hot, dims, preferred_element_type=F32)
    value = value + lax.dot_general(field_low, hot, dims, preferred_element_type=F32)
    rows = lax.broadcasted_iota(jnp.int32, value.shape, 0)
    return jnp.sum(jnp.where(rows == j, value, 0.0), axis=0, keepdims=True)


CHUNK = 256


def strip_kernel(z, main, sent_a, sent_b, got_a, got_b, cell, weight, out, strip_members, strip_coeff, x, coeff, beside, merged):
    even = lax.rem(lax.axis_index("tile"), 2) == 0
    lane = lanes()

    def parts(rows):
        sa, sb, ga, gb = sent_a[rows, :], sent_b[rows, :], got_a[rows, :], got_b[rows, :]
        pick = lambda p, q: jnp.where(even, p, q)
        return pick(sa, sb), pick(ga, gb), pick(gb, ga), pick(sb, sa)

    for q in range(z.half):
        four = parts(pl.ds(q * SUB, SUB))
        for h in range(2):
            at = pl.ds((q + h * z.half) * SUB, SUB)
            for ref, offset in ((strip_members, 0), (x, -EDGE)):
                value = None
                for p, part in enumerate(four):
                    piece = roll(part, EDGE * p - 32 * h + offset)
                    value = piece if p == 0 else jnp.where(((lane >> 4) & 3) == p, piece, value)
                ref[at, :] = value * weight[0] if offset == 0 else value
    four = parts(pl.ds(z.at_coeff, z.half))
    lane = lanes((z.half, 128))
    for k in range(3):
        for h in range(2):
            value = None
            for g in range(2):
                for p, part in enumerate(four):
                    piece = roll(part, EDGE * p + 64 * g - 64 * h - EDGE * k)
                    value = piece if value is None else jnp.where((lane >> 4) == 4 * g + p, piece, value)
            strip_coeff[k, pl.ds(h * z.half, z.half), :] = value
    put_coefficients(coeff, coefficients(strip_coeff[0], strip_coeff[1], strip_coeff[2], True))

    def step(_, carry):
        step_rows(x, coeff, z.rows, 1)
        return carry

    lax.fori_loop(0, STEPS, step, 0)
    lane = lanes()
    for r in range(z.rows):
        at = pl.ds(r * SUB, SUB)
        value = x[at, :] * strip_members[at, :]
        x[at, :] = value
        for g in range(2):
            here = (at, pl.ds(128 * g, 128))
            fixed = jnp.where(lane >= z.columns - STEPS, roll(value, 112 - 64 * g), main[here])
            merged[here] = jnp.where(lane < STEPS, roll(value, -48 - 64 * g), fixed)
    for q in range(z.quarter):
        value = None
        for k in range(4):
            piece = roll(x[pl.ds((k * z.quarter + q) * SUB, SUB), :], 16 * k)
            value = piece if k == 0 else jnp.where(quarter_mask(lane, k), piece, value)
        beside[pl.ds(q * SUB, SUB), :] = value

    def gather(at, index, high, low, i_j):
        for n in range(z.obs_rows // 2):
            row = jnp.concatenate([index[2 * n : 2 * n + 1, :], index[2 * n + 1 : 2 * n + 2, :]], axis=1)
            value = read_off(high, low, *i_j(row))
            out[at + 2 * n : at + 2 * n + 1, :] = value[:, :128]
            out[at + 2 * n + 1 : at + 2 * n + 2, :] = value[:, 128:]

    high, low = split(merged[...])
    gather(0, cell[...], high, low, lambda c: own_index(z, c))
    high, low = split(beside[...])
    rows = pl.ds(z.at_obs, z.obs_rows)
    _, right, left, _ = parts(rows)
    gather(z.obs_rows, right.astype(jnp.int32), high, low, lambda c: beside_index(z, c, False))
    gather(2 * z.obs_rows, left.astype(jnp.int32), high, low, lambda c: beside_index(z, c, True))


def adjoint_kernel(
    z, alpha, members, weight, kappa, scale, ocean, cell, obs_weight, got_a, got_b, strip_members, strip_coeff,
    v0, v1, v2, v3, out, x, coeff, strip, strip_c, beside, wide, hot, spread,
):
    even = lax.rem(lax.axis_index("tile"), 2) == 0
    lane = lanes()
    wide[...] = members[...].astype(F32) * weight[0]
    put_coefficients(coeff, coefficients(kappa[...], scale[...], ocean[...].astype(F32), False))
    put_coefficients(strip_c, coefficients(strip_coeff[0], strip_coeff[1], strip_coeff[2], False))
    value = (v0[...] + v1[...]) + (v2[...] + v3[...])
    n = z.obs_rows
    pick = lambda p, q: jnp.where(even, p, q)
    cells, weights = pl.ds(z.at_obs, n), pl.ds(z.at_obs + n, n)
    right = pick(got_a[cells, :], got_b[cells, :]).astype(jnp.int32)
    left = pick(got_b[cells, :], got_a[cells, :]).astype(jnp.int32)
    right_weight = pick(got_a[weights, :], got_b[weights, :])
    left_weight = pick(got_b[weights, :], got_a[weights, :])

    def spread_out(groups, tall, wide_):
        at = 0
        for index, amount, i_j in groups:
            for r in range(n):
                i, j = i_j(index[r : r + 1, :])
                hot[:tall, pl.ds(at * 128, 128)] = one_hot(i, tall)
                rows = lax.broadcasted_iota(jnp.int32, (wide_, 128), 0)
                high, low = split(jnp.where(rows == j, amount[r : r + 1, :], 0.0))
                spread[:wide_, pl.ds(at * 128, 128)] = high
                spread[pl.ds(wide_, wide_), pl.ds(at * 128, 128)] = low
                at += 1
        dims = (((1,), (1,)), ((), ()))
        value = lax.dot_general(hot[:tall, : at * 128], spread[: 2 * wide_, : at * 128], dims, preferred_element_type=F32)
        return value[:, :wide_] + value[:, wide_:]

    x[...] = spread_out([(cell[...], obs_weight[...] * value[:n], lambda c: own_index(z, c))], z.tall, 256)
    beside[...] = spread_out(
        [
            (right, right_weight * value[n : 2 * n], lambda c: beside_index(z, c, False)),
            (left, left_weight * value[2 * n :], lambda c: beside_index(z, c, True)),
        ],
        z.short,
        128,
    )
    part = (lane >> 4) & 3
    within = lane & 15
    outer = ((part == 1) & (within < STEPS)) | ((part == 2) & (within >= STEPS))
    for r in range(z.rows):
        at = pl.ds(r * SUB, SUB)
        k, q = divmod(r, z.quarter)
        value = jnp.where(outer, roll(beside[pl.ds(q * SUB, SUB), :], -16 * k), 0.0)
        for g in range(2):
            here = (at, pl.ds(128 * g, 128))
            field = x[here]
            mine = (lane >> 6) == g
            value = jnp.where(mine & (part == 0), roll(field, EDGE + 64 * g), value)
            value = jnp.where(mine & (part == 3), roll(field, 48 + 64 * g), value)
            x[here] = field * wide[level_rows(z, g, r), :]
        strip[at, :] = value * strip_members[at, :]

    def step(_, carry):
        step_rows(x, coeff, z.rows, 2)
        step_rows(strip, strip_c, z.rows, 1)
        return carry

    lax.fori_loop(0, STEPS, step, 0)
    for r in range(z.rows):
        at = pl.ds(r * SUB, SUB)
        value = strip[at, :]
        for g in range(2):
            fixed = jnp.where(lane >= z.columns - STEPS, roll(value, 112 - 64 * g), x[at, pl.ds(128 * g, 128)])
            fixed = jnp.where(lane < STEPS, roll(value, -48 - 64 * g), fixed)
            rows = level_rows(z, g, r)
            out[rows, :] = alpha[rows, :] + fixed


def local(alpha, members, mem_weight, kappa, norm_scale, land_sea, obs_cell, obs_weight):
    shape = alpha.shape
    z = Sizes(shape[1], shape[2], shape[3], obs_cell.shape[0])
    tiles, holders = lax.axis_size("tile"), lax.axis_size("mem")
    assert tiles % 2 == 0 and holders == 4 and shape[0] == 1
    alpha = alpha.reshape(z.levels * z.rows, z.columns)
    members = members.reshape(z.levels * z.rows, z.columns)
    cell = obs_cell.reshape(z.obs_rows, 128)
    weight = obs_weight.reshape(z.obs_rows, 128)
    smem = pl.BlockSpec(memory_space=pltpu.SMEM)
    whole = pl.BlockSpec(memory_space=pltpu.VMEM)
    sds = jax.ShapeDtypeStruct
    field = pltpu.VMEM((z.levels * z.rows, z.columns), F32)
    coeff = pltpu.VMEM((5, z.tall, 128), F32)
    payload = sds((z.payload, 128), F32)
    sent_a, sent_b = pl.pallas_call(
        functools.partial(pack_kernel, z),
        out_shape=(payload, payload),
        scratch_shapes=[field],
        name="pack",
    )(alpha, members, kappa, norm_scale, land_sea, cell, weight)
    near = [(i, i ^ 1) for i in range(tiles)]
    far = [(i, (i + 1) % tiles if i % 2 else (i - 1) % tiles) for i in range(tiles)]
    got_a = lax.ppermute(sent_a, "tile", near)
    got_b = lax.ppermute(sent_b, "tile", far)
    main = pl.pallas_call(
        functools.partial(main_kernel, z),
        out_shape=sds((z.tall, 256), F32),
        in_specs=[whole, whole, smem, whole, whole, whole],
        scratch_shapes=[coeff, field],
        name="main",
    )(alpha, members, mem_weight, kappa, norm_scale, land_sea)
    values, strip_members, strip_coeff = pl.pallas_call(
        functools.partial(strip_kernel, z),
        out_shape=(sds((3 * z.obs_rows, 128), F32), sds((z.tall, 128), F32), sds((3, z.rows, 128), F32)),
        in_specs=[whole] * 6 + [smem],
        scratch_shapes=[
            pltpu.VMEM((z.tall, 128), F32),
            coeff,
            pltpu.VMEM((z.short, 128), F32),
            pltpu.VMEM((z.tall, 256), F32),
        ],
        name="strip",
    )(main, sent_a, sent_b, got_a, got_b, cell, mem_weight)
    others = [lax.ppermute(values, "mem", [(i, i ^ k) for i in range(holders)]) for k in range(1, holders)]
    product = pl.pallas_call(
        functools.partial(adjoint_kernel, z),
        out_shape=sds((z.levels * z.rows, z.columns), F32),
        in_specs=[whole, whole, smem] + [whole] * 13,
        scratch_shapes=[
            pltpu.VMEM((z.tall, 256), F32),
            coeff,
            pltpu.VMEM((z.tall, 128), F32),
            coeff,
            pltpu.VMEM((z.short, 128), F32),
            field,
            pltpu.VMEM((z.tall, 2 * z.obs), BF16),
            pltpu.VMEM((512, 2 * z.obs), BF16),
        ],
        name="adjoint",
    )(alpha, members, mem_weight, kappa, norm_scale, land_sea, cell, weight, got_a, got_b, strip_members, strip_coeff, values, *others)
    return product.reshape(shape)


def solution(mesh):
    placed = (
        P("mem", None, None, "tile"),
        P("mem", None, None, "tile"),
        P("mem"),
        P(None, "tile"),
        P(None, "tile"),
        P(None, "tile"),
        P("tile"),
        P("tile"),
    )
    return jax.shard_map(
        local, mesh=mesh, in_specs=placed, out_specs=P("mem", None, None, "tile"), check_vma=False
    )
```

time: 133 us -> 43 us (0.32)
  waiting for transfers between devices: 50.5 us -> 2.58 us
  other arithmetic: 30.3 us -> 0 us
  Pallas kernels: 0 us -> 29.2 us
  between operations: 14.6 us -> 0.67 us
  local copies, waits for them, and re-layouts: 15.5 us -> 1.92 us
  starting transfers between devices: 15.7 us -> 8.4 us
  blocking collectives: 6.61 us -> 0 us
    ppermute x6 -> x5, waiting for transfers between devices: 41.2 us -> 2.58 us  [the longest x3 2.57 us: local(): lax.ppermute(values, 'mem', [(i, i ^ k) for i in range(holders)])]
    pallas_call x0 -> x4, Pallas kernels: none -> 29.2 us  [the longest x1 10.5 us: local(): pl.pallas_call(functools.partial(adjoint_kernel, z), out_shape=sds((z.lev...]
    slice x78 -> x0, local copies, waits for them, and re-layouts: 14.1 us -> none  [the longest x30 8.72 us: section(): west_value = jnp.roll(field, 1, -1)]
    mul x18 -> x0, other arithmetic: 13.7 us -> none  [the longest x8 6.44 us: section(): field = scaling * field]
    scatter-add x1 -> x0, other arithmetic: 11.5 us -> none  [local(): obs_field = jnp.zeros((levels * rows * columns,), jnp.float32).at[obs_cel...]
    reduce_scatter x1 -> x0, waiting for transfers between devices: 9.3 us -> none  [local(): lax.psum_scatter(partial_sum, 'mem', scatter_dimension=0, tiled=True)]
    ppermute x6 -> x5, starting transfers between devices: 15.7 us -> 8.4 us  [the longest x1 3.57 us: local(): got_b = lax.ppermute(sent_b, 'tile', far)]
    all_gather x1 -> x0, blocking collectives: 6.61 us -> none  [local(): gradient = lax.all_gather(weighted, 'mem', axis=0, tiled=True)]
  transfers between devices with their start and end apart: 7 -> 5, of which waited for: 5 -> 2; matrix products, arithmetic and copies ran while one was open for 10% -> 0% of each run, Pallas kernels for 0% -> 13%
where the time goes in v1:
time: 43 us; the launch traced here: 42.7 us
  Pallas kernels  29.2 us (68%)
  starting transfers between devices  8.4 us (20%)
  waiting for transfers between devices  2.58 us (6%)
  local copies, waits for them, and re-layouts  1.92 us (4%)
  between operations  0.67 us (2%)
    pallas_call x1, Pallas kernels, local(): pl.pallas_call(functools.partial(adjoint_kernel, z), out_shape=sds((z.lev...  10.5 us
    pallas_call x1, Pallas kernels, local(): pl.pallas_call(functools.partial(strip_kernel, z), out_shape=(sds((3 * z....  7.18 us
    pallas_call x1, Pallas kernels, local(): pl.pallas_call(functools.partial(pack_kernel, z), out_shape=(payload, pay...  5.98 us
    pallas_call x1, Pallas kernels, local(): pl.pallas_call(functools.partial(main_kernel, z), out_shape=sds((z.tall,...  5.49 us
    ppermute x1, starting transfers between devices, local(): got_b = lax.ppermute(sent_b, 'tile', far)  3.57 us
    ppermute x1, starting transfers between devices, local(): got_a = lax.ppermute(sent_a, 'tile', near)  2.97 us
    ppermute x3, waiting for transfers between devices, local(): lax.ppermute(values, 'mem', [(i, i ^ k) for i in range(holders)])  2.57 us
    unnamed x10, local copies, waits for them, and re-layouts  1.92 us
  transfers between devices with their start and end apart: 5, of which 2 were waited for; matrix products, arithmetic and copies ran while one was open for 0% of the time, Pallas kernels for 13%

profile of v1, /device:TPU:0, one launch (start us, length us, event | category | flops | bytes accessed | tf_op | source)
XLA Modules:
  0.0 42.7 jit_solution(3520660518939895269)
XLA Ops:
  0.0 6.0 %pack.1 = (f32[320,128]{1,0:T(8,128)}, f32[320,128]{1,0:T(8,128)}) custom-call(f32[1024,128]{1,0:T(8,128)} %bitcast.5, bf16[1024,128]{1,0:T(8,128)(2,1)} %bitcast.8, f32[64,128]{1,0:T(8,128)} %kappa.5, f32[64,128]{1,0:T(8,128)} %scale.5, s32[64,128]{1,0:T(8,128)} %ocean.5, s32[16,128]{1,0:T(8,128)} %bitcast.11, f32[16,128]{1,0:T(8,128)} %bitcast.14), custom_call_target="tpu_custom_call" | custom-call | tf_op jit(solution)/shard_map/pack/pallas_call | solution.py:367
  6.0 3.0 %collective-permute-start = (f32[320,128]{1,0:T(8,128)}, f32[320,128]{1,0:T(8,128)S(1)}, u32[]{:S(2)}, u32[]{:S(2)}) collective-permute-start(f32[320,128]{1,0:T(8,128)} %get-tuple-element.10.sent_a), channel_id=1, source_target_pairs={{0,4},{4,0},{8,12},{12,8},{16,20},{20,16},{24,28},{28,24},{1,5},{5... | collective-permute-start | bytes 491528 | tf_op jit(solution)/shard_map/ppermute | solution.py:375
  8.9 3.6 %collective-permute-start.1 = (f32[320,128]{1,0:T(8,128)}, f32[320,128]{1,0:T(8,128)S(1)}, u32[]{:S(2)}, u32[]{:S(2)}) collective-permute-start(f32[320,128]{1,0:T(8,128)} %get-tuple-element.11.sent_b), channel_id=1, source_target_pairs={{0,28},{4,8},{8,4},{12,16},{16,12},{20,24},{24,20},{28,0},{1,29},{... | collective-permute-start | bytes 491528 | tf_op jit(solution)/shard_map/ppermute | solution.py:376
  13.2 5.5 %main.1 = f32[512,256]{1,0:T(8,128)} custom-call(f32[1024,128]{1,0:T(8,128)} %bitcast.6, bf16[1024,128]{1,0:T(8,128)(2,1)} %bitcast.9, f32[1]{0:T(128)S(6)} %copy.9.weight, f32[64,128]{1,0:T(8,128)} %kappa.5, f32[64,128]{1,0:T(8,128)} %scale.5, s32[64,128]{1,0:T(8,128)} %ocean.5), custom_call_target="tpu_custom_call" | custom-call | tf_op jit(solution)/shard_map/main/pallas_call | solution.py:377
  18.7 0.0 collective-permute-done.got_a
  18.7 0.0 copy-start
  18.7 0.0 collective-permute-done.1.got_b
  18.7 0.7 %copy-done = f32[320,128]{1,0:T(8,128)} copy-done((f32[320,128]{1,0:T(8,128)}, f32[320,128]{1,0:T(8,128)S(1)}, u32[]{:S(2)}) %copy-start) | copy-done | bytes 163864
  19.3 0.0 copy-start.1
  19.3 0.7 %copy-done.1 = f32[320,128]{1,0:T(8,128)} copy-done((f32[320,128]{1,0:T(8,128)}, f32[320,128]{1,0:T(8,128)S(1)}, u32[]{:S(2)}) %copy-start.1) | copy-done | bytes 163864
  20.0 7.2 %strip.1 = (f32[48,128]{1,0:T(8,128)}, f32[512,128]{1,0:T(8,128)}, f32[3,64,128]{2,1,0:T(8,128)}) custom-call(f32[512,256]{1,0:T(8,128)} %main.1, f32[320,128]{1,0:T(8,128)} %get-tuple-element.10.sent_a, f32[320,128]{1,0:T(8,128)} %get-tuple-element.11.sent_b, f32[320,128]{1,0:T(8,128)} %copy-done, f32[320,128]{1,0:T(8,128)} %copy-done.1, ...), custom_call_target="tpu_custom_call" | custom-call | tf_op jit(solution)/shard_map/strip/pallas_call | solution.py:384
  27.2 0.4 collective-permute-start.4
  27.6 1.1 %collective-permute-start.3 = (f32[48,128]{1,0:T(8,128)}, f32[48,128]{1,0:T(8,128)S(1)}, u32[]{:S(2)}, u32[]{:S(2)}) collective-permute-start(f32[48,128]{1,0:T(8,128)} %get-tuple-element.14.v0), channel_id=1, source_target_pairs={{0,2},{1,3},{2,0},{3,1},{4,6},{5,7},{6,4},{7,5},{8,10},{9,11},{10,... | collective-permute-start | bytes 73736 | tf_op jit(solution)/shard_map/ppermute | solution.py:396
  28.7 0.3 collective-permute-start.2
  29.0 1.8 %collective-permute-done.4.v3 = f32[48,128]{1,0:T(8,128)S(1)} collective-permute-done((f32[48,128]{1,0:T(8,128)}, f32[48,128]{1,0:T(8,128)S(1)}, u32[]{:S(2)}, u32[]{:S(2)}) %collective-permute-start.4) | collective-permute-done | bytes 24608 | tf_op jit(solution)/shard_map/ppermute | solution.py:396
  30.8 0.0 copy-start.2
  30.8 0.8 %collective-permute-done.3.v2 = f32[48,128]{1,0:T(8,128)S(1)} collective-permute-done((f32[48,128]{1,0:T(8,128)}, f32[48,128]{1,0:T(8,128)S(1)}, u32[]{:S(2)}, u32[]{:S(2)}) %collective-permute-start.3) | collective-permute-done | bytes 24608 | tf_op jit(solution)/shard_map/ppermute | solution.py:396
  31.6 0.0 copy-start.3
  31.6 0.0 collective-permute-done.2.v1
  31.6 0.0 copy-start.4
  31.6 0.0 copy-done.2
  31.6 0.6 %copy-done.3 = f32[48,128]{1,0:T(8,128)} copy-done((f32[48,128]{1,0:T(8,128)}, f32[48,128]{1,0:T(8,128)S(1)}, u32[]{:S(2)}) %copy-start.3) | copy-done | bytes 24600
  32.2 0.0 copy-done.4
  32.2 10.5 %adjoint.1 = f32[1024,128]{1,0:T(8,128)} custom-call(f32[1024,128]{1,0:T(8,128)} %bitcast.7, bf16[1024,128]{1,0:T(8,128)(2,1)} %bitcast.10, f32[1]{0:T(128)S(6)} %copy.9.weight, f32[64,128]{1,0:T(8,128)} %kappa.5, f32[64,128]{1,0:T(8,128)} %scale.5, s32[64,128]{1,0:T(8,128)} %ocean.5, s32[16,128]{1,0:T(8,128)} %bitcast.13, f32[16,128]{1,0:T(8,128)} %bitcast.15, ...), custom_call_target="tpu_custom_call" | custom-call | tf_op jit(solution)/shard_map/adjoint/pallas_call | solution.py:397
Async XLA Ops:
  6.0 12.7 %collective-permute-start = (f32[320,128]{1,0:T(8,128)}, f32[320,128]{1,0:T(8,128)S(1)}, u32[]{:S(2)}, u32[]{:S(2)}) collective-permute-start(f32[320,128]{1,0:T(8,128)} %get-tuple-element.10.sent_a), channel_id=1, source_target_pairs={{0,4},{4,0},{8,12},{12,8},{16,20},{20,16},{24,28},{28,24},{1,5},{5... | collective-permute-start | bytes 491528 | tf_op jit(solution)/shard_map/ppermute | solution.py:375
  8.9 9.7 %collective-permute-start.1 = (f32[320,128]{1,0:T(8,128)}, f32[320,128]{1,0:T(8,128)S(1)}, u32[]{:S(2)}, u32[]{:S(2)}) collective-permute-start(f32[320,128]{1,0:T(8,128)} %get-tuple-element.11.sent_b), channel_id=1, source_target_pairs={{0,28},{4,8},{8,4},{12,16},{16,12},{20,24},{24,20},{28,0},{1,29},{... | collective-permute-start | bytes 491528 | tf_op jit(solution)/shard_map/ppermute | solution.py:376
  18.7 0.7 %copy-start = (f32[320,128]{1,0:T(8,128)}, f32[320,128]{1,0:T(8,128)S(1)}, u32[]{:S(2)}) copy-start(f32[320,128]{1,0:T(8,128)S(1)} %collective-permute-done.got_a) | copy-start | bytes 491524
  19.3 0.7 %copy-start.1 = (f32[320,128]{1,0:T(8,128)}, f32[320,128]{1,0:T(8,128)S(1)}, u32[]{:S(2)}) copy-start(f32[320,128]{1,0:T(8,128)S(1)} %collective-permute-done.1.got_b) | copy-start | bytes 491524
  27.2 3.7 %collective-permute-start.4 = (f32[48,128]{1,0:T(8,128)}, f32[48,128]{1,0:T(8,128)S(1)}, u32[]{:S(2)}, u32[]{:S(2)}) collective-permute-start(f32[48,128]{1,0:T(8,128)} %get-tuple-element.14.v0), channel_id=1, source_target_pairs={{0,3},{1,2},{2,1},{3,0},{4,7},{5,6},{6,5},{7,4},{8,11},{9,10},{10,... | collective-permute-start | bytes 73736 | tf_op jit(solution)/shard_map/ppermute | solution.py:396
  27.6 4.0 %collective-permute-start.3 = (f32[48,128]{1,0:T(8,128)}, f32[48,128]{1,0:T(8,128)S(1)}, u32[]{:S(2)}, u32[]{:S(2)}) collective-permute-start(f32[48,128]{1,0:T(8,128)} %get-tuple-element.14.v0), channel_id=1, source_target_pairs={{0,2},{1,3},{2,0},{3,1},{4,6},{5,7},{6,4},{7,5},{8,10},{9,11},{10,... | collective-permute-start | bytes 73736 | tf_op jit(solution)/shard_map/ppermute | solution.py:396
  28.7 2.9 %collective-permute-start.2 = (f32[48,128]{1,0:T(8,128)}, f32[48,128]{1,0:T(8,128)S(1)}, u32[]{:S(2)}, u32[]{:S(2)}) collective-permute-start(f32[48,128]{1,0:T(8,128)} %get-tuple-element.14.v0), channel_id=1, source_target_pairs={{0,1},{1,0},{2,3},{3,2},{4,5},{5,4},{6,7},{7,6},{8,9},{9,8},{10,11... | collective-permute-start | bytes 73736 | tf_op jit(solution)/shard_map/ppermute | solution.py:396
  30.8 0.8 %copy-start.2 = (f32[48,128]{1,0:T(8,128)}, f32[48,128]{1,0:T(8,128)S(1)}, u32[]{:S(2)}) copy-start(f32[48,128]{1,0:T(8,128)S(1)} %collective-permute-done.4.v3) | copy-start | bytes 73732
  31.6 0.6 %copy-start.3 = (f32[48,128]{1,0:T(8,128)}, f32[48,128]{1,0:T(8,128)S(1)}, u32[]{:S(2)}) copy-start(f32[48,128]{1,0:T(8,128)S(1)} %collective-permute-done.3.v2) | copy-start | bytes 73732
  31.6 0.6 %copy-start.4 = (f32[48,128]{1,0:T(8,128)}, f32[48,128]{1,0:T(8,128)S(1)}, u32[]{:S(2)}) copy-start(f32[48,128]{1,0:T(8,128)S(1)} %collective-permute-done.2.v1) | copy-start | bytes 73732

commit v2 on v1

v2 whole, which is shorter than its diff:
```python
import functools

import jax
import jax.numpy as jnp
from jax import lax
from jax.experimental import pallas as pl
from jax.experimental.pallas import tpu as pltpu
from jax.sharding import PartitionSpec as P

STEPS = 8
SUB = 8
EDGE = 2 * STEPS
F32 = jnp.float32
BF16 = jnp.bfloat16


def div_mod(value, size):
    if size & (size - 1) == 0:
        return value >> (size.bit_length() - 1), value & (size - 1)
    return lax.div(value, size), lax.rem(value, size)


def roll(value, shift, axis=1):
    shift %= value.shape[axis]
    return pltpu.roll(value, shift, axis) if shift else value


def lanes(rows):
    return lax.broadcasted_iota(jnp.int32, (rows, 128), 1)


def split(value):
    high = value.astype(BF16)
    return high, (value - high.astype(F32)).astype(BF16)


class Sizes:
    def __init__(self, levels, rows, columns, obs):
        self.levels, self.rows, self.columns, self.obs = levels, rows, columns, obs
        assert columns == 128 and levels == 16 and rows % 16 == 0 and obs % 256 == 0 and STEPS == 8
        self.field = levels * rows
        self.group = self.field // 2
        self.half = self.field // 4
        self.short = self.field // 8
        self.at_coeff = self.half
        self.at_obs = self.at_coeff + rows // 2
        self.obs_rows = obs // 128
        self.payload = self.at_obs + 2 * self.obs_rows


def overlay(pieces, window):
    value = pieces[0]
    for k in range(1, len(pieces)):
        value = jnp.where(window == k, pieces[k], value)
    return value


def pack_kernel(z, alpha, members, kappa, scale, ocean, cell, weight, out_a, out_b):
    even = lax.rem(lax.axis_index("tile"), 2) == 0

    def put(where, right, left):
        out_a[where, :] = jnp.where(even, right, left)
        out_b[where, :] = jnp.where(even, left, right)

    block = 2 * SUB
    lane = lanes(block)
    for q in range(z.half // block):
        right, left = [], []
        for g in range(2):
            for h in range(2):
                rows = pl.ds(g * z.group + h * z.half + q * block, block)
                a, m = alpha[rows, :], members[rows, :].astype(F32)
                base = 64 * g + 32 * h
                right.append(roll(jnp.where(lane >= 128 - EDGE, a, roll(m, -EDGE)), base - (128 - 2 * EDGE)))
                left.append(roll(jnp.where(lane < EDGE, m, roll(a, EDGE)), base))
        put(pl.ds(q * block, block), overlay(right, lane >> 5), overlay(left, lane >> 5))
    half = z.rows // 2
    lane = lanes(half)
    right, left = [], []
    for h in range(2):
        rows = pl.ds(h * half, half)
        for k, ref in enumerate((kappa, scale, ocean)):
            value = ref[rows, :].astype(F32)
            base = 64 * h + EDGE * k
            right.append(roll(value, base - (128 - EDGE)))
            left.append(roll(value, base))
        right.append(right[-1])
        left.append(left[-1])
    put(pl.ds(z.at_coeff, half), overlay(right, lane >> 4), overlay(left, lane >> 4))
    n = z.obs_rows
    for at, value in ((z.at_obs, cell[...].astype(F32)), (z.at_obs + n, weight[...])):
        out_a[pl.ds(at, n), :] = value
        out_b[pl.ds(at, n), :] = value


def up(value):
    return roll(value, -1, 0)


def down(value):
    return roll(value, 1, 0)


def coefficients(kappa, scale, ocean, forward):
    row = lax.broadcasted_iota(jnp.int32, kappa.shape, 0)
    north = 0.5 * (kappa + up(kappa)) * ocean * up(ocean)
    north = jnp.where(row == kappa.shape[0] - 1, 0.0, north)
    east = 0.5 * (kappa + roll(kappa, -1)) * ocean * roll(ocean, -1)
    west, south = roll(east, 1), down(north)
    centre = 1.0 - (east + west) - (north + south)
    if forward:
        return (
            centre * scale,
            east * roll(scale, -1),
            west * roll(scale, 1),
            north * up(scale),
            south * down(scale),
        )
    return tuple(scale * c for c in (centre, east, west, north, south))


def put_coefficients(ref, values):
    for k, value in enumerate(values):
        ref[k] = value


def step_rows(source, target, coeff, rows, levels):
    for t in range(rows // SUB):
        c = [coeff[k, pl.ds(t * SUB, SUB), :] for k in range(5)]
        for level in range(levels):
            at = SUB + level * rows + t * SUB
            u = source[pl.ds(at, SUB), :]
            along = c[3] * source[pl.ds(at + 1, SUB), :] + c[4] * source[pl.ds(at - 1, SUB), :]
            across = c[1] * roll(u, -1) + c[2] * roll(u, 1)
            target[pl.ds(at, SUB), :] = c[0] * u + across + along


def clear_ends(*buffers):
    for ref in buffers:
        zero = jnp.zeros((SUB, 128), F32)
        ref[pl.ds(0, SUB), :] = zero
        ref[pl.ds(ref.shape[0] - SUB, SUB), :] = zero


def sweep(fields, rows):
    def two_steps(_, carry):
        for x, y, coeff, levels in fields:
            step_rows(x, y, coeff, rows, levels)
        for x, y, coeff, levels in fields:
            step_rows(y, x, coeff, rows, levels)
        return carry

    lax.fori_loop(0, STEPS // 2, two_steps, 0)


def cell_parts(z, cell):
    level, rest = div_mod(cell, z.rows * z.columns)
    row, column = div_mod(rest, z.columns)
    return level >> 3, level & 7, row, column


def own_index(z, cell):
    group, part, row, column = cell_parts(z, cell)
    return part * z.rows + row, group * 128 + column


def edge_index(z, cell, windows):
    group, part, row, column = cell_parts(z, cell)
    inside, lane = False, 0
    for first, at in windows:
        here = (column >= first) & (column < first + STEPS)
        inside = here | inside
        lane = jnp.where(here, at - first, lane)
    lane = lane + column + 64 * group + 16 * (part >> 1)
    return jnp.where(inside, (part & 1) * z.rows + row, -1), lane & 127


def own_edges(z):
    return (0, 48), (z.columns - STEPS, 8)


def windows_of(z):
    return own_edges(z), ((0, 16),), ((z.columns - STEPS, 40),)


def quarters(unit, first, second):
    even, odd = (first, second) if first % 2 == 0 else (second, first)
    return jnp.where((unit & 1) == 0, ((unit - even) >> 1) & 3, ((unit - odd) >> 1) & 3)


def one_hot(index, size):
    rows = lax.broadcasted_iota(jnp.int32, (size, index.shape[1]), 0)
    return jnp.where(rows == index, 1.0, 0.0).astype(BF16)


def read_off(field, i, j):
    hot = one_hot(i, field.shape[0])
    value = lax.dot_general(field, hot, (((0,), (0,)), ((), ())), preferred_element_type=F32)
    n = value.shape[0] // 2
    value = value[:n] + value[n:]
    rows = lax.broadcasted_iota(jnp.int32, value.shape, 0)
    return jnp.sum(jnp.where(rows == j, value, 0.0), axis=0, keepdims=True)


def gather(z, out, at, field, cell, index):
    for n in range(z.obs_rows // 2):
        row = jnp.concatenate([cell[2 * n : 2 * n + 1, :], cell[2 * n + 1 : 2 * n + 2, :]], axis=1)
        value = read_off(field, *index(row))
        out[at + 2 * n : at + 2 * n + 1, :] = value[:, :128]
        out[at + 2 * n + 1 : at + 2 * n + 2, :] = value[:, 128:]


def main_kernel(z, alpha, members, weight, kappa, scale, ocean, cell, out, coeff, x, y, both):
    put_coefficients(coeff, coefficients(kappa[...], scale[...], ocean[...].astype(F32), True))
    clear_ends(x, y)
    x[pl.ds(SUB, z.field), :] = alpha[...]
    sweep([(x, y, coeff, z.levels)], z.rows)
    lane = lanes(z.group)
    inner = (lane >= STEPS) & (lane < z.columns - STEPS)
    for g in range(2):
        rows = pl.ds(g * z.group, z.group)
        value = x[pl.ds(SUB + g * z.group, z.group), :] * (members[rows, :].astype(F32) * weight[0])
        high, low = split(jnp.where(inner, value, 0.0))
        both[:, pl.ds(g * 128, 128)] = high
        both[:, pl.ds(256 + g * 128, 128)] = low
    gather(z, out, 0, both[...], cell[...], lambda c: own_index(z, c))


def strip_kernel(
    z, inner, sent_a, sent_b, got_a, got_b, cell, weight, out, strip_members, strip_coeff, coeff, x, y, outer, beside
):
    even = lax.rem(lax.axis_index("tile"), 2) == 0

    def parts(rows):
        sa, sb, ga, gb = sent_a[rows, :], sent_b[rows, :], got_a[rows, :], got_b[rows, :]
        pick = lambda p, q: jnp.where(even, p, q)
        return pick(sa, sb), pick(ga, gb), pick(gb, ga), pick(sb, sa)

    clear_ends(x, y)
    lane = lanes(SUB)
    for q in range(z.half // SUB):
        four = parts(pl.ds(q * SUB, SUB))
        for h in range(2):
            at = h * z.half + q * SUB
            for offset in (0, -EDGE):
                pieces = [roll(part, EDGE * p - 32 * h + offset) for p, part in enumerate(four)]
                value = overlay(pieces, (lane >> 4) & 3)
                if offset:
                    x[pl.ds(SUB + at, SUB), :] = value
                else:
                    strip_members[pl.ds(at, SUB), :] = value * weight[0]
    half = z.rows // 2
    four = parts(pl.ds(z.at_coeff, half))
    lane = lanes(half)
    for k in range(3):
        for h in range(2):
            pieces = [roll(four[p], EDGE * p + 64 * g - 64 * h - EDGE * k) for g in range(2) for p in range(4)]
            strip_coeff[k, pl.ds(h * half, half), :] = overlay(pieces, lane >> 4)
    put_coefficients(coeff, coefficients(strip_coeff[0], strip_coeff[1], strip_coeff[2], True))
    sweep([(x, y, coeff, z.levels // 2)], z.rows)
    unit = lanes(z.short) >> 3
    for ref, first, second in ((outer, 1, 6), (beside, 2, 5)):
        quarter = quarters(unit, first, second)
        pieces = []
        for k in range(4):
            rows = pl.ds(k * z.short, z.short)
            pieces.append(roll(x[pl.ds(SUB + k * z.short, z.short), :] * strip_members[rows, :], 16 * k))
        high, low = split(overlay(pieces, quarter))
        ref[:, :128] = high
        ref[:, 128:] = low
    _, right, left, _ = parts(pl.ds(z.at_obs, z.obs_rows))
    n = z.obs_rows
    for k, (field, cells) in enumerate(
        ((outer, cell[...]), (beside, right.astype(jnp.int32)), (beside, left.astype(jnp.int32)))
    ):
        gather(z, out, k * n, field[...], cells, lambda c: edge_index(z, c, windows_of(z)[k]))
    out[:n, :] = out[:n, :] + inner[...]


def adjoint_kernel(
    z, alpha, members, weight, kappa, scale, ocean, cell, obs_weight, got_a, got_b, strip_members, strip_coeff,
    v0, v1, v2, v3, out, x, y, coeff, strip, spare, strip_c, beside, hot, spread,
):
    even = lax.rem(lax.axis_index("tile"), 2) == 0
    clear_ends(x, y, strip, spare)
    put_coefficients(coeff, coefficients(kappa[...], scale[...], ocean[...].astype(F32), False))
    put_coefficients(strip_c, coefficients(strip_coeff[0], strip_coeff[1], strip_coeff[2], False))
    value = (v0[...] + v1[...]) + (v2[...] + v3[...])
    n = z.obs_rows
    pick = lambda p, q: jnp.where(even, p, q)
    cells, weights = pl.ds(z.at_obs, n), pl.ds(z.at_obs + n, n)
    right = pick(got_a[cells, :], got_b[cells, :]).astype(jnp.int32)
    left = pick(got_b[cells, :], got_a[cells, :]).astype(jnp.int32)
    right_weight = pick(got_a[weights, :], got_b[weights, :])
    left_weight = pick(got_b[weights, :], got_a[weights, :])

    def spread_out(groups, tall, wide):
        at = 0
        for index, amount, place in groups:
            for r in range(n):
                i, j = place(index[r : r + 1, :])
                hot[:tall, pl.ds(at * 128, 128)] = one_hot(i, tall)
                rows = lax.broadcasted_iota(jnp.int32, (wide, 128), 0)
                high, low = split(jnp.where(rows == j, amount[r : r + 1, :], 0.0))
                spread[:wide, pl.ds(at * 128, 128)] = high
                spread[pl.ds(wide, wide), pl.ds(at * 128, 128)] = low
                at += 1
        dims = (((1,), (1,)), ((), ()))
        total = lax.dot_general(
            hot[:tall, : at * 128], spread[: 2 * wide, : at * 128], dims, preferred_element_type=F32
        )
        return total[:, :wide] + total[:, wide:]

    field = spread_out([(cell[...], obs_weight[...] * value[:n], lambda c: own_index(z, c))], z.group, 256)
    for g in range(2):
        x[pl.ds(SUB + g * z.group, z.group), :] = field[:, g * 128 : (g + 1) * 128]
    _, right_window, left_window = windows_of(z)
    beside[...] = spread_out(
        [
            (right, right_weight * value[n : 2 * n], lambda c: edge_index(z, c, right_window)),
            (left, left_weight * value[2 * n :], lambda c: edge_index(z, c, left_window)),
        ],
        z.short,
        128,
    )
    lane = lanes(SUB)
    part = (lane >> 4) & 3
    within = lane & 15
    outside = ((part == 1) & (within < STEPS)) | ((part == 2) & (within >= STEPS))
    for q in range(z.group // SUB):
        k, rest = divmod(q * SUB, z.short)
        value = jnp.where(outside, roll(beside[pl.ds(rest, SUB), :], -16 * k), 0.0)
        for g in range(2):
            at = g * z.group + q * SUB
            here = pl.ds(SUB + at, SUB)
            field = x[here, :]
            mine = (lane >> 6) == g
            value = jnp.where(mine & (part == 0), roll(field, EDGE + 64 * g), value)
            value = jnp.where(mine & (part == 3), roll(field, 48 + 64 * g), value)
        strip[pl.ds(SUB + q * SUB, SUB), :] = value * strip_members[pl.ds(q * SUB, SUB), :]
    here = pl.ds(SUB, z.field)
    x[here, :] = x[here, :] * (members[...].astype(F32) * weight[0])
    sweep([(x, y, coeff, z.levels), (strip, spare, strip_c, z.levels // 2)], z.rows)
    for q in range(z.group // SUB):
        value = strip[pl.ds(SUB + q * SUB, SUB), :]
        for g in range(2):
            at = g * z.group + q * SUB
            fixed = x[pl.ds(SUB + at, SUB), :]
            fixed = jnp.where(lane >= z.columns - STEPS, roll(value, 112 - 64 * g), fixed)
            fixed = jnp.where(lane < STEPS, roll(value, -48 - 64 * g), fixed)
            out[pl.ds(at, SUB), :] = alpha[pl.ds(at, SUB), :] + fixed


def local(alpha, members, mem_weight, kappa, norm_scale, land_sea, obs_cell, obs_weight):
    shape = alpha.shape
    z = Sizes(shape[1], shape[2], shape[3], obs_cell.shape[0])
    tiles, holders = lax.axis_size("tile"), lax.axis_size("mem")
    assert tiles % 2 == 0 and holders == 4 and shape[0] == 1
    alpha = alpha.reshape(z.field, z.columns)
    members = members.reshape(z.field, z.columns)
    cell = obs_cell.reshape(z.obs_rows, 128)
    weight = obs_weight.reshape(z.obs_rows, 128)
    smem = pl.BlockSpec(memory_space=pltpu.SMEM)
    whole = pl.BlockSpec(memory_space=pltpu.VMEM)
    sds = jax.ShapeDtypeStruct
    main_field = pltpu.VMEM((z.field + 2 * SUB, 128), F32)
    strip_field = pltpu.VMEM((z.group + 2 * SUB, 128), F32)
    coeff = pltpu.VMEM((5, z.rows, 128), F32)
    payload = sds((z.payload, 128), F32)
    sent_a, sent_b = pl.pallas_call(
        functools.partial(pack_kernel, z),
        out_shape=(payload, payload),
        name="pack",
    )(alpha, members, kappa, norm_scale, land_sea, cell, weight)
    near = [(i, i ^ 1) for i in range(tiles)]
    far = [(i, (i + 1) % tiles if i % 2 else (i - 1) % tiles) for i in range(tiles)]
    got_b = lax.ppermute(sent_b, "tile", far)
    got_a = lax.ppermute(sent_a, "tile", near)
    inner = pl.pallas_call(
        functools.partial(main_kernel, z),
        out_shape=sds((z.obs_rows, 128), F32),
        in_specs=[whole, whole, smem, whole, whole, whole, whole],
        scratch_shapes=[coeff, main_field, main_field, pltpu.VMEM((z.group, 512), BF16)],
        name="main",
    )(alpha, members, mem_weight, kappa, norm_scale, land_sea, cell)
    packed = pltpu.VMEM((z.short, 256), BF16)
    values, strip_members, strip_coeff = pl.pallas_call(
        functools.partial(strip_kernel, z),
        out_shape=(sds((3 * z.obs_rows, 128), F32), sds((z.group, 128), F32), sds((3, z.rows, 128), F32)),
        in_specs=[whole] * 6 + [smem],
        scratch_shapes=[coeff, strip_field, strip_field, packed, packed],
        name="strip",
    )(inner, sent_a, sent_b, got_a, got_b, cell, mem_weight)
    others = [lax.ppermute(values, "mem", [(i, i ^ k) for i in range(holders)]) for k in range(1, holders)]
    product = pl.pallas_call(
        functools.partial(adjoint_kernel, z),
        out_shape=sds((z.field, z.columns), F32),
        in_specs=[whole, whole, smem] + [whole] * 13,
        scratch_shapes=[
            main_field,
            main_field,
            coeff,
            strip_field,
            strip_field,
            coeff,
            pltpu.VMEM((z.short, 128), F32),
            pltpu.VMEM((z.group, 2 * z.obs), BF16),
            pltpu.VMEM((512, 2 * z.obs), BF16),
        ],
        name="adjoint",
    )(
        alpha, members, mem_weight, kappa, norm_scale, land_sea, cell, weight,
        got_a, got_b, strip_members, strip_coeff, values, *others,
    )
    return product.reshape(shape)


def solution(mesh):
    placed = (
        P("mem", None, None, "tile"),
        P("mem", None, None, "tile"),
        P("mem"),
        P(None, "tile"),
        P(None, "tile"),
        P(None, "tile"),
        P("tile"),
        P("tile"),
    )
    return jax.shard_map(
        local, mesh=mesh, in_specs=placed, out_specs=P("mem", None, None, "tile"), check_vma=False
    )
```

time: 43 us -> 41.8 us (0.972)
  Pallas kernels: 29.2 us -> 28 us
    pallas_call x1, Pallas kernels: 7.18 us -> 5.07 us  [local(): pl.pallas_call(functools.partial(strip_kernel, z), out_shape=(sds((3 * z....]
    pallas_call x1, Pallas kernels: 5.98 us -> 7.38 us  [local(): pl.pallas_call(functools.partial(pack_kernel, z), out_shape=(payload, pay...]
  transfers between devices with their start and end apart: 5 -> 5, of which waited for: 2 -> 2; matrix products, arithmetic and copies ran while one was open for 0% -> 0% of each run, Pallas kernels for 13% -> 14%
where the time goes in v2:
time: 41.8 us; the launch traced here: 41.6 us
  Pallas kernels  28 us (67%)
  starting transfers between devices  8.4 us (20%)
  waiting for transfers between devices  2.58 us (6%)
  local copies, waits for them, and re-layouts  1.92 us (5%)
  between operations  0.67 us (2%)
    pallas_call x1, Pallas kernels, local(): pl.pallas_call(functools.partial(adjoint_kernel, z), out_shape=sds((z.fie...  9.77 us
    pallas_call x1, Pallas kernels, local(): pl.pallas_call(functools.partial(pack_kernel, z), out_shape=(payload, pay...  7.38 us
    pallas_call x1, Pallas kernels, local(): pl.pallas_call(functools.partial(main_kernel, z), out_shape=sds((z.obs_ro...  5.82 us
    pallas_call x1, Pallas kernels, local(): pl.pallas_call(functools.partial(strip_kernel, z), out_shape=(sds((3 * z....  5.07 us
    ppermute x1, starting transfers between devices, local(): got_b = lax.ppermute(sent_b, 'tile', far)  3.57 us
    ppermute x1, starting transfers between devices, local(): got_a = lax.ppermute(sent_a, 'tile', near)  2.97 us
    ppermute x3, waiting for transfers between devices, local(): lax.ppermute(values, 'mem', [(i, i ^ k) for i in range(holders)])  2.57 us
    unnamed x10, local copies, waits for them, and re-layouts  1.92 us
  transfers between devices with their start and end apart: 5, of which 2 were waited for; matrix products, arithmetic and copies ran while one was open for 0% of the time, Pallas kernels for 14%

profile of v2, /device:TPU:0, one launch (start us, length us, event | category | flops | bytes accessed | tf_op | source)
XLA Modules:
  0.0 41.6 jit_solution(3425191936523338679)
XLA Ops:
  0.0 7.4 %pack.1 = (f32[320,128]{1,0:T(8,128)}, f32[320,128]{1,0:T(8,128)}) custom-call(f32[1024,128]{1,0:T(8,128)} %bitcast.5, bf16[1024,128]{1,0:T(8,128)(2,1)} %bitcast.8, f32[64,128]{1,0:T(8,128)} %kappa.5, f32[64,128]{1,0:T(8,128)} %scale.5, s32[64,128]{1,0:T(8,128)} %ocean.5, s32[16,128]{1,0:T(8,128)} %bitcast.11, f32[16,128]{1,0:T(8,128)} %bitcast.15), custom_call_target="tpu_custom_call" | custom-call | tf_op jit(solution)/shard_map/pack/pallas_call | solution.py:370
  7.4 3.0 %collective-permute-start = (f32[320,128]{1,0:T(8,128)}, f32[320,128]{1,0:T(8,128)S(1)}, u32[]{:S(2)}, u32[]{:S(2)}) collective-permute-start(f32[320,128]{1,0:T(8,128)} %get-tuple-element.10.sent_a), channel_id=1, source_target_pairs={{0,4},{4,0},{8,12},{12,8},{16,20},{20,16},{24,28},{28,24},{1,5},{5... | collective-permute-start | bytes 491528 | tf_op jit(solution)/shard_map/ppermute | solution.py:378
  10.4 3.6 %collective-permute-start.1 = (f32[320,128]{1,0:T(8,128)}, f32[320,128]{1,0:T(8,128)S(1)}, u32[]{:S(2)}, u32[]{:S(2)}) collective-permute-start(f32[320,128]{1,0:T(8,128)} %get-tuple-element.11.sent_b), channel_id=1, source_target_pairs={{0,28},{4,8},{8,4},{12,16},{16,12},{20,24},{24,20},{28,0},{1,29},{... | collective-permute-start | bytes 491528 | tf_op jit(solution)/shard_map/ppermute | solution.py:377
  14.6 5.8 %main.1.inner = f32[16,128]{1,0:T(8,128)} custom-call(f32[1024,128]{1,0:T(8,128)} %bitcast.6, bf16[1024,128]{1,0:T(8,128)(2,1)} %bitcast.9, f32[1]{0:T(128)S(6)} %copy.9.weight, f32[64,128]{1,0:T(8,128)} %kappa.5, f32[64,128]{1,0:T(8,128)} %scale.5, s32[64,128]{1,0:T(8,128)} %ocean.5, s32[16,128]{1,0:T(8,128)} %bitcast.12), custom_call_target="tpu_custom_call" | custom-call | tf_op jit(solution)/shard_map/main/pallas_call | solution.py:379
  20.4 0.0 collective-permute-done.got_a
  20.4 0.0 copy-start
  20.4 0.0 collective-permute-done.1.got_b
  20.4 0.7 %copy-done = f32[320,128]{1,0:T(8,128)} copy-done((f32[320,128]{1,0:T(8,128)}, f32[320,128]{1,0:T(8,128)S(1)}, u32[]{:S(2)}) %copy-start) | copy-done | bytes 163864
  21.1 0.0 copy-start.1
  21.1 0.7 %copy-done.1 = f32[320,128]{1,0:T(8,128)} copy-done((f32[320,128]{1,0:T(8,128)}, f32[320,128]{1,0:T(8,128)S(1)}, u32[]{:S(2)}) %copy-start.1) | copy-done | bytes 163864
  21.7 5.1 %strip.1 = (f32[48,128]{1,0:T(8,128)}, f32[512,128]{1,0:T(8,128)}, f32[3,64,128]{2,1,0:T(8,128)}) custom-call(f32[16,128]{1,0:T(8,128)} %main.1.inner, f32[320,128]{1,0:T(8,128)} %get-tuple-element.10.sent_a, f32[320,128]{1,0:T(8,128)} %get-tuple-element.11.sent_b, f32[320,128]{1,0:T(8,128)} %copy-done, f32[320,128]{1,0:T(8,128)} %copy-done.1, ...), custom_call_target="tpu_custom_call" | custom-call | tf_op jit(solution)/shard_map/strip/pallas_call | solution.py:387
  26.8 0.4 collective-permute-start.4
  27.2 1.1 %collective-permute-start.3 = (f32[48,128]{1,0:T(8,128)}, f32[48,128]{1,0:T(8,128)S(1)}, u32[]{:S(2)}, u32[]{:S(2)}) collective-permute-start(f32[48,128]{1,0:T(8,128)} %get-tuple-element.14.v0), channel_id=1, source_target_pairs={{0,2},{1,3},{2,0},{3,1},{4,6},{5,7},{6,4},{7,5},{8,10},{9,11},{10,... | collective-permute-start | bytes 73736 | tf_op jit(solution)/shard_map/ppermute | solution.py:394
  28.3 0.3 collective-permute-start.2
  28.7 1.8 %collective-permute-done.4.v3 = f32[48,128]{1,0:T(8,128)S(1)} collective-permute-done((f32[48,128]{1,0:T(8,128)}, f32[48,128]{1,0:T(8,128)S(1)}, u32[]{:S(2)}, u32[]{:S(2)}) %collective-permute-start.4) | collective-permute-done | bytes 24608 | tf_op jit(solution)/shard_map/ppermute | solution.py:394
  30.4 0.0 copy-start.2
  30.4 0.8 %collective-permute-done.3.v2 = f32[48,128]{1,0:T(8,128)S(1)} collective-permute-done((f32[48,128]{1,0:T(8,128)}, f32[48,128]{1,0:T(8,128)S(1)}, u32[]{:S(2)}, u32[]{:S(2)}) %collective-permute-start.3) | collective-permute-done | bytes 24608 | tf_op jit(solution)/shard_map/ppermute | solution.py:394
  31.2 0.0 copy-start.3
  31.2 0.0 collective-permute-done.2.v1
  31.2 0.0 copy-start.4
  31.2 0.0 copy-done.2
  31.2 0.6 %copy-done.3 = f32[48,128]{1,0:T(8,128)} copy-done((f32[48,128]{1,0:T(8,128)}, f32[48,128]{1,0:T(8,128)S(1)}, u32[]{:S(2)}) %copy-start.3) | copy-done | bytes 24600
  31.8 0.0 copy-done.4
  31.8 9.8 %adjoint.1 = f32[1024,128]{1,0:T(8,128)} custom-call(f32[1024,128]{1,0:T(8,128)} %bitcast.7, bf16[1024,128]{1,0:T(8,128)(2,1)} %bitcast.10, f32[1]{0:T(128)S(6)} %copy.9.weight, f32[64,128]{1,0:T(8,128)} %kappa.5, f32[64,128]{1,0:T(8,128)} %scale.5, s32[64,128]{1,0:T(8,128)} %ocean.5, s32[16,128]{1,0:T(8,128)} %bitcast.14, f32[16,128]{1,0:T(8,128)} %bitcast.16, ...), custom_call_target="tpu_custom_call" | custom-call | tf_op jit(solution)/shard_map/adjoint/pallas_call | solution.py:395
Async XLA Ops:
  7.4 13.0 %collective-permute-start = (f32[320,128]{1,0:T(8,128)}, f32[320,128]{1,0:T(8,128)S(1)}, u32[]{:S(2)}, u32[]{:S(2)}) collective-permute-start(f32[320,128]{1,0:T(8,128)} %get-tuple-element.10.sent_a), channel_id=1, source_target_pairs={{0,4},{4,0},{8,12},{12,8},{16,20},{20,16},{24,28},{28,24},{1,5},{5... | collective-permute-start | bytes 491528 | tf_op jit(solution)/shard_map/ppermute | solution.py:378
  10.4 10.1 %collective-permute-start.1 = (f32[320,128]{1,0:T(8,128)}, f32[320,128]{1,0:T(8,128)S(1)}, u32[]{:S(2)}, u32[]{:S(2)}) collective-permute-start(f32[320,128]{1,0:T(8,128)} %get-tuple-element.11.sent_b), channel_id=1, source_target_pairs={{0,28},{4,8},{8,4},{12,16},{16,12},{20,24},{24,20},{28,0},{1,29},{... | collective-permute-start | bytes 491528 | tf_op jit(solution)/shard_map/ppermute | solution.py:377
  20.4 0.7 %copy-start = (f32[320,128]{1,0:T(8,128)}, f32[320,128]{1,0:T(8,128)S(1)}, u32[]{:S(2)}) copy-start(f32[320,128]{1,0:T(8,128)S(1)} %collective-permute-done.got_a) | copy-start | bytes 491524
  21.1 0.7 %copy-start.1 = (f32[320,128]{1,0:T(8,128)}, f32[320,128]{1,0:T(8,128)S(1)}, u32[]{:S(2)}) copy-start(f32[320,128]{1,0:T(8,128)S(1)} %collective-permute-done.1.got_b) | copy-start | bytes 491524
  26.8 3.6 %collective-permute-start.4 = (f32[48,128]{1,0:T(8,128)}, f32[48,128]{1,0:T(8,128)S(1)}, u32[]{:S(2)}, u32[]{:S(2)}) collective-permute-start(f32[48,128]{1,0:T(8,128)} %get-tuple-element.14.v0), channel_id=1, source_target_pairs={{0,3},{1,2},{2,1},{3,0},{4,7},{5,6},{6,5},{7,4},{8,11},{9,10},{10,... | collective-permute-start | bytes 73736 | tf_op jit(solution)/shard_map/ppermute | solution.py:394
  27.2 4.0 %collective-permute-start.3 = (f32[48,128]{1,0:T(8,128)}, f32[48,128]{1,0:T(8,128)S(1)}, u32[]{:S(2)}, u32[]{:S(2)}) collective-permute-start(f32[48,128]{1,0:T(8,128)} %get-tuple-element.14.v0), channel_id=1, source_target_pairs={{0,2},{1,3},{2,0},{3,1},{4,6},{5,7},{6,4},{7,5},{8,10},{9,11},{10,... | collective-permute-start | bytes 73736 | tf_op jit(solution)/shard_map/ppermute | solution.py:394
  28.3 2.9 %collective-permute-start.2 = (f32[48,128]{1,0:T(8,128)}, f32[48,128]{1,0:T(8,128)S(1)}, u32[]{:S(2)}, u32[]{:S(2)}) collective-permute-start(f32[48,128]{1,0:T(8,128)} %get-tuple-element.14.v0), channel_id=1, source_target_pairs={{0,1},{1,0},{2,3},{3,2},{4,5},{5,4},{6,7},{7,6},{8,9},{9,8},{10,11... | collective-permute-start | bytes 73736 | tf_op jit(solution)/shard_map/ppermute | solution.py:394
  30.4 0.8 %copy-start.2 = (f32[48,128]{1,0:T(8,128)}, f32[48,128]{1,0:T(8,128)S(1)}, u32[]{:S(2)}) copy-start(f32[48,128]{1,0:T(8,128)S(1)} %collective-permute-done.4.v3) | copy-start | bytes 73732
  31.2 0.6 %copy-start.3 = (f32[48,128]{1,0:T(8,128)}, f32[48,128]{1,0:T(8,128)S(1)}, u32[]{:S(2)}) copy-start(f32[48,128]{1,0:T(8,128)S(1)} %collective-permute-done.3.v2) | copy-start | bytes 73732
  31.2 0.6 %copy-start.4 = (f32[48,128]{1,0:T(8,128)}, f32[48,128]{1,0:T(8,128)S(1)}, u32[]{:S(2)}) copy-start(f32[48,128]{1,0:T(8,128)S(1)} %collective-permute-done.2.v1) | copy-start | bytes 73732

commit v3 on v2

--- a/solution.py
+++ b/solution.py
@@ -62,7 +62,7 @@
         out_a[where, :] = jnp.where(even, right, left)
         out_b[where, :] = jnp.where(even, left, right)
 
-    block = 2 * SUB
+    block = 4 * SUB
     lane = lanes(block)
     for q in range(z.half // block):
         right, left = [], []
@@ -71,9 +71,9 @@
                 rows = pl.ds(g * z.group + h * z.half + q * block, block)
                 a, m = alpha[rows, :], members[rows, :].astype(F32)
                 base = 64 * g + 32 * h
-                right.append(roll(jnp.where(lane >= 128 - EDGE, a, roll(m, -EDGE)), base - (128 - 2 * EDGE)))
-                left.append(roll(jnp.where(lane < EDGE, m, roll(a, EDGE)), base))
-        put(pl.ds(q * block, block), overlay(right, lane >> 5), overlay(left, lane >> 5))
+                right += [roll(m, base + EDGE), roll(a, base + 2 * EDGE)]
+                left += [roll(m, base), roll(a, base + EDGE)]
+        put(pl.ds(q * block, block), overlay(right, lane >> 4), overlay(left, lane >> 4))
     half = z.rows // 2
     lane = lanes(half)
     right, left = [], []

time: 41.8 us -> 36.8 us (0.88)
  Pallas kernels: 28 us -> 23 us
    pallas_call x1, Pallas kernels: 7.38 us -> 2.36 us  [local(): pl.pallas_call(functools.partial(pack_kernel, z), out_shape=(payload, pay...]
  transfers between devices with their start and end apart: 5 -> 5, of which waited for: 2 -> 2; matrix products, arithmetic and copies ran while one was open for 0% -> 0% of each run, Pallas kernels for 14% -> 16%
where the time goes in v3:
time: 36.8 us; the launch traced here: 36.6 us
  Pallas kernels  23 us (63%)
  starting transfers between devices  8.4 us (23%)
  waiting for transfers between devices  2.58 us (7%)
  local copies, waits for them, and re-layouts  1.92 us (5%)
  between operations  0.67 us (2%)
    pallas_call x1, Pallas kernels, local(): pl.pallas_call(functools.partial(adjoint_kernel, z), out_shape=sds((z.fie...  9.77 us
    pallas_call x1, Pallas kernels, local(): pl.pallas_call(functools.partial(main_kernel, z), out_shape=sds((z.obs_ro...  5.82 us
    pallas_call x1, Pallas kernels, local(): pl.pallas_call(functools.partial(strip_kernel, z), out_shape=(sds((3 * z....  5.07 us
    ppermute x1, starting transfers between devices, local(): got_b = lax.ppermute(sent_b, 'tile', far)  3.57 us
    ppermute x1, starting transfers between devices, local(): got_a = lax.ppermute(sent_a, 'tile', near)  2.97 us
    ppermute x3, waiting for transfers between devices, local(): lax.ppermute(values, 'mem', [(i, i ^ k) for i in range(holders)])  2.58 us
    pallas_call x1, Pallas kernels, local(): pl.pallas_call(functools.partial(pack_kernel, z), out_shape=(payload, pay...  2.36 us
    unnamed x10, local copies, waits for them, and re-layouts  1.92 us
  transfers between devices with their start and end apart: 5, of which 2 were waited for; matrix products, arithmetic and copies ran while one was open for 0% of the time, Pallas kernels for 16%

profile of v3, /device:TPU:0, one launch (start us, length us, event | category | flops | bytes accessed | tf_op | source)
XLA Modules:
  0.0 36.6 jit_solution(7366884300277134734)
XLA Ops:
  0.0 2.4 %pack.1 = (f32[320,128]{1,0:T(8,128)}, f32[320,128]{1,0:T(8,128)}) custom-call(f32[1024,128]{1,0:T(8,128)} %bitcast.5, bf16[1024,128]{1,0:T(8,128)(2,1)} %bitcast.8, f32[64,128]{1,0:T(8,128)} %kappa.5, f32[64,128]{1,0:T(8,128)} %scale.5, s32[64,128]{1,0:T(8,128)} %ocean.5, s32[16,128]{1,0:T(8,128)} %bitcast.11, f32[16,128]{1,0:T(8,128)} %bitcast.15), custom_call_target="tpu_custom_call" | custom-call | tf_op jit(solution)/shard_map/pack/pallas_call | solution.py:370
  2.4 3.0 %collective-permute-start = (f32[320,128]{1,0:T(8,128)}, f32[320,128]{1,0:T(8,128)S(1)}, u32[]{:S(2)}, u32[]{:S(2)}) collective-permute-start(f32[320,128]{1,0:T(8,128)} %get-tuple-element.10.sent_a), channel_id=1, source_target_pairs={{0,4},{4,0},{8,12},{12,8},{16,20},{20,16},{24,28},{28,24},{1,5},{5... | collective-permute-start | bytes 491528 | tf_op jit(solution)/shard_map/ppermute | solution.py:378
  5.3 3.6 %collective-permute-start.1 = (f32[320,128]{1,0:T(8,128)}, f32[320,128]{1,0:T(8,128)S(1)}, u32[]{:S(2)}, u32[]{:S(2)}) collective-permute-start(f32[320,128]{1,0:T(8,128)} %get-tuple-element.11.sent_b), channel_id=1, source_target_pairs={{0,28},{4,8},{8,4},{12,16},{16,12},{20,24},{24,20},{28,0},{1,29},{... | collective-permute-start | bytes 491528 | tf_op jit(solution)/shard_map/ppermute | solution.py:377
  9.5 5.8 %main.1.inner = f32[16,128]{1,0:T(8,128)} custom-call(f32[1024,128]{1,0:T(8,128)} %bitcast.6, bf16[1024,128]{1,0:T(8,128)(2,1)} %bitcast.9, f32[1]{0:T(128)S(6)} %copy.9.weight, f32[64,128]{1,0:T(8,128)} %kappa.5, f32[64,128]{1,0:T(8,128)} %scale.5, s32[64,128]{1,0:T(8,128)} %ocean.5, s32[16,128]{1,0:T(8,128)} %bitcast.12), custom_call_target="tpu_custom_call" | custom-call | tf_op jit(solution)/shard_map/main/pallas_call | solution.py:379
  15.4 0.0 collective-permute-done.got_a
  15.4 0.0 copy-start
  15.4 0.0 collective-permute-done.1.got_b
  15.4 0.7 %copy-done = f32[320,128]{1,0:T(8,128)} copy-done((f32[320,128]{1,0:T(8,128)}, f32[320,128]{1,0:T(8,128)S(1)}, u32[]{:S(2)}) %copy-start) | copy-done | bytes 163864
  16.0 0.0 copy-start.1
  16.0 0.7 %copy-done.1 = f32[320,128]{1,0:T(8,128)} copy-done((f32[320,128]{1,0:T(8,128)}, f32[320,128]{1,0:T(8,128)S(1)}, u32[]{:S(2)}) %copy-start.1) | copy-done | bytes 163864
  16.7 5.1 %strip.1 = (f32[48,128]{1,0:T(8,128)}, f32[512,128]{1,0:T(8,128)}, f32[3,64,128]{2,1,0:T(8,128)}) custom-call(f32[16,128]{1,0:T(8,128)} %main.1.inner, f32[320,128]{1,0:T(8,128)} %get-tuple-element.10.sent_a, f32[320,128]{1,0:T(8,128)} %get-tuple-element.11.sent_b, f32[320,128]{1,0:T(8,128)} %copy-done, f32[320,128]{1,0:T(8,128)} %copy-done.1, ...), custom_call_target="tpu_custom_call" | custom-call | tf_op jit(solution)/shard_map/strip/pallas_call | solution.py:387
  21.8 0.4 %collective-permute-start.4 = (f32[48,128]{1,0:T(8,128)}, f32[48,128]{1,0:T(8,128)S(1)}, u32[]{:S(2)}, u32[]{:S(2)}) collective-permute-start(f32[48,128]{1,0:T(8,128)} %get-tuple-element.14.v0), channel_id=1, source_target_pairs={{0,3},{1,2},{2,1},{3,0},{4,7},{5,6},{6,5},{7,4},{8,11},{9,10},{10,... | collective-permute-start | bytes 73736 | tf_op jit(solution)/shard_map/ppermute | solution.py:394
  22.2 1.1 %collective-permute-start.3 = (f32[48,128]{1,0:T(8,128)}, f32[48,128]{1,0:T(8,128)S(1)}, u32[]{:S(2)}, u32[]{:S(2)}) collective-permute-start(f32[48,128]{1,0:T(8,128)} %get-tuple-element.14.v0), channel_id=1, source_target_pairs={{0,2},{1,3},{2,0},{3,1},{4,6},{5,7},{6,4},{7,5},{8,10},{9,11},{10,... | collective-permute-start | bytes 73736 | tf_op jit(solution)/shard_map/ppermute | solution.py:394
  23.3 0.4 %collective-permute-start.2 = (f32[48,128]{1,0:T(8,128)}, f32[48,128]{1,0:T(8,128)S(1)}, u32[]{:S(2)}, u32[]{:S(2)}) collective-permute-start(f32[48,128]{1,0:T(8,128)} %get-tuple-element.14.v0), channel_id=1, source_target_pairs={{0,1},{1,0},{2,3},{3,2},{4,5},{5,4},{6,7},{7,6},{8,9},{9,8},{10,11... | collective-permute-start | bytes 73736 | tf_op jit(solution)/shard_map/ppermute | solution.py:394
  23.6 1.8 %collective-permute-done.4.v3 = f32[48,128]{1,0:T(8,128)S(1)} collective-permute-done((f32[48,128]{1,0:T(8,128)}, f32[48,128]{1,0:T(8,128)S(1)}, u32[]{:S(2)}, u32[]{:S(2)}) %collective-permute-start.4) | collective-permute-done | bytes 24608 | tf_op jit(solution)/shard_map/ppermute | solution.py:394
  25.5 0.0 copy-start.2
  25.5 0.8 %collective-permute-done.3.v2 = f32[48,128]{1,0:T(8,128)S(1)} collective-permute-done((f32[48,128]{1,0:T(8,128)}, f32[48,128]{1,0:T(8,128)S(1)}, u32[]{:S(2)}, u32[]{:S(2)}) %collective-permute-start.3) | collective-permute-done | bytes 24608 | tf_op jit(solution)/shard_map/ppermute | solution.py:394
  26.2 0.0 copy-start.3
  26.2 0.0 collective-permute-done.2.v1
  26.2 0.0 copy-start.4
  26.2 0.0 copy-done.2
  26.2 0.6 %copy-done.3 = f32[48,128]{1,0:T(8,128)} copy-done((f32[48,128]{1,0:T(8,128)}, f32[48,128]{1,0:T(8,128)S(1)}, u32[]{:S(2)}) %copy-start.3) | copy-done | bytes 24600
  26.8 0.0 copy-done.4
  26.8 9.8 %adjoint.1 = f32[1024,128]{1,0:T(8,128)} custom-call(f32[1024,128]{1,0:T(8,128)} %bitcast.7, bf16[1024,128]{1,0:T(8,128)(2,1)} %bitcast.10, f32[1]{0:T(128)S(6)} %copy.9.weight, f32[64,128]{1,0:T(8,128)} %kappa.5, f32[64,128]{1,0:T(8,128)} %scale.5, s32[64,128]{1,0:T(8,128)} %ocean.5, s32[16,128]{1,0:T(8,128)} %bitcast.14, f32[16,128]{1,0:T(8,128)} %bitcast.16, ...), custom_call_target="tpu_custom_call" | custom-call | tf_op jit(solution)/shard_map/adjoint/pallas_call | solution.py:395
Async XLA Ops:
  2.4 13.0 %collective-permute-start = (f32[320,128]{1,0:T(8,128)}, f32[320,128]{1,0:T(8,128)S(1)}, u32[]{:S(2)}, u32[]{:S(2)}) collective-permute-start(f32[320,128]{1,0:T(8,128)} %get-tuple-element.10.sent_a), channel_id=1, source_target_pairs={{0,4},{4,0},{8,12},{12,8},{16,20},{20,16},{24,28},{28,24},{1,5},{5... | collective-permute-start | bytes 491528 | tf_op jit(solution)/shard_map/ppermute | solution.py:378
  5.3 10.1 %collective-permute-start.1 = (f32[320,128]{1,0:T(8,128)}, f32[320,128]{1,0:T(8,128)S(1)}, u32[]{:S(2)}, u32[]{:S(2)}) collective-permute-start(f32[320,128]{1,0:T(8,128)} %get-tuple-element.11.sent_b), channel_id=1, source_target_pairs={{0,28},{4,8},{8,4},{12,16},{16,12},{20,24},{24,20},{28,0},{1,29},{... | collective-permute-start | bytes 491528 | tf_op jit(solution)/shard_map/ppermute | solution.py:377
  15.4 0.7 %copy-start = (f32[320,128]{1,0:T(8,128)}, f32[320,128]{1,0:T(8,128)S(1)}, u32[]{:S(2)}) copy-start(f32[320,128]{1,0:T(8,128)S(1)} %collective-permute-done.got_a) | copy-start | bytes 491524
  16.0 0.7 %copy-start.1 = (f32[320,128]{1,0:T(8,128)}, f32[320,128]{1,0:T(8,128)S(1)}, u32[]{:S(2)}) copy-start(f32[320,128]{1,0:T(8,128)S(1)} %collective-permute-done.1.got_b) | copy-start | bytes 491524
  21.8 3.7 %collective-permute-start.4 = (f32[48,128]{1,0:T(8,128)}, f32[48,128]{1,0:T(8,128)S(1)}, u32[]{:S(2)}, u32[]{:S(2)}) collective-permute-start(f32[48,128]{1,0:T(8,128)} %get-tuple-element.14.v0), channel_id=1, source_target_pairs={{0,3},{1,2},{2,1},{3,0},{4,7},{5,6},{6,5},{7,4},{8,11},{9,10},{10,... | collective-permute-start | bytes 73736 | tf_op jit(solution)/shard_map/ppermute | solution.py:394
  22.2 4.1 %collective-permute-start.3 = (f32[48,128]{1,0:T(8,128)}, f32[48,128]{1,0:T(8,128)S(1)}, u32[]{:S(2)}, u32[]{:S(2)}) collective-permute-start(f32[48,128]{1,0:T(8,128)} %get-tuple-element.14.v0), channel_id=1, source_target_pairs={{0,2},{1,3},{2,0},{3,1},{4,6},{5,7},{6,4},{7,5},{8,10},{9,11},{10,... | collective-permute-start | bytes 73736 | tf_op jit(solution)/shard_map/ppermute | solution.py:394
  23.3 3.0 %collective-permute-start.2 = (f32[48,128]{1,0:T(8,128)}, f32[48,128]{1,0:T(8,128)S(1)}, u32[]{:S(2)}, u32[]{:S(2)}) collective-permute-start(f32[48,128]{1,0:T(8,128)} %get-tuple-element.14.v0), channel_id=1, source_target_pairs={{0,1},{1,0},{2,3},{3,2},{4,5},{5,4},{6,7},{7,6},{8,9},{9,8},{10,11... | collective-permute-start | bytes 73736 | tf_op jit(solution)/shard_map/ppermute | solution.py:394
  25.5 0.8 %copy-start.2 = (f32[48,128]{1,0:T(8,128)}, f32[48,128]{1,0:T(8,128)S(1)}, u32[]{:S(2)}) copy-start(f32[48,128]{1,0:T(8,128)S(1)} %collective-permute-done.4.v3) | copy-start | bytes 73732
  26.2 0.6 %copy-start.3 = (f32[48,128]{1,0:T(8,128)}, f32[48,128]{1,0:T(8,128)S(1)}, u32[]{:S(2)}) copy-start(f32[48,128]{1,0:T(8,128)S(1)} %collective-permute-done.3.v2) | copy-start | bytes 73732
  26.2 0.6 %copy-start.4 = (f32[48,128]{1,0:T(8,128)}, f32[48,128]{1,0:T(8,128)S(1)}, u32[]{:S(2)}) copy-start(f32[48,128]{1,0:T(8,128)S(1)} %collective-permute-done.2.v1) | copy-start | bytes 73732

commit v4 on v3

--- a/solution.py
+++ b/solution.py
@@ -55,7 +55,12 @@
     return value
 
 
-def pack_kernel(z, alpha, members, kappa, scale, ocean, cell, weight, out_a, out_b):
+def early(tiles):
+    tile = lax.axis_index("tile")
+    return (tile == 0) | ((lax.rem(tile, 2) == 1) & (tile != tiles - 1))
+
+
+def pack_kernel(z, tiles, alpha, members, kappa, scale, ocean, cell, weight, out_a, out_b, x, coeff, y):
     even = lax.rem(lax.axis_index("tile"), 2) == 0
 
     def put(where, right, left):
@@ -92,6 +97,10 @@
         out_a[pl.ds(at, n), :] = value
         out_b[pl.ds(at, n), :] = value
 
+    @pl.when(early(tiles))
+    def _():
+        forward_sweep(z, alpha, kappa, scale, ocean, coeff, x, y)
+
 
 def up(value):
     return roll(value, -1, 0)
@@ -193,8 +202,7 @@
     return jnp.where(rows == index, 1.0, 0.0).astype(BF16)
 
 
-def read_off(field, i, j):
-    hot = one_hot(i, field.shape[0])
+def read_off(field, hot, j):
     value = lax.dot_general(field, hot, (((0,), (0,)), ((), ())), preferred_element_type=F32)
     n = value.shape[0] // 2
     value = value[:n] + value[n:]
@@ -202,19 +210,36 @@
     return jnp.sum(jnp.where(rows == j, value, 0.0), axis=0, keepdims=True)
 
 
-def gather(z, out, at, field, cell, index):
+def gather(z, out, at, field, cell, index, keep=None, start=0):
     for n in range(z.obs_rows // 2):
         row = jnp.concatenate([cell[2 * n : 2 * n + 1, :], cell[2 * n + 1 : 2 * n + 2, :]], axis=1)
-        value = read_off(field, *index(row))
+        i, j = index(row)
+        hot = one_hot(i, field.shape[0])
+        if keep is not None:
+            keep[:, pl.ds(start + 256 * n, 256)] = hot
+        value = read_off(field, hot, j)
         out[at + 2 * n : at + 2 * n + 1, :] = value[:, :128]
         out[at + 2 * n + 1 : at + 2 * n + 2, :] = value[:, 128:]
 
 
-def main_kernel(z, alpha, members, weight, kappa, scale, ocean, cell, out, coeff, x, y, both):
+def forward_sweep(z, alpha, kappa, scale, ocean, coeff, x, y):
     put_coefficients(coeff, coefficients(kappa[...], scale[...], ocean[...].astype(F32), True))
     clear_ends(x, y)
     x[pl.ds(SUB, z.field), :] = alpha[...]
     sweep([(x, y, coeff, z.levels)], z.rows)
+
+
+def main_kernel(z, tiles, swept, alpha, members, weight, kappa, scale, ocean, cell, out, hot, x, coeff, y, both):
+    first = early(tiles)
+
+    @pl.when(first)
+    def _():
+        x[...] = swept[...]
+
+    @pl.when(jnp.logical_not(first))
+    def _():
+        forward_sweep(z, alpha, kappa, scale, ocean, coeff, x, y)
+
     lane = lanes(z.group)
     inner = (lane >= STEPS) & (lane < z.columns - STEPS)
     for g in range(2):
@@ -223,11 +248,11 @@
         high, low = split(jnp.where(inner, value, 0.0))
         both[:, pl.ds(g * 128, 128)] = high
         both[:, pl.ds(256 + g * 128, 128)] = low
-    gather(z, out, 0, both[...], cell[...], lambda c: own_index(z, c))
+    gather(z, out, 0, both[...], cell[...], lambda c: own_index(z, c), hot)
 
 
 def strip_kernel(
-    z, inner, sent_a, sent_b, got_a, got_b, cell, weight, out, strip_members, strip_coeff, coeff, x, y, outer, beside
+    z, inner, sent_a, sent_b, got_a, got_b, cell, weight, out, strip_members, strip_coeff, hot, coeff, x, y, outer, beside
 ):
     even = lax.rem(lax.axis_index("tile"), 2) == 0
 
@@ -273,55 +298,68 @@
     for k, (field, cells) in enumerate(
         ((outer, cell[...]), (beside, right.astype(jnp.int32)), (beside, left.astype(jnp.int32)))
     ):
-        gather(z, out, k * n, field[...], cells, lambda c: edge_index(z, c, windows_of(z)[k]))
+        keep = hot if k else None
+        gather(z, out, k * n, field[...], cells, lambda c: edge_index(z, c, windows_of(z)[k]), keep, (k - 1) * z.obs)
     out[:n, :] = out[:n, :] + inner[...]
 
 
-def adjoint_kernel(
-    z, alpha, members, weight, kappa, scale, ocean, cell, obs_weight, got_a, got_b, strip_members, strip_coeff,
-    v0, v1, v2, v3, out, x, y, coeff, strip, spare, strip_c, beside, hot, spread,
-):
+def beside_rows(z, got_a, got_b, at):
     even = lax.rem(lax.axis_index("tile"), 2) == 0
-    clear_ends(x, y, strip, spare)
+    a, b = got_a[pl.ds(at, z.obs_rows), :], got_b[pl.ds(at, z.obs_rows), :]
+    return jnp.where(even, a, b), jnp.where(even, b, a)
+
+
+def ready_kernel(z, kappa, scale, ocean, cell, got_a, got_b, strip_coeff, coeff, strip_c, own_lane, beside_lane):
     put_coefficients(coeff, coefficients(kappa[...], scale[...], ocean[...].astype(F32), False))
     put_coefficients(strip_c, coefficients(strip_coeff[0], strip_coeff[1], strip_coeff[2], False))
+    _, right_window, left_window = windows_of(z)
+    right, left = beside_rows(z, got_a, got_b, z.at_obs)
+    n = z.obs_rows
+    for r in range(n):
+        at = pl.ds(r * 128, 128)
+        own_lane[:, at] = one_hot(own_index(z, cell[r : r + 1, :])[1], 256)
+        index = right[r : r + 1, :].astype(jnp.int32)
+        beside_lane[:, at] = one_hot(edge_index(z, index, right_window)[1], 128)
+        index = left[r : r + 1, :].astype(jnp.int32)
+        beside_lane[:, pl.ds(z.obs + r * 128, 128)] = one_hot(edge_index(z, index, left_window)[1], 128)
+
+
+def adjoint_kernel(
+    z, alpha_hbm, members_hbm, weight, obs_weight, got_a, got_b, strip_members, coeff, strip_c,
+    own_row, own_lane, beside_row, beside_lane, v0, v1, v2, v3,
+    out_hbm, x, y, strip, spare, beside, spread, alpha, members, out, sems,
+):
+    bring_alpha = pltpu.make_async_copy(alpha_hbm, alpha, sems.at[0])
+    bring_members = pltpu.make_async_copy(members_hbm, members, sems.at[1])
+    bring_members.start()
+    bring_alpha.start()
+    clear_ends(x, y, strip, spare)
     value = (v0[...] + v1[...]) + (v2[...] + v3[...])
     n = z.obs_rows
-    pick = lambda p, q: jnp.where(even, p, q)
-    cells, weights = pl.ds(z.at_obs, n), pl.ds(z.at_obs + n, n)
-    right = pick(got_a[cells, :], got_b[cells, :]).astype(jnp.int32)
-    left = pick(got_b[cells, :], got_a[cells, :]).astype(jnp.int32)
-    right_weight = pick(got_a[weights, :], got_b[weights, :])
-    left_weight = pick(got_b[weights, :], got_a[weights, :])
-
-    def spread_out(groups, tall, wide):
-        at = 0
-        for index, amount, place in groups:
+    right_weight, left_weight = beside_rows(z, got_a, got_b, z.at_obs + n)
+
+    def spread_out(amounts, row_hot, lane_hot):
+        wide = lane_hot.shape[0]
+        for group, amount in enumerate(amounts):
+            high, low = split(amount)
             for r in range(n):
-                i, j = place(index[r : r + 1, :])
-                hot[:tall, pl.ds(at * 128, 128)] = one_hot(i, tall)
-                rows = lax.broadcasted_iota(jnp.int32, (wide, 128), 0)
-                high, low = split(jnp.where(rows == j, amount[r : r + 1, :], 0.0))
-                spread[:wide, pl.ds(at * 128, 128)] = high
-                spread[pl.ds(wide, wide), pl.ds(at * 128, 128)] = low
-                at += 1
+                at = pl.ds(group * z.obs + r * 128, 128)
+                for k, part in enumerate((high, low)):
+                    line = jnp.broadcast_to(part[r : r + 1, :].astype(F32), (2 * SUB, 128)).astype(BF16)
+                    for t in range(wide // (2 * SUB)):
+                        rows = pl.ds(t * 2 * SUB, 2 * SUB)
+                        spread[pl.ds(k * wide + t * 2 * SUB, 2 * SUB), at] = lane_hot[rows, at] * line
         dims = (((1,), (1,)), ((), ()))
         total = lax.dot_general(
-            hot[:tall, : at * 128], spread[: 2 * wide, : at * 128], dims, preferred_element_type=F32
+            row_hot[...], spread[: 2 * wide, : len(amounts) * z.obs], dims, preferred_element_type=F32
         )
         return total[:, :wide] + total[:, wide:]
 
-    field = spread_out([(cell[...], obs_weight[...] * value[:n], lambda c: own_index(z, c))], z.group, 256)
+    field = spread_out([obs_weight[...] * value[:n]], own_row, own_lane)
     for g in range(2):
         x[pl.ds(SUB + g * z.group, z.group), :] = field[:, g * 128 : (g + 1) * 128]
-    _, right_window, left_window = windows_of(z)
     beside[...] = spread_out(
-        [
-            (right, right_weight * value[n : 2 * n], lambda c: edge_index(z, c, right_window)),
-            (left, left_weight * value[2 * n :], lambda c: edge_index(z, c, left_window)),
-        ],
-        z.short,
-        128,
+        [right_weight * value[n : 2 * n], left_weight * value[2 * n :]], beside_row, beside_lane
     )
     lane = lanes(SUB)
     part = (lane >> 4) & 3
@@ -339,16 +377,28 @@
             value = jnp.where(mine & (part == 3), roll(field, 48 + 64 * g), value)
         strip[pl.ds(SUB + q * SUB, SUB), :] = value * strip_members[pl.ds(q * SUB, SUB), :]
     here = pl.ds(SUB, z.field)
+    bring_members.wait()
     x[here, :] = x[here, :] * (members[...].astype(F32) * weight[0])
     sweep([(x, y, coeff, z.levels), (strip, spare, strip_c, z.levels // 2)], z.rows)
-    for q in range(z.group // SUB):
-        value = strip[pl.ds(SUB + q * SUB, SUB), :]
-        for g in range(2):
-            at = g * z.group + q * SUB
-            fixed = x[pl.ds(SUB + at, SUB), :]
-            fixed = jnp.where(lane >= z.columns - STEPS, roll(value, 112 - 64 * g), fixed)
-            fixed = jnp.where(lane < STEPS, roll(value, -48 - 64 * g), fixed)
-            out[pl.ds(at, SUB), :] = alpha[pl.ds(at, SUB), :] + fixed
+    bring_alpha.wait()
+    sent = []
+    for part in range(z.levels // 2):
+        for t in range(z.rows // SUB):
+            q = part * z.rows + t * SUB
+            value = strip[pl.ds(SUB + q, SUB), :]
+            for g in range(2):
+                at = g * z.group + q
+                fixed = x[pl.ds(SUB + at, SUB), :]
+                fixed = jnp.where(lane >= z.columns - STEPS, roll(value, 112 - 64 * g), fixed)
+                fixed = jnp.where(lane < STEPS, roll(value, -48 - 64 * g), fixed)
+                out[pl.ds(at, SUB), :] = alpha[pl.ds(at, SUB), :] + fixed
+        if part % 2:
+            for g in range(2):
+                rows = pl.ds(g * z.group + (part - 1) * z.rows, 2 * z.rows)
+                sent.append(pltpu.make_async_copy(out.at[rows, :], out_hbm.at[rows, :], sems.at[2 + len(sent)]))
+                sent[-1].start()
+    for copy in sent:
+        copy.wait()
 
 
 def local(alpha, members, mem_weight, kappa, norm_scale, land_sea, obs_cell, obs_weight):
@@ -362,55 +412,81 @@
     weight = obs_weight.reshape(z.obs_rows, 128)
     smem = pl.BlockSpec(memory_space=pltpu.SMEM)
     whole = pl.BlockSpec(memory_space=pltpu.VMEM)
+    stays = pl.BlockSpec(memory_space=pl.ANY)
     sds = jax.ShapeDtypeStruct
     main_field = pltpu.VMEM((z.field + 2 * SUB, 128), F32)
     strip_field = pltpu.VMEM((z.group + 2 * SUB, 128), F32)
     coeff = pltpu.VMEM((5, z.rows, 128), F32)
+    packed = pltpu.VMEM((z.short, 256), BF16)
     payload = sds((z.payload, 128), F32)
-    sent_a, sent_b = pl.pallas_call(
-        functools.partial(pack_kernel, z),
-        out_shape=(payload, payload),
+    limit = pltpu.CompilerParams(vmem_limit_bytes=24 << 20)
+    call = functools.partial(pl.pallas_call, compiler_params=limit)
+    sent_a, sent_b, swept = call(
+        functools.partial(pack_kernel, z, tiles),
+        out_shape=(payload, payload, sds((z.field + 2 * SUB, 128), F32)),
+        out_specs=(whole, whole, whole),
+        scratch_shapes=[coeff, main_field],
         name="pack",
     )(alpha, members, kappa, norm_scale, land_sea, cell, weight)
     near = [(i, i ^ 1) for i in range(tiles)]
     far = [(i, (i + 1) % tiles if i % 2 else (i - 1) % tiles) for i in range(tiles)]
     got_b = lax.ppermute(sent_b, "tile", far)
     got_a = lax.ppermute(sent_a, "tile", near)
-    inner = pl.pallas_call(
-        functools.partial(main_kernel, z),
-        out_shape=sds((z.obs_rows, 128), F32),
-        in_specs=[whole, whole, smem, whole, whole, whole, whole],
-        scratch_shapes=[coeff, main_field, main_field, pltpu.VMEM((z.group, 512), BF16)],
+    inner, own_row = call(
+        functools.partial(main_kernel, z, tiles),
+        out_shape=(sds((z.obs_rows, 128), F32), sds((z.group, z.obs), BF16)),
+        in_specs=[whole] * 3 + [smem] + [whole] * 4,
+        out_specs=(whole, whole),
+        scratch_shapes=[main_field, coeff, main_field, pltpu.VMEM((z.group, 512), BF16)],
         name="main",
-    )(alpha, members, mem_weight, kappa, norm_scale, land_sea, cell)
-    packed = pltpu.VMEM((z.short, 256), BF16)
-    values, strip_members, strip_coeff = pl.pallas_call(
+    )(swept, alpha, members, mem_weight, kappa, norm_scale, land_sea, cell)
+    values, strip_members, strip_coeff, beside_row = call(
         functools.partial(strip_kernel, z),
-        out_shape=(sds((3 * z.obs_rows, 128), F32), sds((z.group, 128), F32), sds((3, z.rows, 128), F32)),
+        out_shape=(
+            sds((3 * z.obs_rows, 128), F32),
+            sds((z.group, 128), F32),
+            sds((3, z.rows, 128), F32),
+            sds((z.short, 2 * z.obs), BF16),
+        ),
         in_specs=[whole] * 6 + [smem],
+        out_specs=(whole,) * 4,
         scratch_shapes=[coeff, strip_field, strip_field, packed, packed],
         name="strip",
     )(inner, sent_a, sent_b, got_a, got_b, cell, mem_weight)
     others = [lax.ppermute(values, "mem", [(i, i ^ k) for i in range(holders)]) for k in range(1, holders)]
-    product = pl.pallas_call(
+    main_c, strip_c, own_lane, beside_lane = call(
+        functools.partial(ready_kernel, z),
+        out_shape=(
+            sds((5, z.rows, 128), F32),
+            sds((5, z.rows, 128), F32),
+            sds((2 * 128, z.obs), BF16),
+            sds((128, 2 * z.obs), BF16),
+        ),
+        in_specs=[whole] * 7,
+        out_specs=(whole,) * 4,
+        name="ready",
+    )(kappa, norm_scale, land_sea, cell, got_a, got_b, strip_coeff)
+    product = call(
         functools.partial(adjoint_kernel, z),
         out_shape=sds((z.field, z.columns), F32),
-        in_specs=[whole, whole, smem] + [whole] * 13,
+        in_specs=[stays, stays, smem] + [whole] * 14,
+        out_specs=stays,
         scratch_shapes=[
             main_field,
             main_field,
-            coeff,
             strip_field,
             strip_field,
-            coeff,
             pltpu.VMEM((z.short, 128), F32),
-            pltpu.VMEM((z.group, 2 * z.obs), BF16),
             pltpu.VMEM((512, 2 * z.obs), BF16),
+            pltpu.VMEM((z.field, 128), F32),
+            pltpu.VMEM((z.field, 128), BF16),
+            pltpu.VMEM((z.field, 128), F32),
+            pltpu.SemaphoreType.DMA((2 + z.levels // 2,)),
         ],
         name="adjoint",
     )(
-        alpha, members, mem_weight, kappa, norm_scale, land_sea, cell, weight,
-        got_a, got_b, strip_members, strip_coeff, values, *others,
+        alpha, members, mem_weight, weight, got_a, got_b, strip_members, main_c, strip_c,
+        own_row, own_lane, beside_row, beside_lane, values, *others,
     )
     return product.reshape(shape)
 

time: 36.8 us -> 35.5 us (0.965)
  Pallas kernels: 23 us -> 16.6 us
  local copies, waits for them, and re-layouts: 1.92 us -> 5.68 us
  waiting for transfers between devices: 2.58 us -> 6.15 us
  starting transfers between devices: 8.4 us -> 5.88 us
    pallas_call x4 -> x5, Pallas kernels: 23 us -> 16.6 us  [the longest x1 7.28 us: local(): call(functools.partial(adjoint_kernel, z), out_shape=sds((z.field, z.colu...]
    unnamed x10 -> x28, local copies, waits for them, and re-layouts: 1.92 us -> 5.68 us
    ppermute x1, waiting for transfers between devices: 0.01 us -> 3.76 us  [local(): got_a = lax.ppermute(sent_a, 'tile', near)]
    ppermute x1, starting transfers between devices: 3.57 us -> 0.93 us  [local(): got_b = lax.ppermute(sent_b, 'tile', far)]
    ppermute x3, waiting for transfers between devices: 2.58 us -> 1 us  [local(): lax.ppermute(values, 'mem', [(i, i ^ k) for i in range(holders)])]
    ppermute x1, waiting for transfers between devices: 0.01 us -> 1.39 us  [local(): got_b = lax.ppermute(sent_b, 'tile', far)]
  transfers between devices with their start and end apart: 5 -> 5, of which waited for: 2 -> 4; matrix products, arithmetic and copies ran while one was open for 0% -> 0% of each run, Pallas kernels for 16% -> 8%
where the time goes in v4:
time: 35.5 us; the launch traced here: 35.1 us
  Pallas kernels  16.6 us (47%)
  waiting for transfers between devices  6.15 us (17%)
  starting transfers between devices  5.88 us (17%)
  local copies, waits for them, and re-layouts  5.68 us (16%)
  between operations  0.75 us (2%)
    pallas_call x1, Pallas kernels, local(): call(functools.partial(adjoint_kernel, z), out_shape=sds((z.field, z.colu...  7.28 us
    unnamed x28, local copies, waits for them, and re-layouts  5.68 us
    ppermute x1, waiting for transfers between devices, local(): got_a = lax.ppermute(sent_a, 'tile', near)  3.76 us
    pallas_call x1, Pallas kernels, local(): call(functools.partial(strip_kernel, z), out_shape=(sds((3 * z.obs_rows,...  3.56 us
    pallas_call x1, Pallas kernels, local(): call(functools.partial(pack_kernel, z, tiles), out_shape=(payload, payloa...  3.12 us
    ppermute x1, starting transfers between devices, local(): got_a = lax.ppermute(sent_a, 'tile', near)  3.03 us
    ppermute x3, starting transfers between devices, local(): lax.ppermute(values, 'mem', [(i, i ^ k) for i in range(holders)])  1.92 us
    pallas_call x1, Pallas kernels, local(): call(functools.partial(main_kernel, z, tiles), out_shape=(sds((z.obs_rows...  1.62 us
  transfers between devices with their start and end apart: 5, of which 4 were waited for; matrix products, arithmetic and copies ran while one was open for 0% of the time, Pallas kernels for 8%

profile of v4, /device:TPU:0, one launch (start us, length us, event | category | flops | bytes accessed | tf_op | source)
XLA Modules:
  0.0 35.1 jit_solution(656446024996637282)
XLA Ops:
  0.0 0.0 copy-start
  0.0 1.0 %copy-done = f32[1,16,64,128]{3,2,1,0:T(8,128)S(1)} copy-done((f32[1,16,64,128]{3,2,1,0:T(8,128)S(1)}, f32[1,16,64,128]{3,2,1,0:T(8,128)}, u32[]{:S(2)}) %copy-start) | copy-done | bytes 524312
  1.0 0.0 copy-start.2
  1.0 0.9 %copy-done.2 = bf16[1,16,64,128]{3,2,1,0:T(8,128)(2,1)S(1)} copy-done((bf16[1,16,64,128]{3,2,1,0:T(8,128)(2,1)S(1)}, bf16[1,16,64,128]{3,2,1,0:T(8,128)(2,1)}, u32[]{:S(2)}) %copy-start.2) | copy-done | bytes 262168
  2.0 0.0 copy-start.4
  2.0 0.8 %copy-done.4 = f32[64,128]{1,0:T(8,128)S(1)} copy-done((f32[64,128]{1,0:T(8,128)S(1)}, f32[64,128]{1,0:T(8,128)}, u32[]{:S(2)}) %copy-start.4) | copy-done | bytes 32792
  2.8 0.0 copy-start.6
  2.8 0.8 %copy-done.6 = f32[64,128]{1,0:T(8,128)S(1)} copy-done((f32[64,128]{1,0:T(8,128)S(1)}, f32[64,128]{1,0:T(8,128)}, u32[]{:S(2)}) %copy-start.6) | copy-done | bytes 32792
  3.5 0.0 copy-start.8
  3.5 0.8 %copy-done.8 = s32[64,128]{1,0:T(8,128)S(1)} copy-done((s32[64,128]{1,0:T(8,128)S(1)}, s32[64,128]{1,0:T(8,128)}, u32[]{:S(2)}) %copy-start.8) | copy-done | bytes 32792
  4.3 0.0 copy-start.10
  4.3 0.7 %copy-done.10 = s32[2048]{0:T(1024)S(1)} copy-done((s32[2048]{0:T(1024)S(1)}, s32[2048]{0:T(1024)}, u32[]{:S(2)}) %copy-start.10) | copy-done | bytes 8216
  5.0 0.0 copy-start.12
  5.0 0.7 %copy-done.12 = f32[2048]{0:T(1024)S(1)} copy-done((f32[2048]{0:T(1024)S(1)}, f32[2048]{0:T(1024)}, u32[]{:S(2)}) %copy-start.12) | copy-done | bytes 8216
  5.7 0.0 copy-start.5
  5.7 0.0 copy-start.7
  5.7 0.0 copy-start.9
  5.7 0.0 copy-start.11
  5.7 0.0 copy-start.1
  5.7 0.0 copy-start.3
  5.7 0.0 copy-start.13
  5.7 3.1 %pack.1 = (f32[320,128]{1,0:T(8,128)S(1)}, f32[320,128]{1,0:T(8,128)S(1)}, f32[1040,128]{1,0:T(8,128)S(1)}) custom-call(f32[1024,128]{1,0:T(8,128)S(1)} %bitcast.5, bf16[1024,128]{1,0:T(8,128)(2,1)S(1)} %bitcast.8, f32[64,128]{1,0:T(8,128)S(1)} %copy-done.4, f32[64,128]{1,0:T(8,128)S(1)} %copy-done.6, s32[64,128]{1,0:T(8,128)S(1)} %copy-done.8, ...), custom_call_target="tpu_custom_call" | custom-call | tf_op jit(solution)/shard_map/pack/pallas_call | solution.py:424
  8.8 3.0 %collective-permute-start = (f32[320,128]{1,0:T(8,128)S(1)}, f32[320,128]{1,0:T(8,128)S(1)}, u32[]{:S(2)}, u32[]{:S(2)}) collective-permute-start(f32[320,128]{1,0:T(8,128)S(1)} %get-tuple-element.18.sent_a), channel_id=1, source_target_pairs={{0,4},{4,0},{8,12},{12,8},{16,20},{20,16},{24,28},{28,24},{1,5},{5... | collective-permute-start | bytes 491528 | tf_op jit(solution)/shard_map/ppermute | solution.py:434
  11.9 0.9 %collective-permute-start.1 = (f32[320,128]{1,0:T(8,128)S(1)}, f32[320,128]{1,0:T(8,128)S(1)}, u32[]{:S(2)}, u32[]{:S(2)}) collective-permute-start(f32[320,128]{1,0:T(8,128)S(1)} %get-tuple-element.19.sent_b), channel_id=1, source_target_pairs={{0,28},{4,8},{8,4},{12,16},{16,12},{20,24},{24,20},{28,0},{1,29},{... | collective-permute-start | bytes 491528 | tf_op jit(solution)/shard_map/ppermute | solution.py:433
  13.4 1.6 %main.1 = (f32[16,128]{1,0:T(8,128)S(1)}, bf16[512,2048]{1,0:T(8,128)(2,1)S(1)}) custom-call(f32[1040,128]{1,0:T(8,128)S(1)} %get-tuple-element.20.swept, f32[1024,128]{1,0:T(8,128)S(1)} %bitcast.6, bf16[1024,128]{1,0:T(8,128)(2,1)S(1)} %bitcast.9, f32[1]{0:T(128)S(6)} %copy.9.weight, f32[64,128]{1,0:T(8,128)S(1)} %copy-done.4, f32[64,128]{1,0:T(8,128)S(1)} %copy-done.6, ...), custom_call_target="tpu_custom_call" | custom-call | tf_op jit(solution)/shard_map/main/pallas_call | solution.py:435
  15.1 3.8 %collective-permute-done.got_a = f32[320,128]{1,0:T(8,128)S(1)} collective-permute-done((f32[320,128]{1,0:T(8,128)S(1)}, f32[320,128]{1,0:T(8,128)S(1)}, u32[]{:S(2)}, u32[]{:S(2)}) %collective-permute-start) | collective-permute-done | bytes 163872 | tf_op jit(solution)/shard_map/ppermute | solution.py:434
  18.8 1.4 %collective-permute-done.1.got_b = f32[320,128]{1,0:T(8,128)S(1)} collective-permute-done((f32[320,128]{1,0:T(8,128)S(1)}, f32[320,128]{1,0:T(8,128)S(1)}, u32[]{:S(2)}, u32[]{:S(2)}) %collective-permute-start.1) | collective-permute-done | bytes 163872 | tf_op jit(solution)/shard_map/ppermute | solution.py:433
  20.2 3.6 %strip.1 = (f32[48,128]{1,0:T(8,128)S(1)}, f32[512,128]{1,0:T(8,128)S(1)}, f32[3,64,128]{2,1,0:T(8,128)S(1)}, bf16[128,4096]{1,0:T(8,128)(2,1)S(1)}) custom-call(f32[16,128]{1,0:T(8,128)S(1)} %get-tuple-element.21.inner, f32[320,128]{1,0:T(8,128)S(1)} %get-tuple-element.18.sent_a, f32[320,128]{1,0:T(8,128)S(1)} %get-tuple-element.19.sent_b, ...), custom_call_target="tpu_custom_call" | custom-call | tf_op jit(solution)/shard_map/strip/pallas_call | solution.py:443
  23.8 0.1 collective-permute-start.4
  23.9 1.6 %collective-permute-start.3 = (f32[48,128]{1,0:T(8,128)S(1)}, f32[48,128]{1,0:T(8,128)S(1)}, u32[]{:S(2)}, u32[]{:S(2)}) collective-permute-start(f32[48,128]{1,0:T(8,128)S(1)} %get-tuple-element.30.v0), channel_id=1, source_target_pairs={{0,2},{1,3},{2,0},{3,1},{4,6},{5,7},{6,4},{7,5},{8,10},{9,11},{10,... | collective-permute-start | bytes 73736 | tf_op jit(solution)/shard_map/ppermute | solution.py:456
  25.4 0.3 collective-permute-start.2
  25.7 0.0 copy-done.5
  25.7 0.0 copy-done.7
  25.7 0.0 copy-done.9
  25.7 0.0 copy-done.11
  25.7 1.0 %ready.1 = (f32[5,64,128]{2,1,0:T(8,128)S(1)}, f32[5,64,128]{2,1,0:T(8,128)S(1)}, bf16[256,2048]{1,0:T(8,128)(2,1)S(1)}, bf16[128,4096]{1,0:T(8,128)(2,1)S(1)}) custom-call(f32[64,128]{1,0:T(8,128)S(1)} %copy-done.5, f32[64,128]{1,0:T(8,128)S(1)} %copy-done.7, s32[64,128]{1,0:T(8,128)S(1)} %copy-done.9, s32[16,128]{1,0:T(8,128)S(1)} %bitcast.14, ...), custom_call_target="tpu_custom_call" | custom-call | tf_op jit(solution)/shard_map/ready/pallas_call | solution.py:457
  26.8 0.5 %collective-permute-done.4.v3 = f32[48,128]{1,0:T(8,128)S(1)} collective-permute-done((f32[48,128]{1,0:T(8,128)S(1)}, f32[48,128]{1,0:T(8,128)S(1)}, u32[]{:S(2)}, u32[]{:S(2)}) %collective-permute-start.4) | collective-permute-done | bytes 24608 | tf_op jit(solution)/shard_map/ppermute | solution.py:456
  27.3 0.5 %collective-permute-done.3.v2 = f32[48,128]{1,0:T(8,128)S(1)} collective-permute-done((f32[48,128]{1,0:T(8,128)S(1)}, f32[48,128]{1,0:T(8,128)S(1)}, u32[]{:S(2)}, u32[]{:S(2)}) %collective-permute-start.3) | collective-permute-done | bytes 24608 | tf_op jit(solution)/shard_map/ppermute | solution.py:456
  27.8 0.0 collective-permute-done.2.v1
  27.8 0.0 copy-done.1
  27.8 0.0 copy-done.3
  27.8 0.0 copy-done.13
  27.8 7.3 %adjoint.1 = f32[1024,128]{1,0:T(8,128)} custom-call(f32[1024,128]{1,0:T(8,128)S(1)} %bitcast.7, bf16[1024,128]{1,0:T(8,128)(2,1)S(1)} %bitcast.10, f32[1]{0:T(128)S(6)} %copy.9.weight, f32[16,128]{1,0:T(8,128)S(1)} %bitcast.16, f32[320,128]{1,0:T(8,128)S(1)} %collective-permute-done.got_a, f32[320,128]{1,0:T(8,128)S(1)} %collective-permute-done.1.got_b, ...), custom_call_target="tpu_custom_call" | custom-call | tf_op jit(solution)/shard_map/adjoint/pallas_call | solution.py:469
Async XLA Ops:
  0.0 1.0 %copy-start = (f32[1,16,64,128]{3,2,1,0:T(8,128)S(1)}, f32[1,16,64,128]{3,2,1,0:T(8,128)}, u32[]{:S(2)}) copy-start(f32[1,16,64,128]{3,2,1,0:T(8,128)} %param.8) | copy-start | bytes 1572868
  1.0 0.9 %copy-start.2 = (bf16[1,16,64,128]{3,2,1,0:T(8,128)(2,1)S(1)}, bf16[1,16,64,128]{3,2,1,0:T(8,128)(2,1)}, u32[]{:S(2)}) copy-start(bf16[1,16,64,128]{3,2,1,0:T(8,128)(2,1)} %param.9) | copy-start | bytes 786436
  2.0 0.8 %copy-start.4 = (f32[64,128]{1,0:T(8,128)S(1)}, f32[64,128]{1,0:T(8,128)}, u32[]{:S(2)}) copy-start(f32[64,128]{1,0:T(8,128)} %kappa.5) | copy-start | bytes 98308
  2.8 0.8 %copy-start.6 = (f32[64,128]{1,0:T(8,128)S(1)}, f32[64,128]{1,0:T(8,128)}, u32[]{:S(2)}) copy-start(f32[64,128]{1,0:T(8,128)} %scale.5) | copy-start | bytes 98308
  3.5 0.8 %copy-start.8 = (s32[64,128]{1,0:T(8,128)S(1)}, s32[64,128]{1,0:T(8,128)}, u32[]{:S(2)}) copy-start(s32[64,128]{1,0:T(8,128)} %ocean.5) | copy-start | bytes 98308
  4.3 0.7 %copy-start.10 = (s32[2048]{0:T(1024)S(1)}, s32[2048]{0:T(1024)}, u32[]{:S(2)}) copy-start(s32[2048]{0:T(1024)} %param.14) | copy-start | bytes 24580
  5.0 0.7 %copy-start.12 = (f32[2048]{0:T(1024)S(1)}, f32[2048]{0:T(1024)}, u32[]{:S(2)}) copy-start(f32[2048]{0:T(1024)} %param.15) | copy-start | bytes 24580
  5.7 20.0 %copy-start.5 = (f32[64,128]{1,0:T(8,128)S(1)}, f32[64,128]{1,0:T(8,128)}, u32[]{:S(2)}) copy-start(f32[64,128]{1,0:T(8,128)} %kappa.5) | copy-start | bytes 98308
  5.7 20.0 %copy-start.7 = (f32[64,128]{1,0:T(8,128)S(1)}, f32[64,128]{1,0:T(8,128)}, u32[]{:S(2)}) copy-start(f32[64,128]{1,0:T(8,128)} %scale.5) | copy-start | bytes 98308
  5.7 20.0 %copy-start.9 = (s32[64,128]{1,0:T(8,128)S(1)}, s32[64,128]{1,0:T(8,128)}, u32[]{:S(2)}) copy-start(s32[64,128]{1,0:T(8,128)} %ocean.5) | copy-start | bytes 98308
  5.7 20.1 %copy-start.11 = (s32[2048]{0:T(1024)S(1)}, s32[2048]{0:T(1024)}, u32[]{:S(2)}) copy-start(s32[2048]{0:T(1024)} %param.14) | copy-start | bytes 24580
  5.7 22.1 %copy-start.1 = (f32[1,16,64,128]{3,2,1,0:T(8,128)S(1)}, f32[1,16,64,128]{3,2,1,0:T(8,128)}, u32[]{:S(2)}) copy-start(f32[1,16,64,128]{3,2,1,0:T(8,128)} %param.8) | copy-start | bytes 1572868
  5.7 22.1 %copy-start.3 = (bf16[1,16,64,128]{3,2,1,0:T(8,128)(2,1)S(1)}, bf16[1,16,64,128]{3,2,1,0:T(8,128)(2,1)}, u32[]{:S(2)}) copy-start(bf16[1,16,64,128]{3,2,1,0:T(8,128)(2,1)} %param.9) | copy-start | bytes 786436
  5.7 22.1 %copy-start.13 = (f32[2048]{0:T(1024)S(1)}, f32[2048]{0:T(1024)}, u32[]{:S(2)}) copy-start(f32[2048]{0:T(1024)} %param.15) | copy-start | bytes 24580
  8.8 10.0 %collective-permute-start = (f32[320,128]{1,0:T(8,128)S(1)}, f32[320,128]{1,0:T(8,128)S(1)}, u32[]{:S(2)}, u32[]{:S(2)}) collective-permute-start(f32[320,128]{1,0:T(8,128)S(1)} %get-tuple-element.18.sent_a), channel_id=1, source_target_pairs={{0,4},{4,0},{8,12},{12,8},{16,20},{20,16},{24,28},{28,24},{1,5},{5... | collective-permute-start | bytes 491528 | tf_op jit(solution)/shard_map/ppermute | solution.py:434
  11.9 8.4 %collective-permute-start.1 = (f32[320,128]{1,0:T(8,128)S(1)}, f32[320,128]{1,0:T(8,128)S(1)}, u32[]{:S(2)}, u32[]{:S(2)}) collective-permute-start(f32[320,128]{1,0:T(8,128)S(1)} %get-tuple-element.19.sent_b), channel_id=1, source_target_pairs={{0,28},{4,8},{8,4},{12,16},{16,12},{20,24},{24,20},{28,0},{1,29},{... | collective-permute-start | bytes 491528 | tf_op jit(solution)/shard_map/ppermute | solution.py:433
  23.8 3.5 %collective-permute-start.4 = (f32[48,128]{1,0:T(8,128)S(1)}, f32[48,128]{1,0:T(8,128)S(1)}, u32[]{:S(2)}, u32[]{:S(2)}) collective-permute-start(f32[48,128]{1,0:T(8,128)S(1)} %get-tuple-element.30.v0), channel_id=1, source_target_pairs={{0,3},{1,2},{2,1},{3,0},{4,7},{5,6},{6,5},{7,4},{8,11},{9,10},{10,... | collective-permute-start | bytes 73736 | tf_op jit(solution)/shard_map/ppermute | solution.py:456
  23.9 3.9 %collective-permute-start.3 = (f32[48,128]{1,0:T(8,128)S(1)}, f32[48,128]{1,0:T(8,128)S(1)}, u32[]{:S(2)}, u32[]{:S(2)}) collective-permute-start(f32[48,128]{1,0:T(8,128)S(1)} %get-tuple-element.30.v0), channel_id=1, source_target_pairs={{0,2},{1,3},{2,0},{3,1},{4,6},{5,7},{6,4},{7,5},{8,10},{9,11},{10,... | collective-permute-start | bytes 73736 | tf_op jit(solution)/shard_map/ppermute | solution.py:456
  25.4 2.3 %collective-permute-start.2 = (f32[48,128]{1,0:T(8,128)S(1)}, f32[48,128]{1,0:T(8,128)S(1)}, u32[]{:S(2)}, u32[]{:S(2)}) collective-permute-start(f32[48,128]{1,0:T(8,128)S(1)} %get-tuple-element.30.v0), channel_id=1, source_target_pairs={{0,1},{1,0},{2,3},{3,2},{4,5},{5,4},{6,7},{7,6},{8,9},{9,8},{10,11... | collective-permute-start | bytes 73736 | tf_op jit(solution)/shard_map/ppermute | solution.py:456

commit v5 on v4

--- a/solution.py
+++ b/solution.py
@@ -40,10 +40,12 @@
         assert columns == 128 and levels == 16 and rows % 16 == 0 and obs % 256 == 0 and STEPS == 8
         self.field = levels * rows
         self.group = self.field // 2
-        self.half = self.field // 4
         self.short = self.field // 8
-        self.at_coeff = self.half
-        self.at_obs = self.at_coeff + rows // 2
+        self.tiles = rows // SUB
+        assert self.tiles == 8
+        self.at_members = self.short
+        self.at_coeff = self.at_members + rows
+        self.at_obs = self.at_coeff + 3 * SUB
         self.obs_rows = obs // 128
         self.payload = self.at_obs + 2 * self.obs_rows
 
@@ -55,51 +57,59 @@
     return value
 
 
-def early(tiles):
-    tile = lax.axis_index("tile")
-    return (tile == 0) | ((lax.rem(tile, 2) == 1) & (tile != tiles - 1))
-
-
-def pack_kernel(z, tiles, alpha, members, kappa, scale, ocean, cell, weight, out_a, out_b, x, coeff, y):
+def pack_kernel(
+    z, alpha_hbm, members_hbm, kappa_hbm, scale_hbm, ocean_hbm, cell_hbm, weight_hbm,
+    out_far, out_near, alpha, members, kappa, scale, ocean, cell, weight, sems,
+):
+    pairs = (
+        (members_hbm, members), (alpha_hbm, alpha), (kappa_hbm, kappa), (scale_hbm, scale), (ocean_hbm, ocean),
+        (cell_hbm, cell), (weight_hbm, weight),
+    )
+    copies = [pltpu.make_async_copy(a, b, sems.at[k]) for k, (a, b) in enumerate(pairs)]
+    for copy in copies:
+        copy.start()
     even = lax.rem(lax.axis_index("tile"), 2) == 0
 
     def put(where, right, left):
-        out_a[where, :] = jnp.where(even, right, left)
-        out_b[where, :] = jnp.where(even, left, right)
-
-    block = 4 * SUB
+        out_near[where, :] = jnp.where(even, right, left)
+        out_far[where, :] = jnp.where(even, left, right)
+
+    for copy in copies[2:]:
+        copy.wait()
+    lane = lanes(SUB)
+    for k, ref in enumerate((kappa, scale, ocean)):
+        right, left = [], []
+        for t in range(z.tiles):
+            value = ref[pl.ds(t * SUB, SUB), :].astype(F32)
+            right.append(roll(value, EDGE * (t + 1)))
+            left.append(roll(value, EDGE * t))
+        put(pl.ds(z.at_coeff + k * SUB, SUB), overlay(right, lane >> 4), overlay(left, lane >> 4))
+    n = z.obs_rows
+    for at, value in ((z.at_obs, cell[...].astype(F32)), (z.at_obs + n, weight[...])):
+        out_near[pl.ds(at, n), :] = value
+        out_far[pl.ds(at, n), :] = value
+    copies[0].wait()
+    block = 2 * SUB
     lane = lanes(block)
-    for q in range(z.half // block):
+    for t in range(z.rows // block):
         right, left = [], []
         for g in range(2):
-            for h in range(2):
-                rows = pl.ds(g * z.group + h * z.half + q * block, block)
-                a, m = alpha[rows, :], members[rows, :].astype(F32)
-                base = 64 * g + 32 * h
-                right += [roll(m, base + EDGE), roll(a, base + 2 * EDGE)]
-                left += [roll(m, base), roll(a, base + EDGE)]
-        put(pl.ds(q * block, block), overlay(right, lane >> 4), overlay(left, lane >> 4))
-    half = z.rows // 2
-    lane = lanes(half)
-    right, left = [], []
-    for h in range(2):
-        rows = pl.ds(h * half, half)
-        for k, ref in enumerate((kappa, scale, ocean)):
-            value = ref[rows, :].astype(F32)
-            base = 64 * h + EDGE * k
-            right.append(roll(value, base - (128 - EDGE)))
-            left.append(roll(value, base))
-        right.append(right[-1])
-        left.append(left[-1])
-    put(pl.ds(z.at_coeff, half), overlay(right, lane >> 4), overlay(left, lane >> 4))
-    n = z.obs_rows
-    for at, value in ((z.at_obs, cell[...].astype(F32)), (z.at_obs + n, weight[...])):
-        out_a[pl.ds(at, n), :] = value
-        out_b[pl.ds(at, n), :] = value
-
-    @pl.when(early(tiles))
-    def _():
-        forward_sweep(z, alpha, kappa, scale, ocean, coeff, x, y)
+            for part in range(SUB):
+                value = members[pl.ds(g * z.group + part * z.rows + t * block, block), :].astype(F32)
+                base = 64 * g + STEPS * part
+                right.append(roll(value, base + STEPS))
+                left.append(roll(value, base))
+        put(pl.ds(z.at_members + t * block, block), overlay(right, lane >> 3), overlay(left, lane >> 3))
+    copies[1].wait()
+    for t in range(z.short // block):
+        right, left = [], []
+        for g in range(2):
+            for h in range(4):
+                value = alpha[pl.ds(g * z.group + h * z.short + t * block, block), :]
+                base = 64 * g + EDGE * h
+                right.append(roll(value, base + EDGE))
+                left.append(roll(value, base))
+        put(pl.ds(t * block, block), overlay(right, lane >> 4), overlay(left, lane >> 4))
 
 
 def up(value):
@@ -229,17 +239,8 @@
     sweep([(x, y, coeff, z.levels)], z.rows)
 
 
-def main_kernel(z, tiles, swept, alpha, members, weight, kappa, scale, ocean, cell, out, hot, x, coeff, y, both):
-    first = early(tiles)
-
-    @pl.when(first)
-    def _():
-        x[...] = swept[...]
-
-    @pl.when(jnp.logical_not(first))
-    def _():
-        forward_sweep(z, alpha, kappa, scale, ocean, coeff, x, y)
-
+def main_kernel(z, alpha, members, weight, kappa, scale, ocean, cell, out, hot, x, coeff, y, both):
+    forward_sweep(z, alpha, kappa, scale, ocean, coeff, x, y)
     lane = lanes(z.group)
     inner = (lane >= STEPS) & (lane < z.columns - STEPS)
     for g in range(2):
@@ -252,35 +253,52 @@
 
 
 def strip_kernel(
-    z, inner, sent_a, sent_b, got_a, got_b, cell, weight, out, strip_members, strip_coeff, hot, coeff, x, y, outer, beside
+    z, inner, members, sent_far, sent_near, got_far, got_near, cell, weight,
+    out, strip_members, strip_coeff, hot, coeff, x, y, outer, beside,
 ):
     even = lax.rem(lax.axis_index("tile"), 2) == 0
 
     def parts(rows):
-        sa, sb, ga, gb = sent_a[rows, :], sent_b[rows, :], got_a[rows, :], got_b[rows, :]
-        pick = lambda p, q: jnp.where(even, p, q)
-        return pick(sa, sb), pick(ga, gb), pick(gb, ga), pick(sb, sa)
+        pick = lambda p, q: jnp.where(even, p[rows, :], q[rows, :])
+        return (
+            pick(sent_near, sent_far),
+            pick(got_near, got_far),
+            pick(got_far, got_near),
+            pick(sent_far, sent_near),
+        )
 
     clear_ends(x, y)
     lane = lanes(SUB)
-    for q in range(z.half // SUB):
+    part_of, side = (lane >> 4) & 3, lane >> 6
+    for k in range(3):
+        four = parts(pl.ds(z.at_coeff + k * SUB, SUB))
+        for t in range(z.tiles):
+            pieces = [roll(four[p], EDGE * p + 64 * g - EDGE * t) for g in range(2) for p in range(4)]
+            strip_coeff[k, pl.ds(t * SUB, SUB), :] = overlay(pieces, lane >> 4)
+    for q in range(z.short // SUB):
         four = parts(pl.ds(q * SUB, SUB))
-        for h in range(2):
-            at = h * z.half + q * SUB
-            for offset in (0, -EDGE):
-                pieces = [roll(part, EDGE * p - 32 * h + offset) for p, part in enumerate(four)]
-                value = overlay(pieces, (lane >> 4) & 3)
-                if offset:
-                    x[pl.ds(SUB + at, SUB), :] = value
-                else:
-                    strip_members[pl.ds(at, SUB), :] = value * weight[0]
-    half = z.rows // 2
-    four = parts(pl.ds(z.at_coeff, half))
-    lane = lanes(half)
-    for k in range(3):
-        for h in range(2):
-            pieces = [roll(four[p], EDGE * p + 64 * g - 64 * h - EDGE * k) for g in range(2) for p in range(4)]
-            strip_coeff[k, pl.ds(h * half, half), :] = overlay(pieces, lane >> 4)
+        for h in range(4):
+            pieces = [roll(four[p], EDGE * (p - h)) for p in range(4)]
+            x[pl.ds(SUB + h * z.short + q * SUB, SUB), :] = overlay(pieces, part_of)
+    block = 2 * SUB
+    wide_lane = lanes(block)
+    for t in range(z.rows // block):
+        rows = pl.ds(z.at_members + t * block, block)
+        _, right, left, _ = parts(rows)
+        for part in range(SUB):
+            at = part * z.rows + t * block
+            value = jnp.where(
+                (wide_lane & 32) == 0,
+                roll(right, EDGE - STEPS * part),
+                roll(left, 2 * EDGE + STEPS - STEPS * part),
+            )
+            for g in range(2):
+                own = members[pl.ds(g * z.group + at, block), :].astype(F32)
+                mine = (wide_lane >> 6) == g
+                inside = (wide_lane >> 4) & 3
+                value = jnp.where(mine & (inside == 0), roll(own, EDGE + 64 * g), value)
+                value = jnp.where(mine & (inside == 3), roll(own, 48 + 64 * g), value)
+            strip_members[pl.ds(at, block), :] = value * weight[0]
     put_coefficients(coeff, coefficients(strip_coeff[0], strip_coeff[1], strip_coeff[2], True))
     sweep([(x, y, coeff, z.levels // 2)], z.rows)
     unit = lanes(z.short) >> 3
@@ -303,17 +321,17 @@
     out[:n, :] = out[:n, :] + inner[...]
 
 
-def beside_rows(z, got_a, got_b, at):
+def beside_rows(z, got_far, got_near, at):
     even = lax.rem(lax.axis_index("tile"), 2) == 0
-    a, b = got_a[pl.ds(at, z.obs_rows), :], got_b[pl.ds(at, z.obs_rows), :]
-    return jnp.where(even, a, b), jnp.where(even, b, a)
-
-
-def ready_kernel(z, kappa, scale, ocean, cell, got_a, got_b, strip_coeff, coeff, strip_c, own_lane, beside_lane):
+    far, near = got_far[pl.ds(at, z.obs_rows), :], got_near[pl.ds(at, z.obs_rows), :]
+    return jnp.where(even, near, far), jnp.where(even, far, near)
+
+
+def ready_kernel(z, kappa, scale, ocean, cell, got_far, got_near, strip_coeff, coeff, strip_c, own_lane, beside_lane):
     put_coefficients(coeff, coefficients(kappa[...], scale[...], ocean[...].astype(F32), False))
     put_coefficients(strip_c, coefficients(strip_coeff[0], strip_coeff[1], strip_coeff[2], False))
     _, right_window, left_window = windows_of(z)
-    right, left = beside_rows(z, got_a, got_b, z.at_obs)
+    right, left = beside_rows(z, got_far, got_near, z.at_obs)
     n = z.obs_rows
     for r in range(n):
         at = pl.ds(r * 128, 128)
@@ -325,18 +343,14 @@
 
 
 def adjoint_kernel(
-    z, alpha_hbm, members_hbm, weight, obs_weight, got_a, got_b, strip_members, coeff, strip_c,
+    z, alpha, members, weight, obs_weight, got_far, got_near, strip_members, coeff, strip_c,
     own_row, own_lane, beside_row, beside_lane, v0, v1, v2, v3,
-    out_hbm, x, y, strip, spare, beside, spread, alpha, members, out, sems,
+    out_hbm, x, y, strip, spare, beside, spread, out, sems,
 ):
-    bring_alpha = pltpu.make_async_copy(alpha_hbm, alpha, sems.at[0])
-    bring_members = pltpu.make_async_copy(members_hbm, members, sems.at[1])
-    bring_members.start()
-    bring_alpha.start()
     clear_ends(x, y, strip, spare)
     value = (v0[...] + v1[...]) + (v2[...] + v3[...])
     n = z.obs_rows
-    right_weight, left_weight = beside_rows(z, got_a, got_b, z.at_obs + n)
+    right_weight, left_weight = beside_rows(z, got_far, got_near, z.at_obs + n)
 
     def spread_out(amounts, row_hot, lane_hot):
         wide = lane_hot.shape[0]
@@ -377,10 +391,8 @@
             value = jnp.where(mine & (part == 3), roll(field, 48 + 64 * g), value)
         strip[pl.ds(SUB + q * SUB, SUB), :] = value * strip_members[pl.ds(q * SUB, SUB), :]
     here = pl.ds(SUB, z.field)
-    bring_members.wait()
     x[here, :] = x[here, :] * (members[...].astype(F32) * weight[0])
     sweep([(x, y, coeff, z.levels), (strip, spare, strip_c, z.levels // 2)], z.rows)
-    bring_alpha.wait()
     sent = []
     for part in range(z.levels // 2):
         for t in range(z.rows // SUB):
@@ -395,7 +407,7 @@
         if part % 2:
             for g in range(2):
                 rows = pl.ds(g * z.group + (part - 1) * z.rows, 2 * z.rows)
-                sent.append(pltpu.make_async_copy(out.at[rows, :], out_hbm.at[rows, :], sems.at[2 + len(sent)]))
+                sent.append(pltpu.make_async_copy(out.at[rows, :], out_hbm.at[rows, :], sems.at[len(sent)]))
                 sent[-1].start()
     for copy in sent:
         copy.wait()
@@ -412,7 +424,7 @@
     weight = obs_weight.reshape(z.obs_rows, 128)
     smem = pl.BlockSpec(memory_space=pltpu.SMEM)
     whole = pl.BlockSpec(memory_space=pltpu.VMEM)
-    stays = pl.BlockSpec(memory_space=pl.ANY)
+    stays = pl.BlockSpec(memory_space=pltpu.HBM)
     sds = jax.ShapeDtypeStruct
     main_field = pltpu.VMEM((z.field + 2 * SUB, 128), F32)
     strip_field = pltpu.VMEM((z.group + 2 * SUB, 128), F32)
@@ -421,25 +433,28 @@
     payload = sds((z.payload, 128), F32)
     limit = pltpu.CompilerParams(vmem_limit_bytes=24 << 20)
     call = functools.partial(pl.pallas_call, compiler_params=limit)
-    sent_a, sent_b, swept = call(
-        functools.partial(pack_kernel, z, tiles),
-        out_shape=(payload, payload, sds((z.field + 2 * SUB, 128), F32)),
-        out_specs=(whole, whole, whole),
-        scratch_shapes=[coeff, main_field],
+    given = (alpha, members, kappa, norm_scale, land_sea, cell, weight)
+    sent_far, sent_near, *given = call(
+        functools.partial(pack_kernel, z),
+        out_shape=(payload, payload, *(sds(v.shape, v.dtype) for v in given)),
+        in_specs=[stays] * 7,
+        out_specs=(whole,) * 9,
+        scratch_shapes=[pltpu.SemaphoreType.DMA((7,))],
         name="pack",
-    )(alpha, members, kappa, norm_scale, land_sea, cell, weight)
+    )(*given)
+    alpha, members, kappa, norm_scale, land_sea, cell, weight = given
     near = [(i, i ^ 1) for i in range(tiles)]
     far = [(i, (i + 1) % tiles if i % 2 else (i - 1) % tiles) for i in range(tiles)]
-    got_b = lax.ppermute(sent_b, "tile", far)
-    got_a = lax.ppermute(sent_a, "tile", near)
+    got_far = lax.ppermute(sent_far, "tile", far)
+    got_near = lax.ppermute(sent_near, "tile", near)
     inner, own_row = call(
-        functools.partial(main_kernel, z, tiles),
+        functools.partial(main_kernel, z),
         out_shape=(sds((z.obs_rows, 128), F32), sds((z.group, z.obs), BF16)),
-        in_specs=[whole] * 3 + [smem] + [whole] * 4,
+        in_specs=[whole] * 2 + [smem] + [whole] * 4,
         out_specs=(whole, whole),
         scratch_shapes=[main_field, coeff, main_field, pltpu.VMEM((z.group, 512), BF16)],
         name="main",
-    )(swept, alpha, members, mem_weight, kappa, norm_scale, land_sea, cell)
+    )(alpha, members, mem_weight, kappa, norm_scale, land_sea, cell)
     values, strip_members, strip_coeff, beside_row = call(
         functools.partial(strip_kernel, z),
         out_shape=(
@@ -448,11 +463,11 @@
             sds((3, z.rows, 128), F32),
             sds((z.short, 2 * z.obs), BF16),
         ),
-        in_specs=[whole] * 6 + [smem],
+        in_specs=[whole] * 7 + [smem],
         out_specs=(whole,) * 4,
         scratch_shapes=[coeff, strip_field, strip_field, packed, packed],
         name="strip",
-    )(inner, sent_a, sent_b, got_a, got_b, cell, mem_weight)
+    )(inner, members, sent_far, sent_near, got_far, got_near, cell, mem_weight)
     others = [lax.ppermute(values, "mem", [(i, i ^ k) for i in range(holders)]) for k in range(1, holders)]
     main_c, strip_c, own_lane, beside_lane = call(
         functools.partial(ready_kernel, z),
@@ -465,11 +480,11 @@
         in_specs=[whole] * 7,
         out_specs=(whole,) * 4,
         name="ready",
-    )(kappa, norm_scale, land_sea, cell, got_a, got_b, strip_coeff)
+    )(kappa, norm_scale, land_sea, cell, got_far, got_near, strip_coeff)
     product = call(
         functools.partial(adjoint_kernel, z),
         out_shape=sds((z.field, z.columns), F32),
-        in_specs=[stays, stays, smem] + [whole] * 14,
+        in_specs=[whole, whole, smem] + [whole] * 14,
         out_specs=stays,
         scratch_shapes=[
             main_field,
@@ -479,13 +494,11 @@
             pltpu.VMEM((z.short, 128), F32),
             pltpu.VMEM((512, 2 * z.obs), BF16),
             pltpu.VMEM((z.field, 128), F32),
-            pltpu.VMEM((z.field, 128), BF16),
-            pltpu.VMEM((z.field, 128), F32),
-            pltpu.SemaphoreType.DMA((2 + z.levels // 2,)),
+            pltpu.SemaphoreType.DMA((z.levels // 2,)),
         ],
         name="adjoint",
     )(
-        alpha, members, mem_weight, weight, got_a, got_b, strip_members, main_c, strip_c,
+        alpha, members, mem_weight, weight, got_far, got_near, strip_members, main_c, strip_c,
         own_row, own_lane, beside_row, beside_lane, values, *others,
     )
     return product.reshape(shape)

time: 35.5 us -> 34.9 us (0.983)
  waiting for transfers between devices: 6.15 us -> 3.31 us
  starting transfers between devices: 5.88 us -> 8 us
    ppermute x2, waiting for transfers between devices: 5.15 us -> 1.31 us  [the longest x1 1.3 us: local(): got_near = lax.ppermute(sent_near, 'tile', near)]
    ppermute x2, starting transfers between devices: 3.96 us -> 6.07 us  [the longest x1 6.07 us: local(): got_far = lax.ppermute(sent_far, 'tile', far)]
    ppermute x3, waiting for transfers between devices: 1 us -> 2.01 us  [local(): lax.ppermute(values, 'mem', [(i, i ^ k) for i in range(holders)])]
    unnamed x28 -> x14, local copies, waits for them, and re-layouts: 5.68 us -> 5.66 us
  transfers between devices with their start and end apart: 5 -> 5, of which waited for: 4 -> 3; matrix products, arithmetic and copies ran while one was open for 0% -> 0% of each run, Pallas kernels for 8% -> 15%
where the time goes in v5:
time: 34.9 us; the launch traced here: 34.4 us
  Pallas kernels  16.7 us (48%)
  starting transfers between devices  8 us (23%)
  local copies, waits for them, and re-layouts  5.66 us (16%)
  waiting for transfers between devices  3.31 us (9%)
  between operations  0.7 us (2%)
    pallas_call x1, Pallas kernels, local(): call(functools.partial(adjoint_kernel, z), out_shape=sds((z.field, z.colu...  7.08 us
    ppermute x1, starting transfers between devices, local(): got_far = lax.ppermute(sent_far, 'tile', far)  6.07 us
    unnamed x14, local copies, waits for them, and re-layouts  5.66 us
    pallas_call x1, Pallas kernels, local(): call(functools.partial(main_kernel, z), out_shape=(sds((z.obs_rows, 128),...  4.15 us
    pallas_call x1, Pallas kernels, local(): call(functools.partial(strip_kernel, z), out_shape=(sds((3 * z.obs_rows,...  3.6 us
    ppermute x3, waiting for transfers between devices, local(): lax.ppermute(values, 'mem', [(i, i ^ k) for i in range(holders)])  2.01 us
    ppermute x3, starting transfers between devices, local(): lax.ppermute(values, 'mem', [(i, i ^ k) for i in range(holders)])  1.93 us
    ppermute x1, waiting for transfers between devices, local(): got_near = lax.ppermute(sent_near, 'tile', near)  1.3 us
  transfers between devices with their start and end apart: 5, of which 3 were waited for; matrix products, arithmetic and copies ran while one was open for 0% of the time, Pallas kernels for 15%

profile of v5, /device:TPU:0, one launch (start us, length us, event | category | flops | bytes accessed | tf_op | source)
XLA Modules:
  0.0 34.4 jit_solution(9801375661307607732)
XLA Ops:
  0.0 0.0 copy-start
  0.0 1.0 %copy-done = f32[1,16,64,128]{3,2,1,0:T(8,128)S(1)} copy-done((f32[1,16,64,128]{3,2,1,0:T(8,128)S(1)}, f32[1,16,64,128]{3,2,1,0:T(8,128)}, u32[]{:S(2)}) %copy-start) | copy-done | bytes 524312
  1.0 0.0 copy-start.1
  1.0 0.9 %copy-done.1 = bf16[1,16,64,128]{3,2,1,0:T(8,128)(2,1)S(1)} copy-done((bf16[1,16,64,128]{3,2,1,0:T(8,128)(2,1)S(1)}, bf16[1,16,64,128]{3,2,1,0:T(8,128)(2,1)}, u32[]{:S(2)}) %copy-start.1) | copy-done | bytes 262168
  2.0 0.0 copy-start.2
  2.0 0.8 %copy-done.2 = f32[64,128]{1,0:T(8,128)S(1)} copy-done((f32[64,128]{1,0:T(8,128)S(1)}, f32[64,128]{1,0:T(8,128)}, u32[]{:S(2)}) %copy-start.2) | copy-done | bytes 32792
  2.8 0.0 copy-start.3
  2.8 0.8 %copy-done.3 = f32[64,128]{1,0:T(8,128)S(1)} copy-done((f32[64,128]{1,0:T(8,128)S(1)}, f32[64,128]{1,0:T(8,128)}, u32[]{:S(2)}) %copy-start.3) | copy-done | bytes 32792
  3.5 0.0 copy-start.4
  3.5 0.8 %copy-done.4 = s32[64,128]{1,0:T(8,128)S(1)} copy-done((s32[64,128]{1,0:T(8,128)S(1)}, s32[64,128]{1,0:T(8,128)}, u32[]{:S(2)}) %copy-start.4) | copy-done | bytes 32792
  4.3 0.0 copy-start.5
  4.3 0.7 %copy-done.5 = s32[2048]{0:T(1024)S(1)} copy-done((s32[2048]{0:T(1024)S(1)}, s32[2048]{0:T(1024)}, u32[]{:S(2)}) %copy-start.5) | copy-done | bytes 8216
  5.0 0.0 copy-start.6
  5.0 0.7 %copy-done.6 = f32[2048]{0:T(1024)S(1)} copy-done((f32[2048]{0:T(1024)S(1)}, f32[2048]{0:T(1024)}, u32[]{:S(2)}) %copy-start.6) | copy-done | bytes 8216
  5.7 0.9 %pack.1 = (f32[248,128]{1,0:T(8,128)S(1)}, f32[248,128]{1,0:T(8,128)S(1)}, f32[1024,128]{1,0:T(8,128)S(1)}, bf16[1024,128]{1,0:T(8,128)(2,1)S(1)}, f32[64,128]{1...) custom-call(f32[1024,128]{1,0:T(8,128)S(1)} %bitcast.5, ...), custom_call_target="tpu_custom_call" | custom-call | tf_op jit(solution)/shard_map/pack/pallas_call | solution.py:437
  6.6 6.1 %collective-permute-start = (f32[248,128]{1,0:T(8,128)S(1)}, f32[248,128]{1,0:T(8,128)S(1)}, u32[]{:S(2)}, u32[]{:S(2)}) collective-permute-start(f32[248,128]{1,0:T(8,128)S(1)} %get-tuple-element.27.sent_far), channel_id=1, source_target_pairs={{0,28},{4,8},{8,4},{12,16},{16,12},{20,24},{24,20},{28,0},{1,29},{... | collective-permute-start | bytes 380936 | tf_op jit(solution)/shard_map/ppermute | solution.py:448
  12.6 0.0 collective-permute-start.1
  13.3 4.2 %main.1 = (f32[16,128]{1,0:T(8,128)S(1)}, bf16[512,2048]{1,0:T(8,128)(2,1)S(1)}) custom-call(f32[1024,128]{1,0:T(8,128)S(1)} %get-tuple-element.24.alpha, bf16[1024,128]{1,0:T(8,128)(2,1)S(1)} %get-tuple-element.25.members, f32[1]{0:T(128)S(6)} %copy.9.weight, f32[64,128]{1,0:T(8,128)S(1)} %get-tuple-element.29.kappa, ...), custom_call_target="tpu_custom_call" | custom-call | tf_op jit(solution)/shard_map/main/pallas_call | solution.py:450
  17.5 0.0 collective-permute-done.got_far
  17.5 1.3 %collective-permute-done.1.got_near = f32[248,128]{1,0:T(8,128)S(1)} collective-permute-done((f32[248,128]{1,0:T(8,128)S(1)}, f32[248,128]{1,0:T(8,128)S(1)}, u32[]{:S(2)}, u32[]{:S(2)}) %collective-permute-start.1) | collective-permute-done | bytes 127008 | tf_op jit(solution)/shard_map/ppermute | solution.py:449
  18.8 3.6 %strip.1 = (f32[48,128]{1,0:T(8,128)S(1)}, f32[512,128]{1,0:T(8,128)S(1)}, f32[3,64,128]{2,1,0:T(8,128)S(1)}, bf16[128,4096]{1,0:T(8,128)(2,1)S(1)}) custom-call(f32[16,128]{1,0:T(8,128)S(1)} %get-tuple-element.33.inner, bf16[1024,128]{1,0:T(8,128)(2,1)S(1)} %get-tuple-element.25.members, f32[248,128]{1,0:T(8,128)S(1)} %get-tuple-element.27.sent_far, ...), custom_call_target="tpu_custom_call" | custom-call | tf_op jit(solution)/shard_map/strip/pallas_call | solution.py:458
  22.4 1.1 %collective-permute-start.4 = (f32[48,128]{1,0:T(8,128)S(1)}, f32[48,128]{1,0:T(8,128)S(1)}, u32[]{:S(2)}, u32[]{:S(2)}) collective-permute-start(f32[48,128]{1,0:T(8,128)S(1)} %get-tuple-element.42.v0), channel_id=1, source_target_pairs={{0,3},{1,2},{2,1},{3,0},{4,7},{5,6},{6,5},{7,4},{8,11},{9,10},{10,... | collective-permute-start | bytes 73736 | tf_op jit(solution)/shard_map/ppermute | solution.py:471
  23.5 0.5 %collective-permute-start.3 = (f32[48,128]{1,0:T(8,128)S(1)}, f32[48,128]{1,0:T(8,128)S(1)}, u32[]{:S(2)}, u32[]{:S(2)}) collective-permute-start(f32[48,128]{1,0:T(8,128)S(1)} %get-tuple-element.42.v0), channel_id=1, source_target_pairs={{0,2},{1,3},{2,0},{3,1},{4,6},{5,7},{6,4},{7,5},{8,10},{9,11},{10,... | collective-permute-start | bytes 73736 | tf_op jit(solution)/shard_map/ppermute | solution.py:471
  24.0 0.3 collective-permute-start.2
  24.3 1.0 %ready.1 = (f32[5,64,128]{2,1,0:T(8,128)S(1)}, f32[5,64,128]{2,1,0:T(8,128)S(1)}, bf16[256,2048]{1,0:T(8,128)(2,1)S(1)}, bf16[128,4096]{1,0:T(8,128)(2,1)S(1)}) custom-call(f32[64,128]{1,0:T(8,128)S(1)} %get-tuple-element.29.kappa, f32[64,128]{1,0:T(8,128)S(1)} %get-tuple-element.30.scale, s32[64,128]{1,0:T(8,128)S(1)} %get-tuple-element.31.ocean, ...), custom_call_target="tpu_custom_call" | custom-call | tf_op jit(solution)/shard_map/ready/pallas_call | solution.py:472
  25.3 0.5 %collective-permute-done.4.v3 = f32[48,128]{1,0:T(8,128)S(1)} collective-permute-done((f32[48,128]{1,0:T(8,128)S(1)}, f32[48,128]{1,0:T(8,128)S(1)}, u32[]{:S(2)}, u32[]{:S(2)}) %collective-permute-start.4) | collective-permute-done | bytes 24608 | tf_op jit(solution)/shard_map/ppermute | solution.py:471
  25.8 1.5 %collective-permute-done.3.v2 = f32[48,128]{1,0:T(8,128)S(1)} collective-permute-done((f32[48,128]{1,0:T(8,128)S(1)}, f32[48,128]{1,0:T(8,128)S(1)}, u32[]{:S(2)}, u32[]{:S(2)}) %collective-permute-start.3) | collective-permute-done | bytes 24608 | tf_op jit(solution)/shard_map/ppermute | solution.py:471
  27.3 0.0 collective-permute-done.2.v1
  27.3 7.1 %adjoint.1 = f32[1024,128]{1,0:T(8,128)} custom-call(f32[1024,128]{1,0:T(8,128)S(1)} %get-tuple-element.24.alpha, bf16[1024,128]{1,0:T(8,128)(2,1)S(1)} %get-tuple-element.25.members, f32[1]{0:T(128)S(6)} %copy.9.weight, f32[16,128]{1,0:T(8,128)S(1)} %get-tuple-element.26.obs_weight, f32[248,128]{1,0:T(8,128)S(1)} %collective-permute-done.got_far, ...), custom_call_target="tpu_custom_call" | custom-call | tf_op jit(solution)/shard_map/adjoint/pallas_call | solution.py:484
Async XLA Ops:
  0.0 1.0 %copy-start = (f32[1,16,64,128]{3,2,1,0:T(8,128)S(1)}, f32[1,16,64,128]{3,2,1,0:T(8,128)}, u32[]{:S(2)}) copy-start(f32[1,16,64,128]{3,2,1,0:T(8,128)} %param.8) | copy-start | bytes 1572868
  1.0 0.9 %copy-start.1 = (bf16[1,16,64,128]{3,2,1,0:T(8,128)(2,1)S(1)}, bf16[1,16,64,128]{3,2,1,0:T(8,128)(2,1)}, u32[]{:S(2)}) copy-start(bf16[1,16,64,128]{3,2,1,0:T(8,128)(2,1)} %param.9) | copy-start | bytes 786436
  2.0 0.8 %copy-start.2 = (f32[64,128]{1,0:T(8,128)S(1)}, f32[64,128]{1,0:T(8,128)}, u32[]{:S(2)}) copy-start(f32[64,128]{1,0:T(8,128)} %kappa_hbm.1) | copy-start | bytes 98308
  2.8 0.8 %copy-start.3 = (f32[64,128]{1,0:T(8,128)S(1)}, f32[64,128]{1,0:T(8,128)}, u32[]{:S(2)}) copy-start(f32[64,128]{1,0:T(8,128)} %scale_hbm.1) | copy-start | bytes 98308
  3.5 0.8 %copy-start.4 = (s32[64,128]{1,0:T(8,128)S(1)}, s32[64,128]{1,0:T(8,128)}, u32[]{:S(2)}) copy-start(s32[64,128]{1,0:T(8,128)} %ocean_hbm.1) | copy-start | bytes 98308
  4.3 0.7 %copy-start.5 = (s32[2048]{0:T(1024)S(1)}, s32[2048]{0:T(1024)}, u32[]{:S(2)}) copy-start(s32[2048]{0:T(1024)} %param.14) | copy-start | bytes 24580
  5.0 0.7 %copy-start.6 = (f32[2048]{0:T(1024)S(1)}, f32[2048]{0:T(1024)}, u32[]{:S(2)}) copy-start(f32[2048]{0:T(1024)} %param.15) | copy-start | bytes 24580
  6.6 10.9 %collective-permute-start = (f32[248,128]{1,0:T(8,128)S(1)}, f32[248,128]{1,0:T(8,128)S(1)}, u32[]{:S(2)}, u32[]{:S(2)}) collective-permute-start(f32[248,128]{1,0:T(8,128)S(1)} %get-tuple-element.27.sent_far), channel_id=1, source_target_pairs={{0,28},{4,8},{8,4},{12,16},{16,12},{20,24},{24,20},{28,0},{1,29},{... | collective-permute-start | bytes 380936 | tf_op jit(solution)/shard_map/ppermute | solution.py:448
  12.6 6.1 %collective-permute-start.1 = (f32[248,128]{1,0:T(8,128)S(1)}, f32[248,128]{1,0:T(8,128)S(1)}, u32[]{:S(2)}, u32[]{:S(2)}) collective-permute-start(f32[248,128]{1,0:T(8,128)S(1)} %get-tuple-element.28.sent_near), channel_id=1, source_target_pairs={{0,4},{4,0},{8,12},{12,8},{16,20},{20,16},{24,28},{28,24},{1,5},{5... | collective-permute-start | bytes 380936 | tf_op jit(solution)/shard_map/ppermute | solution.py:449
  22.4 3.4 %collective-permute-start.4 = (f32[48,128]{1,0:T(8,128)S(1)}, f32[48,128]{1,0:T(8,128)S(1)}, u32[]{:S(2)}, u32[]{:S(2)}) collective-permute-start(f32[48,128]{1,0:T(8,128)S(1)} %get-tuple-element.42.v0), channel_id=1, source_target_pairs={{0,3},{1,2},{2,1},{3,0},{4,7},{5,6},{6,5},{7,4},{8,11},{9,10},{10,... | collective-permute-start | bytes 73736 | tf_op jit(solution)/shard_map/ppermute | solution.py:471
  23.5 3.8 %collective-permute-start.3 = (f32[48,128]{1,0:T(8,128)S(1)}, f32[48,128]{1,0:T(8,128)S(1)}, u32[]{:S(2)}, u32[]{:S(2)}) collective-permute-start(f32[48,128]{1,0:T(8,128)S(1)} %get-tuple-element.42.v0), channel_id=1, source_target_pairs={{0,2},{1,3},{2,0},{3,1},{4,6},{5,7},{6,4},{7,5},{8,10},{9,11},{10,... | collective-permute-start | bytes 73736 | tf_op jit(solution)/shard_map/ppermute | solution.py:471
  24.0 3.3 %collective-permute-start.2 = (f32[48,128]{1,0:T(8,128)S(1)}, f32[48,128]{1,0:T(8,128)S(1)}, u32[]{:S(2)}, u32[]{:S(2)}) collective-permute-start(f32[48,128]{1,0:T(8,128)S(1)} %get-tuple-element.42.v0), channel_id=1, source_target_pairs={{0,1},{1,0},{2,3},{3,2},{4,5},{5,4},{6,7},{7,6},{8,9},{9,8},{10,11... | collective-permute-start | bytes 73736 | tf_op jit(solution)/shard_map/ppermute | solution.py:471

commit v6 on v5

--- a/solution.py
+++ b/solution.py
@@ -245,7 +245,7 @@
     inner = (lane >= STEPS) & (lane < z.columns - STEPS)
     for g in range(2):
         rows = pl.ds(g * z.group, z.group)
-        value = x[pl.ds(SUB + g * z.group, z.group), :] * (members[rows, :].astype(F32) * weight[0])
+        value = x[pl.ds(SUB + g * z.group, z.group), :] * (members[rows, :].astype(F32) * weight[0:1, :])
         high, low = split(jnp.where(inner, value, 0.0))
         both[:, pl.ds(g * 128, 128)] = high
         both[:, pl.ds(256 + g * 128, 128)] = low
@@ -298,7 +298,7 @@
                 inside = (wide_lane >> 4) & 3
                 value = jnp.where(mine & (inside == 0), roll(own, EDGE + 64 * g), value)
                 value = jnp.where(mine & (inside == 3), roll(own, 48 + 64 * g), value)
-            strip_members[pl.ds(at, block), :] = value * weight[0]
+            strip_members[pl.ds(at, block), :] = value * weight[0:1, :]
     put_coefficients(coeff, coefficients(strip_coeff[0], strip_coeff[1], strip_coeff[2], True))
     sweep([(x, y, coeff, z.levels // 2)], z.rows)
     unit = lanes(z.short) >> 3
@@ -391,7 +391,7 @@
             value = jnp.where(mine & (part == 3), roll(field, 48 + 64 * g), value)
         strip[pl.ds(SUB + q * SUB, SUB), :] = value * strip_members[pl.ds(q * SUB, SUB), :]
     here = pl.ds(SUB, z.field)
-    x[here, :] = x[here, :] * (members[...].astype(F32) * weight[0])
+    x[here, :] = x[here, :] * (members[...].astype(F32) * weight[0:1, :])
     sweep([(x, y, coeff, z.levels), (strip, spare, strip_c, z.levels // 2)], z.rows)
     sent = []
     for part in range(z.levels // 2):
@@ -422,7 +422,6 @@
     members = members.reshape(z.field, z.columns)
     cell = obs_cell.reshape(z.obs_rows, 128)
     weight = obs_weight.reshape(z.obs_rows, 128)
-    smem = pl.BlockSpec(memory_space=pltpu.SMEM)
     whole = pl.BlockSpec(memory_space=pltpu.VMEM)
     stays = pl.BlockSpec(memory_space=pltpu.HBM)
     sds = jax.ShapeDtypeStruct
@@ -441,8 +440,9 @@
         out_specs=(whole,) * 9,
         scratch_shapes=[pltpu.SemaphoreType.DMA((7,))],
         name="pack",
-    )(*given)
+    )(*(pltpu.with_memory_space_constraint(v, pltpu.HBM) for v in given))
     alpha, members, kappa, norm_scale, land_sea, cell, weight = given
+    factor = jnp.broadcast_to(mem_weight, (SUB, 128))
     near = [(i, i ^ 1) for i in range(tiles)]
     far = [(i, (i + 1) % tiles if i % 2 else (i - 1) % tiles) for i in range(tiles)]
     got_far = lax.ppermute(sent_far, "tile", far)
@@ -450,11 +450,11 @@
     inner, own_row = call(
         functools.partial(main_kernel, z),
         out_shape=(sds((z.obs_rows, 128), F32), sds((z.group, z.obs), BF16)),
-        in_specs=[whole] * 2 + [smem] + [whole] * 4,
+        in_specs=[whole] * 7,
         out_specs=(whole, whole),
         scratch_shapes=[main_field, coeff, main_field, pltpu.VMEM((z.group, 512), BF16)],
         name="main",
-    )(alpha, members, mem_weight, kappa, norm_scale, land_sea, cell)
+    )(alpha, members, factor, kappa, norm_scale, land_sea, cell)
     values, strip_members, strip_coeff, beside_row = call(
         functools.partial(strip_kernel, z),
         out_shape=(
@@ -463,11 +463,11 @@
             sds((3, z.rows, 128), F32),
             sds((z.short, 2 * z.obs), BF16),
         ),
-        in_specs=[whole] * 7 + [smem],
+        in_specs=[whole] * 8,
         out_specs=(whole,) * 4,
         scratch_shapes=[coeff, strip_field, strip_field, packed, packed],
         name="strip",
-    )(inner, members, sent_far, sent_near, got_far, got_near, cell, mem_weight)
+    )(inner, members, sent_far, sent_near, got_far, got_near, cell, factor)
     others = [lax.ppermute(values, "mem", [(i, i ^ k) for i in range(holders)]) for k in range(1, holders)]
     main_c, strip_c, own_lane, beside_lane = call(
         functools.partial(ready_kernel, z),
@@ -484,7 +484,7 @@
     product = call(
         functools.partial(adjoint_kernel, z),
         out_shape=sds((z.field, z.columns), F32),
-        in_specs=[whole, whole, smem] + [whole] * 14,
+        in_specs=[whole] * 17,
         out_specs=stays,
         scratch_shapes=[
             main_field,
@@ -498,7 +498,7 @@
         ],
         name="adjoint",
     )(
-        alpha, members, mem_weight, weight, got_far, got_near, strip_members, main_c, strip_c,
+        alpha, members, factor, weight, got_far, got_near, strip_members, main_c, strip_c,
         own_row, own_lane, beside_row, beside_lane, values, *others,
     )
     return product.reshape(shape)

time: 34.9 us -> 29.9 us (0.86)
  local copies, waits for them, and re-layouts: 5.66 us -> 0.01 us
  Pallas kernels: 16.7 us -> 17.7 us
    unnamed x14 -> x0, local copies, waits for them, and re-layouts: 5.66 us -> none
    pallas_call x1, Pallas kernels: 0.89 us -> 1.77 us  [local(): call(functools.partial(pack_kernel, z), out_shape=(payload, payload, *(sd...]
  transfers between devices with their start and end apart: 5 -> 5, of which waited for: 3 -> 3; matrix products, arithmetic and copies ran while one was open for 0% -> 0% of each run, Pallas kernels for 15% -> 17%
where the time goes in v6:
time: 29.9 us; the launch traced here: 29.7 us
  Pallas kernels  17.7 us (59%)
  starting transfers between devices  8 us (27%)
  waiting for transfers between devices  3.32 us (11%)
  between operations  0.7 us (2%)
    pallas_call x1, Pallas kernels, local(): call(functools.partial(adjoint_kernel, z), out_shape=sds((z.field, z.colu...  7.14 us
    ppermute x1, starting transfers between devices, local(): got_far = lax.ppermute(sent_far, 'tile', far)  6.07 us
    pallas_call x1, Pallas kernels, local(): call(functools.partial(main_kernel, z), out_shape=(sds((z.obs_rows, 128),...  4.15 us
    pallas_call x1, Pallas kernels, local(): call(functools.partial(strip_kernel, z), out_shape=(sds((3 * z.obs_rows,...  3.59 us
    ppermute x3, waiting for transfers between devices, local(): lax.ppermute(values, 'mem', [(i, i ^ k) for i in range(holders)])  2.02 us
    ppermute x3, starting transfers between devices, local(): lax.ppermute(values, 'mem', [(i, i ^ k) for i in range(holders)])  1.93 us
    pallas_call x1, Pallas kernels, local(): call(functools.partial(pack_kernel, z), out_shape=(payload, payload, *(sd...  1.77 us
    ppermute x1, waiting for transfers between devices, local(): got_near = lax.ppermute(sent_near, 'tile', near)  1.3 us
  transfers between devices with their start and end apart: 5, of which 3 were waited for; matrix products, arithmetic and copies ran while one was open for 0% of the time, Pallas kernels for 17%

profile of v6, /device:TPU:0, one launch (start us, length us, event | category | flops | bytes accessed | tf_op | source)
XLA Modules:
  0.0 29.7 jit_solution(8671775375195734721)
XLA Ops:
  0.0 1.8 %pack.1 = (f32[248,128]{1,0:T(8,128)S(1)}, f32[248,128]{1,0:T(8,128)S(1)}, f32[1024,128]{1,0:T(8,128)S(1)}, bf16[1024,128]{1,0:T(8,128)(2,1)S(1)}, f32[64,128]{1...) custom-call(f32[1024,128]{1,0:T(8,128)} %bitcast.7, ...), custom_call_target="tpu_custom_call" | custom-call | tf_op jit(solution)/shard_map/pack/pallas_call | solution.py:436
  1.8 6.1 %collective-permute-start = (f32[248,128]{1,0:T(8,128)S(1)}, f32[248,128]{1,0:T(8,128)S(1)}, u32[]{:S(2)}, u32[]{:S(2)}) collective-permute-start(f32[248,128]{1,0:T(8,128)S(1)} %get-tuple-element.27.sent_far), channel_id=1, source_target_pairs={{0,28},{4,8},{8,4},{12,16},{16,12},{20,24},{24,20},{28,0},{1,29},{... | collective-permute-start | bytes 380936 | tf_op jit(solution)/shard_map/ppermute | solution.py:448
  7.8 0.0 collective-permute-start.1
  8.5 4.1 %main.1 = (f32[16,128]{1,0:T(8,128)S(1)}, bf16[512,2048]{1,0:T(8,128)(2,1)S(1)}) custom-call(f32[1024,128]{1,0:T(8,128)S(1)} %get-tuple-element.24.alpha, bf16[1024,128]{1,0:T(8,128)(2,1)S(1)} %get-tuple-element.25.members, f32[8,128]{1,0:T(8,128)S(1)} %broadcast_in_dim.2.weight, f32[64,128]{1,0:T(8,128)S(1)} %get-tuple-element.29.kappa, ...), custom_call_target="tpu_custom_call" | custom-call | tf_op jit(solution)/shard_map/main/pallas_call | solution.py:450
  12.7 0.0 collective-permute-done.got_far
  12.7 1.3 %collective-permute-done.1.got_near = f32[248,128]{1,0:T(8,128)S(1)} collective-permute-done((f32[248,128]{1,0:T(8,128)S(1)}, f32[248,128]{1,0:T(8,128)S(1)}, u32[]{:S(2)}, u32[]{:S(2)}) %collective-permute-start.1) | collective-permute-done | bytes 127008 | tf_op jit(solution)/shard_map/ppermute | solution.py:449
  14.0 3.6 %strip.1 = (f32[48,128]{1,0:T(8,128)S(1)}, f32[512,128]{1,0:T(8,128)S(1)}, f32[3,64,128]{2,1,0:T(8,128)S(1)}, bf16[128,4096]{1,0:T(8,128)(2,1)S(1)}) custom-call(f32[16,128]{1,0:T(8,128)S(1)} %get-tuple-element.33.inner, bf16[1024,128]{1,0:T(8,128)(2,1)S(1)} %get-tuple-element.25.members, f32[248,128]{1,0:T(8,128)S(1)} %get-tuple-element.27.sent_far, ...), custom_call_target="tpu_custom_call" | custom-call | tf_op jit(solution)/shard_map/strip/pallas_call | solution.py:458
  17.6 1.1 %collective-permute-start.4 = (f32[48,128]{1,0:T(8,128)S(1)}, f32[48,128]{1,0:T(8,128)S(1)}, u32[]{:S(2)}, u32[]{:S(2)}) collective-permute-start(f32[48,128]{1,0:T(8,128)S(1)} %get-tuple-element.42.v0), channel_id=1, source_target_pairs={{0,3},{1,2},{2,1},{3,0},{4,7},{5,6},{6,5},{7,4},{8,11},{9,10},{10,... | collective-permute-start | bytes 73736 | tf_op jit(solution)/shard_map/ppermute | solution.py:471
  18.7 0.5 %collective-permute-start.3 = (f32[48,128]{1,0:T(8,128)S(1)}, f32[48,128]{1,0:T(8,128)S(1)}, u32[]{:S(2)}, u32[]{:S(2)}) collective-permute-start(f32[48,128]{1,0:T(8,128)S(1)} %get-tuple-element.42.v0), channel_id=1, source_target_pairs={{0,2},{1,3},{2,0},{3,1},{4,6},{5,7},{6,4},{7,5},{8,10},{9,11},{10,... | collective-permute-start | bytes 73736 | tf_op jit(solution)/shard_map/ppermute | solution.py:471
  19.2 0.3 collective-permute-start.2
  19.5 1.0 %ready.1 = (f32[5,64,128]{2,1,0:T(8,128)S(1)}, f32[5,64,128]{2,1,0:T(8,128)S(1)}, bf16[256,2048]{1,0:T(8,128)(2,1)S(1)}, bf16[128,4096]{1,0:T(8,128)(2,1)S(1)}) custom-call(f32[64,128]{1,0:T(8,128)S(1)} %get-tuple-element.29.kappa, f32[64,128]{1,0:T(8,128)S(1)} %get-tuple-element.30.scale, s32[64,128]{1,0:T(8,128)S(1)} %get-tuple-element.31.ocean, ...), custom_call_target="tpu_custom_call" | custom-call | tf_op jit(solution)/shard_map/ready/pallas_call | solution.py:472
  20.5 0.5 %collective-permute-done.4.v3 = f32[48,128]{1,0:T(8,128)S(1)} collective-permute-done((f32[48,128]{1,0:T(8,128)S(1)}, f32[48,128]{1,0:T(8,128)S(1)}, u32[]{:S(2)}, u32[]{:S(2)}) %collective-permute-start.4) | collective-permute-done | bytes 24608 | tf_op jit(solution)/shard_map/ppermute | solution.py:471
  21.0 1.5 %collective-permute-done.3.v2 = f32[48,128]{1,0:T(8,128)S(1)} collective-permute-done((f32[48,128]{1,0:T(8,128)S(1)}, f32[48,128]{1,0:T(8,128)S(1)}, u32[]{:S(2)}, u32[]{:S(2)}) %collective-permute-start.3) | collective-permute-done | bytes 24608 | tf_op jit(solution)/shard_map/ppermute | solution.py:471
  22.6 0.0 collective-permute-done.2.v1
  22.6 7.1 %adjoint.1 = f32[1024,128]{1,0:T(8,128)} custom-call(f32[1024,128]{1,0:T(8,128)S(1)} %get-tuple-element.24.alpha, bf16[1024,128]{1,0:T(8,128)(2,1)S(1)} %get-tuple-element.25.members, f32[8,128]{1,0:T(8,128)S(1)} %broadcast_in_dim.2.weight, f32[16,128]{1,0:T(8,128)S(1)} %get-tuple-element.26.obs_weight, f32[248,128]{1,0:T(8,128)S(1)} %collective-permute-done.got_far, ...), custom_call_target="tpu_custom_call" | custom-call | tf_op jit(solution)/shard_map/adjoint/pallas_call | solution.py:484
  (1 shorter events, 0.0 us)
Async XLA Ops:
  1.8 10.9 %collective-permute-start = (f32[248,128]{1,0:T(8,128)S(1)}, f32[248,128]{1,0:T(8,128)S(1)}, u32[]{:S(2)}, u32[]{:S(2)}) collective-permute-start(f32[248,128]{1,0:T(8,128)S(1)} %get-tuple-element.27.sent_far), channel_id=1, source_target_pairs={{0,28},{4,8},{8,4},{12,16},{16,12},{20,24},{24,20},{28,0},{1,29},{... | collective-permute-start | bytes 380936 | tf_op jit(solution)/shard_map/ppermute | solution.py:448
  7.8 6.1 %collective-permute-start.1 = (f32[248,128]{1,0:T(8,128)S(1)}, f32[248,128]{1,0:T(8,128)S(1)}, u32[]{:S(2)}, u32[]{:S(2)}) collective-permute-start(f32[248,128]{1,0:T(8,128)S(1)} %get-tuple-element.28.sent_near), channel_id=1, source_target_pairs={{0,4},{4,0},{8,12},{12,8},{16,20},{20,16},{24,28},{28,24},{1,5},{5... | collective-permute-start | bytes 380936 | tf_op jit(solution)/shard_map/ppermute | solution.py:449
  17.6 3.4 %collective-permute-start.4 = (f32[48,128]{1,0:T(8,128)S(1)}, f32[48,128]{1,0:T(8,128)S(1)}, u32[]{:S(2)}, u32[]{:S(2)}) collective-permute-start(f32[48,128]{1,0:T(8,128)S(1)} %get-tuple-element.42.v0), channel_id=1, source_target_pairs={{0,3},{1,2},{2,1},{3,0},{4,7},{5,6},{6,5},{7,4},{8,11},{9,10},{10,... | collective-permute-start | bytes 73736 | tf_op jit(solution)/shard_map/ppermute | solution.py:471
  18.7 3.8 %collective-permute-start.3 = (f32[48,128]{1,0:T(8,128)S(1)}, f32[48,128]{1,0:T(8,128)S(1)}, u32[]{:S(2)}, u32[]{:S(2)}) collective-permute-start(f32[48,128]{1,0:T(8,128)S(1)} %get-tuple-element.42.v0), channel_id=1, source_target_pairs={{0,2},{1,3},{2,0},{3,1},{4,6},{5,7},{6,4},{7,5},{8,10},{9,11},{10,... | collective-permute-start | bytes 73736 | tf_op jit(solution)/shard_map/ppermute | solution.py:471
  19.2 3.3 %collective-permute-start.2 = (f32[48,128]{1,0:T(8,128)S(1)}, f32[48,128]{1,0:T(8,128)S(1)}, u32[]{:S(2)}, u32[]{:S(2)}) collective-permute-start(f32[48,128]{1,0:T(8,128)S(1)} %get-tuple-element.42.v0), channel_id=1, source_target_pairs={{0,1},{1,0},{2,3},{3,2},{4,5},{5,4},{6,7},{7,6},{8,9},{9,8},{10,11... | collective-permute-start | bytes 73736 | tf_op jit(solution)/shard_map/ppermute | solution.py:471

commit v7 on v6

--- a/solution.py
+++ b/solution.py
@@ -59,7 +59,7 @@
 
 def pack_kernel(
     z, alpha_hbm, members_hbm, kappa_hbm, scale_hbm, ocean_hbm, cell_hbm, weight_hbm,
-    out_far, out_near, alpha, members, kappa, scale, ocean, cell, weight, sems,
+    out_right, out_left, alpha, members, kappa, scale, ocean, cell, weight, sems,
 ):
     pairs = (
         (members_hbm, members), (alpha_hbm, alpha), (kappa_hbm, kappa), (scale_hbm, scale), (ocean_hbm, ocean),
@@ -68,11 +68,10 @@
     copies = [pltpu.make_async_copy(a, b, sems.at[k]) for k, (a, b) in enumerate(pairs)]
     for copy in copies:
         copy.start()
-    even = lax.rem(lax.axis_index("tile"), 2) == 0
 
     def put(where, right, left):
-        out_near[where, :] = jnp.where(even, right, left)
-        out_far[where, :] = jnp.where(even, left, right)
+        out_right[where, :] = right
+        out_left[where, :] = left
 
     for copy in copies[2:]:
         copy.wait()
@@ -86,8 +85,7 @@
         put(pl.ds(z.at_coeff + k * SUB, SUB), overlay(right, lane >> 4), overlay(left, lane >> 4))
     n = z.obs_rows
     for at, value in ((z.at_obs, cell[...].astype(F32)), (z.at_obs + n, weight[...])):
-        out_near[pl.ds(at, n), :] = value
-        out_far[pl.ds(at, n), :] = value
+        put(pl.ds(at, n), value, value)
     copies[0].wait()
     block = 2 * SUB
     lane = lanes(block)
@@ -239,13 +237,13 @@
     sweep([(x, y, coeff, z.levels)], z.rows)
 
 
-def main_kernel(z, alpha, members, weight, kappa, scale, ocean, cell, out, hot, x, coeff, y, both):
+def main_kernel(z, alpha, members, kappa, scale, ocean, cell, out, hot, x, coeff, y, both):
     forward_sweep(z, alpha, kappa, scale, ocean, coeff, x, y)
     lane = lanes(z.group)
     inner = (lane >= STEPS) & (lane < z.columns - STEPS)
     for g in range(2):
         rows = pl.ds(g * z.group, z.group)
-        value = x[pl.ds(SUB + g * z.group, z.group), :] * (members[rows, :].astype(F32) * weight[0:1, :])
+        value = x[pl.ds(SUB + g * z.group, z.group), :] * members[rows, :].astype(F32)
         high, low = split(jnp.where(inner, value, 0.0))
         both[:, pl.ds(g * 128, 128)] = high
         both[:, pl.ds(256 + g * 128, 128)] = low
@@ -253,19 +251,12 @@
 
 
 def strip_kernel(
-    z, inner, members, sent_far, sent_near, got_far, got_near, cell, weight,
+    z, inner, members, own_right, own_left, from_left, from_right, cell, weight,
     out, strip_members, strip_coeff, hot, coeff, x, y, outer, beside,
 ):
-    even = lax.rem(lax.axis_index("tile"), 2) == 0
 
     def parts(rows):
-        pick = lambda p, q: jnp.where(even, p[rows, :], q[rows, :])
-        return (
-            pick(sent_near, sent_far),
-            pick(got_near, got_far),
-            pick(got_far, got_near),
-            pick(sent_far, sent_near),
-        )
+        return own_right[rows, :], from_right[rows, :], from_left[rows, :], own_left[rows, :]
 
     clear_ends(x, y)
     lane = lanes(SUB)
@@ -298,7 +289,7 @@
                 inside = (wide_lane >> 4) & 3
                 value = jnp.where(mine & (inside == 0), roll(own, EDGE + 64 * g), value)
                 value = jnp.where(mine & (inside == 3), roll(own, 48 + 64 * g), value)
-            strip_members[pl.ds(at, block), :] = value * weight[0:1, :]
+            strip_members[pl.ds(at, block), :] = value
     put_coefficients(coeff, coefficients(strip_coeff[0], strip_coeff[1], strip_coeff[2], True))
     sweep([(x, y, coeff, z.levels // 2)], z.rows)
     unit = lanes(z.short) >> 3
@@ -308,73 +299,91 @@
         for k in range(4):
             rows = pl.ds(k * z.short, z.short)
             pieces.append(roll(x[pl.ds(SUB + k * z.short, z.short), :] * strip_members[rows, :], 16 * k))
-        high, low = split(overlay(pieces, quarter))
-        ref[:, :128] = high
-        ref[:, 128:] = low
-    _, right, left, _ = parts(pl.ds(z.at_obs, z.obs_rows))
+        value = overlay(pieces, quarter)
+        if ref is outer:
+            rights = ((0, value),)
+        else:
+            rights = ((0, jnp.where((unit & 1) == 0, value, 0.0)), (z.short, jnp.where((unit & 1) == 1, value, 0.0)))
+        for at, value in rights:
+            high, low = split(value)
+            ref[pl.ds(at, z.short), :128] = high
+            ref[pl.ds(at, z.short), 128:] = low
     n = z.obs_rows
-    for k, (field, cells) in enumerate(
-        ((outer, cell[...]), (beside, right.astype(jnp.int32)), (beside, left.astype(jnp.int32)))
-    ):
-        keep = hot if k else None
-        gather(z, out, k * n, field[...], cells, lambda c: edge_index(z, c, windows_of(z)[k]), keep, (k - 1) * z.obs)
-    out[:n, :] = out[:n, :] + inner[...]
-
-
-def beside_rows(z, got_far, got_near, at):
-    even = lax.rem(lax.axis_index("tile"), 2) == 0
-    far, near = got_far[pl.ds(at, z.obs_rows), :], got_near[pl.ds(at, z.obs_rows), :]
-    return jnp.where(even, near, far), jnp.where(even, far, near)
-
-
-def ready_kernel(z, kappa, scale, ocean, cell, got_far, got_near, strip_coeff, coeff, strip_c, own_lane, beside_lane):
+    own_window, right_window, left_window = windows_of(z)
+    gather(z, out, 0, outer[...], cell[...], lambda c: edge_index(z, c, own_window))
+    out[:n, :] = (out[:n, :] + inner[...]) * weight[0:1, :]
+    right = from_right[pl.ds(z.at_obs, n), :].astype(jnp.int32)
+    left = from_left[pl.ds(z.at_obs, n), :].astype(jnp.int32)
+    field = beside[...]
+    for r in range(0, n, 2):
+        pair = lambda v: jnp.concatenate([v[r : r + 1, :], v[r + 1 : r + 2, :]], axis=1)
+        i_right, j_right = edge_index(z, pair(right), right_window)
+        i_left, j_left = edge_index(z, pair(left), left_window)
+        both = jnp.concatenate([one_hot(i_right, z.short), one_hot(i_left, z.short)], axis=0)
+        hot[:, pl.ds(r * 128, 256)] = both
+        value = lax.dot_general(field, both, (((0,), (0,)), ((), ())), preferred_element_type=F32)
+        value = value[:128] + value[128:]
+        rows = lax.broadcasted_iota(jnp.int32, (SUB, 256), 0)
+        for side, j in enumerate((j_right, j_left)):
+            total = None
+            for t in range(side, 16, 2):
+                piece = jnp.where(rows == j - t * SUB, value[t * SUB : (t + 1) * SUB], 0.0)
+                total = piece if total is None else total + piece
+            total = jnp.sum(total, axis=0, keepdims=True) * weight[0:1, 0:1]
+            at = (1 + side) * n + r
+            out[at : at + 1, :] = total[:, :128]
+            out[at + 1 : at + 2, :] = total[:, 128:]
+
+
+def ready_kernel(z, kappa, scale, ocean, cell, from_left, from_right, strip_coeff, coeff, strip_c, own_lane, beside_lane):
     put_coefficients(coeff, coefficients(kappa[...], scale[...], ocean[...].astype(F32), False))
     put_coefficients(strip_c, coefficients(strip_coeff[0], strip_coeff[1], strip_coeff[2], False))
     _, right_window, left_window = windows_of(z)
-    right, left = beside_rows(z, got_far, got_near, z.at_obs)
     n = z.obs_rows
+    right = from_right[pl.ds(z.at_obs, n), :].astype(jnp.int32)
+    left = from_left[pl.ds(z.at_obs, n), :].astype(jnp.int32)
+    rows = lax.broadcasted_iota(jnp.int32, (128, 128), 0)
     for r in range(n):
         at = pl.ds(r * 128, 128)
         own_lane[:, at] = one_hot(own_index(z, cell[r : r + 1, :])[1], 256)
-        index = right[r : r + 1, :].astype(jnp.int32)
-        beside_lane[:, at] = one_hot(edge_index(z, index, right_window)[1], 128)
-        index = left[r : r + 1, :].astype(jnp.int32)
-        beside_lane[:, pl.ds(z.obs + r * 128, 128)] = one_hot(edge_index(z, index, left_window)[1], 128)
+        j_right = edge_index(z, right[r : r + 1, :], right_window)[1]
+        j_left = edge_index(z, left[r : r + 1, :], left_window)[1]
+        lane = jnp.where((rows & SUB) == 0, j_right, j_left)
+        beside_lane[:, at] = jnp.where(rows == lane, 1.0, 0.0).astype(BF16)
 
 
 def adjoint_kernel(
-    z, alpha, members, weight, obs_weight, got_far, got_near, strip_members, coeff, strip_c,
+    z, alpha, members, weight, obs_weight, from_left, from_right, strip_members, coeff, strip_c,
     own_row, own_lane, beside_row, beside_lane, v0, v1, v2, v3,
     out_hbm, x, y, strip, spare, beside, spread, out, sems,
 ):
     clear_ends(x, y, strip, spare)
     value = (v0[...] + v1[...]) + (v2[...] + v3[...])
     n = z.obs_rows
-    right_weight, left_weight = beside_rows(z, got_far, got_near, z.at_obs + n)
-
-    def spread_out(amounts, row_hot, lane_hot):
+    weights = pl.ds(z.at_obs + n, n)
+
+    def spread_out(tops, bottoms, row_hot, lane_hot):
         wide = lane_hot.shape[0]
-        for group, amount in enumerate(amounts):
-            high, low = split(amount)
+        for k, (top, bottom) in enumerate(zip(split(tops), split(bottoms))):
             for r in range(n):
-                at = pl.ds(group * z.obs + r * 128, 128)
-                for k, part in enumerate((high, low)):
-                    line = jnp.broadcast_to(part[r : r + 1, :].astype(F32), (2 * SUB, 128)).astype(BF16)
-                    for t in range(wide // (2 * SUB)):
-                        rows = pl.ds(t * 2 * SUB, 2 * SUB)
-                        spread[pl.ds(k * wide + t * 2 * SUB, 2 * SUB), at] = lane_hot[rows, at] * line
+                at = pl.ds(r * 128, 128)
+                line = jnp.concatenate(
+                    [jnp.broadcast_to(v[r : r + 1, :].astype(F32), (SUB, 128)) for v in (top, bottom)], axis=0
+                ).astype(BF16)
+                for t in range(wide // (2 * SUB)):
+                    rows = pl.ds(t * 2 * SUB, 2 * SUB)
+                    spread[pl.ds(k * wide + t * 2 * SUB, 2 * SUB), at] = lane_hot[rows, at] * line
         dims = (((1,), (1,)), ((), ()))
-        total = lax.dot_general(
-            row_hot[...], spread[: 2 * wide, : len(amounts) * z.obs], dims, preferred_element_type=F32
-        )
+        total = lax.dot_general(row_hot[...], spread[: 2 * wide, :], dims, preferred_element_type=F32)
         return total[:, :wide] + total[:, wide:]
 
-    field = spread_out([obs_weight[...] * value[:n]], own_row, own_lane)
+    amount = obs_weight[...] * value[:n]
+    field = spread_out(amount, amount, own_row, own_lane)
     for g in range(2):
         x[pl.ds(SUB + g * z.group, z.group), :] = field[:, g * 128 : (g + 1) * 128]
-    beside[...] = spread_out(
-        [right_weight * value[n : 2 * n], left_weight * value[2 * n :]], beside_row, beside_lane
-    )
+    right, left = from_right[weights, :] * value[n : 2 * n], from_left[weights, :] * value[2 * n :]
+    field = spread_out(right, left, beside_row, beside_lane)
+    beside[...] = jnp.where((lanes(z.short) & SUB) == 0, field[: z.short], field[z.short :])
     lane = lanes(SUB)
     part = (lane >> 4) & 3
     within = lane & 15
@@ -389,7 +398,7 @@
             mine = (lane >> 6) == g
             value = jnp.where(mine & (part == 0), roll(field, EDGE + 64 * g), value)
             value = jnp.where(mine & (part == 3), roll(field, 48 + 64 * g), value)
-        strip[pl.ds(SUB + q * SUB, SUB), :] = value * strip_members[pl.ds(q * SUB, SUB), :]
+        strip[pl.ds(SUB + q * SUB, SUB), :] = value * (strip_members[pl.ds(q * SUB, SUB), :] * weight[...])
     here = pl.ds(SUB, z.field)
     x[here, :] = x[here, :] * (members[...].astype(F32) * weight[0:1, :])
     sweep([(x, y, coeff, z.levels), (strip, spare, strip_c, z.levels // 2)], z.rows)
@@ -417,7 +426,7 @@
     shape = alpha.shape
     z = Sizes(shape[1], shape[2], shape[3], obs_cell.shape[0])
     tiles, holders = lax.axis_size("tile"), lax.axis_size("mem")
-    assert tiles % 2 == 0 and holders == 4 and shape[0] == 1
+    assert holders == 4 and shape[0] == 1
     alpha = alpha.reshape(z.field, z.columns)
     members = members.reshape(z.field, z.columns)
     cell = obs_cell.reshape(z.obs_rows, 128)
@@ -433,7 +442,7 @@
     limit = pltpu.CompilerParams(vmem_limit_bytes=24 << 20)
     call = functools.partial(pl.pallas_call, compiler_params=limit)
     given = (alpha, members, kappa, norm_scale, land_sea, cell, weight)
-    sent_far, sent_near, *given = call(
+    sent_right, sent_left, *given = call(
         functools.partial(pack_kernel, z),
         out_shape=(payload, payload, *(sds(v.shape, v.dtype) for v in given)),
         in_specs=[stays] * 7,
@@ -442,32 +451,32 @@
         name="pack",
     )(*(pltpu.with_memory_space_constraint(v, pltpu.HBM) for v in given))
     alpha, members, kappa, norm_scale, land_sea, cell, weight = given
-    factor = jnp.broadcast_to(mem_weight, (SUB, 128))
-    near = [(i, i ^ 1) for i in range(tiles)]
-    far = [(i, (i + 1) % tiles if i % 2 else (i - 1) % tiles) for i in range(tiles)]
-    got_far = lax.ppermute(sent_far, "tile", far)
-    got_near = lax.ppermute(sent_near, "tile", near)
+    up_ring = [(i, (i + 1) % tiles) for i in range(tiles)]
+    from_left = lax.ppermute(sent_right, "tile", up_ring)
+    from_right = lax.ppermute(sent_left, "tile", [(b, a) for a, b in up_ring])
     inner, own_row = call(
         functools.partial(main_kernel, z),
         out_shape=(sds((z.obs_rows, 128), F32), sds((z.group, z.obs), BF16)),
-        in_specs=[whole] * 7,
+        in_specs=[whole] * 6,
         out_specs=(whole, whole),
         scratch_shapes=[main_field, coeff, main_field, pltpu.VMEM((z.group, 512), BF16)],
         name="main",
-    )(alpha, members, factor, kappa, norm_scale, land_sea, cell)
+    )(alpha, members, kappa, norm_scale, land_sea, cell)
+    mem_weight, inner = lax.optimization_barrier((mem_weight, inner))
+    factor = jnp.broadcast_to(mem_weight, (SUB, 128))
     values, strip_members, strip_coeff, beside_row = call(
         functools.partial(strip_kernel, z),
         out_shape=(
             sds((3 * z.obs_rows, 128), F32),
             sds((z.group, 128), F32),
             sds((3, z.rows, 128), F32),
-            sds((z.short, 2 * z.obs), BF16),
+            sds((2 * z.short, z.obs), BF16),
         ),
         in_specs=[whole] * 8,
         out_specs=(whole,) * 4,
-        scratch_shapes=[coeff, strip_field, strip_field, packed, packed],
+        scratch_shapes=[coeff, strip_field, strip_field, packed, pltpu.VMEM((2 * z.short, 256), BF16)],
         name="strip",
-    )(inner, members, sent_far, sent_near, got_far, got_near, cell, factor)
+    )(inner, members, sent_right, sent_left, from_left, from_right, cell, factor)
     others = [lax.ppermute(values, "mem", [(i, i ^ k) for i in range(holders)]) for k in range(1, holders)]
     main_c, strip_c, own_lane, beside_lane = call(
         functools.partial(ready_kernel, z),
@@ -475,12 +484,12 @@
             sds((5, z.rows, 128), F32),
             sds((5, z.rows, 128), F32),
             sds((2 * 128, z.obs), BF16),
-            sds((128, 2 * z.obs), BF16),
+            sds((128, z.obs), BF16),
         ),
         in_specs=[whole] * 7,
         out_specs=(whole,) * 4,
         name="ready",
-    )(kappa, norm_scale, land_sea, cell, got_far, got_near, strip_coeff)
+    )(kappa, norm_scale, land_sea, cell, from_left, from_right, strip_coeff)
     product = call(
         functools.partial(adjoint_kernel, z),
         out_shape=sds((z.field, z.columns), F32),
@@ -492,13 +501,13 @@
             strip_field,
             strip_field,
             pltpu.VMEM((z.short, 128), F32),
-            pltpu.VMEM((512, 2 * z.obs), BF16),
+            pltpu.VMEM((512, z.obs), BF16),
             pltpu.VMEM((z.field, 128), F32),
             pltpu.SemaphoreType.DMA((z.levels // 2,)),
         ],
         name="adjoint",
     )(
-        alpha, members, factor, weight, got_far, got_near, strip_members, main_c, strip_c,
+        alpha, members, factor, weight, from_left, from_right, strip_members, main_c, strip_c,
         own_row, own_lane, beside_row, beside_lane, values, *others,
     )
     return product.reshape(shape)

time: 29.9 us -> 27.8 us (0.930)
  waiting for transfers between devices: 3.32 us -> 1.95 us
  Pallas kernels: 17.7 us -> 16.9 us
    ppermute x2, waiting for transfers between devices: 1.3 us -> 0.01 us  [the longest x1 0.01 us: local(): from_right = lax.ppermute(sent_left, 'tile', [(b, a) for a, b in up_ring])]
    pallas_call x1, Pallas kernels: 7.14 us -> 6.73 us  [local(): call(functools.partial(adjoint_kernel, z), out_shape=sds((z.field, z.colu...]
  transfers between devices with their start and end apart: 5 -> 5, of which waited for: 3 -> 2; matrix products, arithmetic and copies ran while one was open for 0% -> 0% of each run, Pallas kernels for 17% -> 18%
where the time goes in v7:
time: 27.8 us; the launch traced here: 27.6 us
  Pallas kernels  16.9 us (61%)
  starting transfers between devices  8.05 us (29%)
  waiting for transfers between devices  1.95 us (7%)
  between operations  0.71 us (3%)
    pallas_call x1, Pallas kernels, local(): call(functools.partial(adjoint_kernel, z), out_shape=sds((z.field, z.colu...  6.73 us
    pallas_call x1, Pallas kernels, local(): call(functools.partial(main_kernel, z), out_shape=(sds((z.obs_rows, 128),...  4.18 us
    pallas_call x1, Pallas kernels, local(): call(functools.partial(strip_kernel, z), out_shape=(sds((3 * z.obs_rows,...  3.34 us
    ppermute x1, starting transfers between devices, local(): from_right = lax.ppermute(sent_left, 'tile', [(b, a) for a, b in up_ring])  3.1 us
    ppermute x1, starting transfers between devices, local(): from_left = lax.ppermute(sent_right, 'tile', up_ring)  3.02 us
    ppermute x3, waiting for transfers between devices, local(): lax.ppermute(values, 'mem', [(i, i ^ k) for i in range(holders)])  1.94 us
    ppermute x3, starting transfers between devices, local(): lax.ppermute(values, 'mem', [(i, i ^ k) for i in range(holders)])  1.93 us
    pallas_call x1, Pallas kernels, local(): call(functools.partial(pack_kernel, z), out_shape=(payload, payload, *(sd...  1.76 us
  transfers between devices with their start and end apart: 5, of which 2 were waited for; matrix products, arithmetic and copies ran while one was open for 0% of the time, Pallas kernels for 18%

profile of v7, /device:TPU:0, one launch (start us, length us, event | category | flops | bytes accessed | tf_op | source)
XLA Modules:
  0.0 27.6 jit_solution(3090736342520133161)
XLA Ops:
  0.0 1.8 %pack.1 = (f32[248,128]{1,0:T(8,128)S(1)}, f32[248,128]{1,0:T(8,128)S(1)}, f32[1024,128]{1,0:T(8,128)S(1)}, bf16[1024,128]{1,0:T(8,128)(2,1)S(1)}, f32[64,128]{1...) custom-call(f32[1024,128]{1,0:T(8,128)} %bitcast.7, ...), custom_call_target="tpu_custom_call" | custom-call | tf_op jit(solution)/shard_map/pack/pallas_call | solution.py:445
  1.8 3.0 %collective-permute-start = (f32[248,128]{1,0:T(8,128)S(1)}, f32[248,128]{1,0:T(8,128)S(1)}, u32[]{:S(2)}, u32[]{:S(2)}) collective-permute-start(f32[248,128]{1,0:T(8,128)S(1)} %get-tuple-element.35.own_right), channel_id=1, source_target_pairs={{0,4},{4,8},{8,12},{12,16},{16,20},{20,24},{24,28},{28,0},{1,5},{5... | collective-permute-start | bytes 380936 | tf_op jit(solution)/shard_map/ppermute | solution.py:455
  4.8 3.1 %collective-permute-start.1 = (f32[248,128]{1,0:T(8,128)S(1)}, f32[248,128]{1,0:T(8,128)S(1)}, u32[]{:S(2)}, u32[]{:S(2)}) collective-permute-start(f32[248,128]{1,0:T(8,128)S(1)} %get-tuple-element.36.own_left), channel_id=1, source_target_pairs={{4,0},{8,4},{12,8},{16,12},{20,16},{24,20},{28,24},{0,28},{5,1},{9... | collective-permute-start | bytes 380936 | tf_op jit(solution)/shard_map/ppermute | solution.py:456
  8.5 4.2 %main.1 = (f32[16,128]{1,0:T(8,128)S(1)}, bf16[512,2048]{1,0:T(8,128)(2,1)S(1)}) custom-call(f32[1024,128]{1,0:T(8,128)S(1)} %get-tuple-element.26.alpha, bf16[1024,128]{1,0:T(8,128)(2,1)S(1)} %get-tuple-element.27.members, f32[64,128]{1,0:T(8,128)S(1)} %get-tuple-element.28.kappa, f32[64,128]{1,0:T(8,128)S(1)} %get-tuple-element.29.scale, ...), custom_call_target="tpu_custom_call" | custom-call | tf_op jit(solution)/shard_map/main/pallas_call | solution.py:457
  12.7 0.0 collective-permute-done.from_left
  12.7 0.0 collective-permute-done.1.from_right
  12.8 3.3 %strip.1 = (f32[48,128]{1,0:T(8,128)S(1)}, f32[512,128]{1,0:T(8,128)S(1)}, f32[3,64,128]{2,1,0:T(8,128)S(1)}, bf16[256,2048]{1,0:T(8,128)(2,1)S(1)}) custom-call(f32[16,128]{1,0:T(8,128)S(1)} %get-tuple-element.37.inner, bf16[1024,128]{1,0:T(8,128)(2,1)S(1)} %get-tuple-element.27.members, f32[248,128]{1,0:T(8,128)S(1)} %get-tuple-element.35.own_right, ...), custom_call_target="tpu_custom_call" | custom-call | tf_op jit(solution)/shard_map/strip/pallas_call | solution.py:467
  16.1 0.7 %collective-permute-start.4 = (f32[48,128]{1,0:T(8,128)S(1)}, f32[48,128]{1,0:T(8,128)S(1)}, u32[]{:S(2)}, u32[]{:S(2)}) collective-permute-start(f32[48,128]{1,0:T(8,128)S(1)} %get-tuple-element.46.v0), channel_id=1, source_target_pairs={{0,3},{1,2},{2,1},{3,0},{4,7},{5,6},{6,5},{7,4},{8,11},{9,10},{10,... | collective-permute-start | bytes 73736 | tf_op jit(solution)/shard_map/ppermute | solution.py:480
  16.9 1.1 %collective-permute-start.3 = (f32[48,128]{1,0:T(8,128)S(1)}, f32[48,128]{1,0:T(8,128)S(1)}, u32[]{:S(2)}, u32[]{:S(2)}) collective-permute-start(f32[48,128]{1,0:T(8,128)S(1)} %get-tuple-element.46.v0), channel_id=1, source_target_pairs={{0,2},{1,3},{2,0},{3,1},{4,6},{5,7},{6,4},{7,5},{8,10},{9,11},{10,... | collective-permute-start | bytes 73736 | tf_op jit(solution)/shard_map/ppermute | solution.py:480
  17.9 0.1 collective-permute-start.2
  18.0 0.8 %ready.1 = (f32[5,64,128]{2,1,0:T(8,128)S(1)}, f32[5,64,128]{2,1,0:T(8,128)S(1)}, bf16[256,2048]{1,0:T(8,128)(2,1)S(1)}, bf16[128,2048]{1,0:T(8,128)(2,1)S(1)}) custom-call(f32[64,128]{1,0:T(8,128)S(1)} %get-tuple-element.28.kappa, f32[64,128]{1,0:T(8,128)S(1)} %get-tuple-element.29.scale, s32[64,128]{1,0:T(8,128)S(1)} %get-tuple-element.30.ocean, ...), custom_call_target="tpu_custom_call" | custom-call | tf_op jit(solution)/shard_map/ready/pallas_call | solution.py:481
  18.9 0.6 %collective-permute-done.4.v3 = f32[48,128]{1,0:T(8,128)S(1)} collective-permute-done((f32[48,128]{1,0:T(8,128)S(1)}, f32[48,128]{1,0:T(8,128)S(1)}, u32[]{:S(2)}, u32[]{:S(2)}) %collective-permute-start.4) | collective-permute-done | bytes 24608 | tf_op jit(solution)/shard_map/ppermute | solution.py:480
  19.5 1.4 %collective-permute-done.3.v2 = f32[48,128]{1,0:T(8,128)S(1)} collective-permute-done((f32[48,128]{1,0:T(8,128)S(1)}, f32[48,128]{1,0:T(8,128)S(1)}, u32[]{:S(2)}, u32[]{:S(2)}) %collective-permute-start.3) | collective-permute-done | bytes 24608 | tf_op jit(solution)/shard_map/ppermute | solution.py:480
  20.8 0.0 collective-permute-done.2.v1
  20.8 6.7 %adjoint.1 = f32[1024,128]{1,0:T(8,128)} custom-call(f32[1024,128]{1,0:T(8,128)S(1)} %get-tuple-element.26.alpha, bf16[1024,128]{1,0:T(8,128)(2,1)S(1)} %get-tuple-element.27.members, f32[8,128]{1,0:T(8,128)S(1)} %broadcast_in_dim.2.weight, f32[16,128]{1,0:T(8,128)S(1)} %get-tuple-element.34.obs_weight, f32[248,128]{1,0:T(8,128)S(1)} %collective-permute-done.from_left, ...), custom_call_target="tpu_custom_call" | custom-call | tf_op jit(solution)/shard_map/adjoint/pallas_call | solution.py:493
  (1 shorter events, 0.0 us)
Async XLA Ops:
  1.8 11.0 %collective-permute-start = (f32[248,128]{1,0:T(8,128)S(1)}, f32[248,128]{1,0:T(8,128)S(1)}, u32[]{:S(2)}, u32[]{:S(2)}) collective-permute-start(f32[248,128]{1,0:T(8,128)S(1)} %get-tuple-element.35.own_right), channel_id=1, source_target_pairs={{0,4},{4,8},{8,12},{12,16},{16,20},{20,24},{24,28},{28,0},{1,5},{5... | collective-permute-start | bytes 380936 | tf_op jit(solution)/shard_map/ppermute | solution.py:455
  4.8 8.0 %collective-permute-start.1 = (f32[248,128]{1,0:T(8,128)S(1)}, f32[248,128]{1,0:T(8,128)S(1)}, u32[]{:S(2)}, u32[]{:S(2)}) collective-permute-start(f32[248,128]{1,0:T(8,128)S(1)} %get-tuple-element.36.own_left), channel_id=1, source_target_pairs={{4,0},{8,4},{12,8},{16,12},{20,16},{24,20},{28,24},{0,28},{5,1},{9... | collective-permute-start | bytes 380936 | tf_op jit(solution)/shard_map/ppermute | solution.py:456
  16.1 3.4 %collective-permute-start.4 = (f32[48,128]{1,0:T(8,128)S(1)}, f32[48,128]{1,0:T(8,128)S(1)}, u32[]{:S(2)}, u32[]{:S(2)}) collective-permute-start(f32[48,128]{1,0:T(8,128)S(1)} %get-tuple-element.46.v0), channel_id=1, source_target_pairs={{0,3},{1,2},{2,1},{3,0},{4,7},{5,6},{6,5},{7,4},{8,11},{9,10},{10,... | collective-permute-start | bytes 73736 | tf_op jit(solution)/shard_map/ppermute | solution.py:480
  16.9 4.0 %collective-permute-start.3 = (f32[48,128]{1,0:T(8,128)S(1)}, f32[48,128]{1,0:T(8,128)S(1)}, u32[]{:S(2)}, u32[]{:S(2)}) collective-permute-start(f32[48,128]{1,0:T(8,128)S(1)} %get-tuple-element.46.v0), channel_id=1, source_target_pairs={{0,2},{1,3},{2,0},{3,1},{4,6},{5,7},{6,4},{7,5},{8,10},{9,11},{10,... | collective-permute-start | bytes 73736 | tf_op jit(solution)/shard_map/ppermute | solution.py:480
  17.9 2.9 %collective-permute-start.2 = (f32[48,128]{1,0:T(8,128)S(1)}, f32[48,128]{1,0:T(8,128)S(1)}, u32[]{:S(2)}, u32[]{:S(2)}) collective-permute-start(f32[48,128]{1,0:T(8,128)S(1)} %get-tuple-element.46.v0), channel_id=1, source_target_pairs={{0,1},{1,0},{2,3},{3,2},{4,5},{5,4},{6,7},{7,6},{8,9},{9,8},{10,11... | collective-permute-start | bytes 73736 | tf_op jit(solution)/shard_map/ppermute | solution.py:480

commit v8 on v7

--- a/solution.py
+++ b/solution.py
@@ -10,6 +10,7 @@
 STEPS = 8
 SUB = 8
 EDGE = 2 * STEPS
+ASSISTED = 5
 F32 = jnp.float32
 BF16 = jnp.bfloat16
 
@@ -141,14 +142,30 @@
         ref[k] = value
 
 
-def step_rows(source, target, coeff, rows, levels):
+def shift_matrix():
+    row = lax.broadcasted_iota(jnp.int32, (256, 256), 0)
+    column = lax.broadcasted_iota(jnp.int32, (256, 256), 1)
+    wanted = jnp.where(column < 128, column + 1, column - 1)
+    return jnp.where((row & 127) == (wanted & 127), 1.0, 0.0).astype(BF16)
+
+
+def step_rows(source, target, coeff, rows, levels, shift):
+    assisted = 0
+    if shift is not None:
+        assisted = ASSISTED
+        both = jnp.concatenate(split(source[pl.ds(SUB, assisted * rows), :]), axis=1)
+        beside = jnp.dot(both, shift[...], preferred_element_type=F32)
     for t in range(rows // SUB):
         c = [coeff[k, pl.ds(t * SUB, SUB), :] for k in range(5)]
         for level in range(levels):
-            at = SUB + level * rows + t * SUB
+            r = level * rows + t * SUB
+            at = SUB + r
             u = source[pl.ds(at, SUB), :]
             along = c[3] * source[pl.ds(at + 1, SUB), :] + c[4] * source[pl.ds(at - 1, SUB), :]
-            across = c[1] * roll(u, -1) + c[2] * roll(u, 1)
+            if level < assisted:
+                across = c[1] * beside[r : r + SUB, :128] + c[2] * beside[r : r + SUB, 128:]
+            else:
+                across = c[1] * roll(u, -1) + c[2] * roll(u, 1)
             target[pl.ds(at, SUB), :] = c[0] * u + across + along
 
 
@@ -160,14 +177,10 @@
 
 
 def sweep(fields, rows):
-    def two_steps(_, carry):
-        for x, y, coeff, levels in fields:
-            step_rows(x, y, coeff, rows, levels)
-        for x, y, coeff, levels in fields:
-            step_rows(y, x, coeff, rows, levels)
-        return carry
-
-    lax.fori_loop(0, STEPS // 2, two_steps, 0)
+    for step in range(STEPS):
+        for x, y, coeff, levels, shift in fields:
+            source, target = (y, x) if step % 2 else (x, y)
+            step_rows(source, target, coeff, rows, levels, shift)
 
 
 def cell_parts(z, cell):
@@ -230,15 +243,16 @@
         out[at + 2 * n + 1 : at + 2 * n + 2, :] = value[:, 128:]
 
 
-def forward_sweep(z, alpha, kappa, scale, ocean, coeff, x, y):
+def forward_sweep(z, alpha, kappa, scale, ocean, coeff, x, y, shift):
     put_coefficients(coeff, coefficients(kappa[...], scale[...], ocean[...].astype(F32), True))
     clear_ends(x, y)
     x[pl.ds(SUB, z.field), :] = alpha[...]
-    sweep([(x, y, coeff, z.levels)], z.rows)
-
-
-def main_kernel(z, alpha, members, kappa, scale, ocean, cell, out, hot, x, coeff, y, both):
-    forward_sweep(z, alpha, kappa, scale, ocean, coeff, x, y)
+    shift[...] = shift_matrix()
+    sweep([(x, y, coeff, z.levels, shift)], z.rows)
+
+
+def main_kernel(z, alpha, members, kappa, scale, ocean, cell, out, hot, x, coeff, y, both, shift):
+    forward_sweep(z, alpha, kappa, scale, ocean, coeff, x, y, shift)
     lane = lanes(z.group)
     inner = (lane >= STEPS) & (lane < z.columns - STEPS)
     for g in range(2):
@@ -291,7 +305,7 @@
                 value = jnp.where(mine & (inside == 3), roll(own, 48 + 64 * g), value)
             strip_members[pl.ds(at, block), :] = value
     put_coefficients(coeff, coefficients(strip_coeff[0], strip_coeff[1], strip_coeff[2], True))
-    sweep([(x, y, coeff, z.levels // 2)], z.rows)
+    sweep([(x, y, coeff, z.levels // 2, None)], z.rows)
     unit = lanes(z.short) >> 3
     for ref, first, second in ((outer, 1, 6), (beside, 2, 5)):
         quarter = quarters(unit, first, second)
@@ -355,9 +369,10 @@
 def adjoint_kernel(
     z, alpha, members, weight, obs_weight, from_left, from_right, strip_members, coeff, strip_c,
     own_row, own_lane, beside_row, beside_lane, v0, v1, v2, v3,
-    out_hbm, x, y, strip, spare, beside, spread, out, sems,
+    out_hbm, x, y, strip, spare, beside, spread, out, shift, sems,
 ):
     clear_ends(x, y, strip, spare)
+    shift[...] = shift_matrix()
     value = (v0[...] + v1[...]) + (v2[...] + v3[...])
     n = z.obs_rows
     weights = pl.ds(z.at_obs + n, n)
@@ -401,7 +416,7 @@
         strip[pl.ds(SUB + q * SUB, SUB), :] = value * (strip_members[pl.ds(q * SUB, SUB), :] * weight[...])
     here = pl.ds(SUB, z.field)
     x[here, :] = x[here, :] * (members[...].astype(F32) * weight[0:1, :])
-    sweep([(x, y, coeff, z.levels), (strip, spare, strip_c, z.levels // 2)], z.rows)
+    sweep([(x, y, coeff, z.levels, shift), (strip, spare, strip_c, z.levels // 2, None)], z.rows)
     sent = []
     for part in range(z.levels // 2):
         for t in range(z.rows // SUB):
@@ -437,6 +452,7 @@
     main_field = pltpu.VMEM((z.field + 2 * SUB, 128), F32)
     strip_field = pltpu.VMEM((z.group + 2 * SUB, 128), F32)
     coeff = pltpu.VMEM((5, z.rows, 128), F32)
+    square = pltpu.VMEM((256, 256), BF16)
     packed = pltpu.VMEM((z.short, 256), BF16)
     payload = sds((z.payload, 128), F32)
     limit = pltpu.CompilerParams(vmem_limit_bytes=24 << 20)
@@ -459,7 +475,7 @@
         out_shape=(sds((z.obs_rows, 128), F32), sds((z.group, z.obs), BF16)),
         in_specs=[whole] * 6,
         out_specs=(whole, whole),
-        scratch_shapes=[main_field, coeff, main_field, pltpu.VMEM((z.group, 512), BF16)],
+        scratch_shapes=[main_field, coeff, main_field, pltpu.VMEM((z.group, 512), BF16), square],
         name="main",
     )(alpha, members, kappa, norm_scale, land_sea, cell)
     mem_weight, inner = lax.optimization_barrier((mem_weight, inner))
@@ -503,6 +519,7 @@
             pltpu.VMEM((z.short, 128), F32),
             pltpu.VMEM((512, z.obs), BF16),
             pltpu.VMEM((z.field, 128), F32),
+            square,
             pltpu.SemaphoreType.DMA((z.levels // 2,)),
         ],
         name="adjoint",

time: 27.8 us -> 26.1 us (0.939)
  Pallas kernels: 16.9 us -> 15.3 us
    pallas_call x1, Pallas kernels: 4.18 us -> 3.33 us  [local(): call(functools.partial(main_kernel, z), out_shape=(sds((z.obs_rows, 128),...]
    ppermute x3, waiting for transfers between devices: 1.94 us -> 1.28 us  [local(): lax.ppermute(values, 'mem', [(i, i ^ k) for i in range(holders)])]
    ppermute x1, waiting for transfers between devices: 0.01 us -> 0.54 us  [local(): from_right = lax.ppermute(sent_left, 'tile', [(b, a) for a, b in up_ring])]
    pallas_call x1, Pallas kernels: 6.73 us -> 6.38 us  [local(): call(functools.partial(adjoint_kernel, z), out_shape=sds((z.field, z.colu...]
    pallas_call x1, Pallas kernels: 3.34 us -> 3.03 us  [local(): call(functools.partial(strip_kernel, z), out_shape=(sds((3 * z.obs_rows,...]
  transfers between devices with their start and end apart: 5 -> 5, of which waited for: 2 -> 3; matrix products, arithmetic and copies ran while one was open for 0% -> 0% of each run, Pallas kernels for 18% -> 16%
where the time goes in v8:
time: 26.1 us; the launch traced here: 25.9 us
  Pallas kernels  15.3 us (59%)
  starting transfers between devices  8.05 us (31%)
  waiting for transfers between devices  1.82 us (7%)
  between operations  0.7 us (3%)
    pallas_call x1, Pallas kernels, local(): call(functools.partial(adjoint_kernel, z), out_shape=sds((z.field, z.colu...  6.38 us
    pallas_call x1, Pallas kernels, local(): call(functools.partial(main_kernel, z), out_shape=(sds((z.obs_rows, 128),...  3.33 us
    ppermute x1, starting transfers between devices, local(): from_right = lax.ppermute(sent_left, 'tile', [(b, a) for a, b in up_ring])  3.1 us
    pallas_call x1, Pallas kernels, local(): call(functools.partial(strip_kernel, z), out_shape=(sds((3 * z.obs_rows,...  3.03 us
    ppermute x1, starting transfers between devices, local(): from_left = lax.ppermute(sent_right, 'tile', up_ring)  3.02 us
    ppermute x3, starting transfers between devices, local(): lax.ppermute(values, 'mem', [(i, i ^ k) for i in range(holders)])  1.93 us
    pallas_call x1, Pallas kernels, local(): call(functools.partial(pack_kernel, z), out_shape=(payload, payload, *(sd...  1.76 us
    ppermute x3, waiting for transfers between devices, local(): lax.ppermute(values, 'mem', [(i, i ^ k) for i in range(holders)])  1.28 us
  transfers between devices with their start and end apart: 5, of which 3 were waited for; matrix products, arithmetic and copies ran while one was open for 0% of the time, Pallas kernels for 16%

profile of v8, /device:TPU:0, one launch (start us, length us, event | category | flops | bytes accessed | tf_op | source)
XLA Modules:
  0.0 25.9 jit_solution(14039358871844717180)
XLA Ops:
  0.0 1.8 %pack.1 = (f32[248,128]{1,0:T(8,128)S(1)}, f32[248,128]{1,0:T(8,128)S(1)}, f32[1024,128]{1,0:T(8,128)S(1)}, bf16[1024,128]{1,0:T(8,128)(2,1)S(1)}, f32[64,128]{1...) custom-call(f32[1024,128]{1,0:T(8,128)} %bitcast.7, ...), custom_call_target="tpu_custom_call" | custom-call | tf_op jit(solution)/shard_map/pack/pallas_call | solution.py:461
  1.8 3.0 %collective-permute-start = (f32[248,128]{1,0:T(8,128)S(1)}, f32[248,128]{1,0:T(8,128)S(1)}, u32[]{:S(2)}, u32[]{:S(2)}) collective-permute-start(f32[248,128]{1,0:T(8,128)S(1)} %get-tuple-element.35.own_right), channel_id=1, source_target_pairs={{0,4},{4,8},{8,12},{12,16},{16,20},{20,24},{24,28},{28,0},{1,5},{5... | collective-permute-start | bytes 380936 | tf_op jit(solution)/shard_map/ppermute | solution.py:471
  4.8 3.1 %collective-permute-start.1 = (f32[248,128]{1,0:T(8,128)S(1)}, f32[248,128]{1,0:T(8,128)S(1)}, u32[]{:S(2)}, u32[]{:S(2)}) collective-permute-start(f32[248,128]{1,0:T(8,128)S(1)} %get-tuple-element.36.own_left), channel_id=1, source_target_pairs={{4,0},{8,4},{12,8},{16,12},{20,16},{24,20},{28,24},{0,28},{5,1},{9... | collective-permute-start | bytes 380936 | tf_op jit(solution)/shard_map/ppermute | solution.py:472
  8.5 3.3 %main.1 = (f32[16,128]{1,0:T(8,128)S(1)}, bf16[512,2048]{1,0:T(8,128)(2,1)S(1)}) custom-call(f32[1024,128]{1,0:T(8,128)S(1)} %get-tuple-element.26.alpha, bf16[1024,128]{1,0:T(8,128)(2,1)S(1)} %get-tuple-element.27.members, f32[64,128]{1,0:T(8,128)S(1)} %get-tuple-element.28.kappa, f32[64,128]{1,0:T(8,128)S(1)} %get-tuple-element.29.scale, ...), custom_call_target="tpu_custom_call" | custom-call | tf_op jit(solution)/shard_map/main/pallas_call | solution.py:473
  11.9 0.0 collective-permute-done.from_left
  11.9 0.5 %collective-permute-done.1.from_right = f32[248,128]{1,0:T(8,128)S(1)} collective-permute-done((f32[248,128]{1,0:T(8,128)S(1)}, f32[248,128]{1,0:T(8,128)S(1)}, u32[]{:S(2)}, u32[]{:S(2)}) %collective-permute-start.1) | collective-permute-done | bytes 127008 | tf_op jit(solution)/shard_map/ppermute | solution.py:472
  12.4 3.0 %strip.1 = (f32[48,128]{1,0:T(8,128)S(1)}, f32[512,128]{1,0:T(8,128)S(1)}, f32[3,64,128]{2,1,0:T(8,128)S(1)}, bf16[256,2048]{1,0:T(8,128)(2,1)S(1)}) custom-call(f32[16,128]{1,0:T(8,128)S(1)} %get-tuple-element.37.inner, bf16[1024,128]{1,0:T(8,128)(2,1)S(1)} %get-tuple-element.27.members, f32[248,128]{1,0:T(8,128)S(1)} %get-tuple-element.35.own_right, ...), custom_call_target="tpu_custom_call" | custom-call | tf_op jit(solution)/shard_map/strip/pallas_call | solution.py:483
  15.5 0.2 collective-permute-start.4
  15.7 1.4 %collective-permute-start.3 = (f32[48,128]{1,0:T(8,128)S(1)}, f32[48,128]{1,0:T(8,128)S(1)}, u32[]{:S(2)}, u32[]{:S(2)}) collective-permute-start(f32[48,128]{1,0:T(8,128)S(1)} %get-tuple-element.46.v0), channel_id=1, source_target_pairs={{0,2},{1,3},{2,0},{3,1},{4,6},{5,7},{6,4},{7,5},{8,10},{9,11},{10,... | collective-permute-start | bytes 73736 | tf_op jit(solution)/shard_map/ppermute | solution.py:496
  17.1 0.3 %collective-permute-start.2 = (f32[48,128]{1,0:T(8,128)S(1)}, f32[48,128]{1,0:T(8,128)S(1)}, u32[]{:S(2)}, u32[]{:S(2)}) collective-permute-start(f32[48,128]{1,0:T(8,128)S(1)} %get-tuple-element.46.v0), channel_id=1, source_target_pairs={{0,1},{1,0},{2,3},{3,2},{4,5},{5,4},{6,7},{7,6},{8,9},{9,8},{10,11... | collective-permute-start | bytes 73736 | tf_op jit(solution)/shard_map/ppermute | solution.py:496
  17.4 0.8 %ready.1 = (f32[5,64,128]{2,1,0:T(8,128)S(1)}, f32[5,64,128]{2,1,0:T(8,128)S(1)}, bf16[256,2048]{1,0:T(8,128)(2,1)S(1)}, bf16[128,2048]{1,0:T(8,128)(2,1)S(1)}) custom-call(f32[64,128]{1,0:T(8,128)S(1)} %get-tuple-element.28.kappa, f32[64,128]{1,0:T(8,128)S(1)} %get-tuple-element.29.scale, s32[64,128]{1,0:T(8,128)S(1)} %get-tuple-element.30.ocean, ...), custom_call_target="tpu_custom_call" | custom-call | tf_op jit(solution)/shard_map/ready/pallas_call | solution.py:497
  18.2 0.7 %collective-permute-done.4.v3 = f32[48,128]{1,0:T(8,128)S(1)} collective-permute-done((f32[48,128]{1,0:T(8,128)S(1)}, f32[48,128]{1,0:T(8,128)S(1)}, u32[]{:S(2)}, u32[]{:S(2)}) %collective-permute-start.4) | collective-permute-done | bytes 24608 | tf_op jit(solution)/shard_map/ppermute | solution.py:496
  19.0 0.5 %collective-permute-done.3.v2 = f32[48,128]{1,0:T(8,128)S(1)} collective-permute-done((f32[48,128]{1,0:T(8,128)S(1)}, f32[48,128]{1,0:T(8,128)S(1)}, u32[]{:S(2)}, u32[]{:S(2)}) %collective-permute-start.3) | collective-permute-done | bytes 24608 | tf_op jit(solution)/shard_map/ppermute | solution.py:496
  19.5 0.0 collective-permute-done.2.v1
  19.5 6.4 %adjoint.1 = f32[1024,128]{1,0:T(8,128)} custom-call(f32[1024,128]{1,0:T(8,128)S(1)} %get-tuple-element.26.alpha, bf16[1024,128]{1,0:T(8,128)(2,1)S(1)} %get-tuple-element.27.members, f32[8,128]{1,0:T(8,128)S(1)} %broadcast_in_dim.2.weight, f32[16,128]{1,0:T(8,128)S(1)} %get-tuple-element.34.obs_weight, f32[248,128]{1,0:T(8,128)S(1)} %collective-permute-done.from_left, ...), custom_call_target="tpu_custom_call" | custom-call | tf_op jit(solution)/shard_map/adjoint/pallas_call | solution.py:509
  (1 shorter events, 0.0 us)
Async XLA Ops:
  1.8 10.1 %collective-permute-start = (f32[248,128]{1,0:T(8,128)S(1)}, f32[248,128]{1,0:T(8,128)S(1)}, u32[]{:S(2)}, u32[]{:S(2)}) collective-permute-start(f32[248,128]{1,0:T(8,128)S(1)} %get-tuple-element.35.own_right), channel_id=1, source_target_pairs={{0,4},{4,8},{8,12},{12,16},{16,20},{20,24},{24,28},{28,0},{1,5},{5... | collective-permute-start | bytes 380936 | tf_op jit(solution)/shard_map/ppermute | solution.py:471
  4.8 7.6 %collective-permute-start.1 = (f32[248,128]{1,0:T(8,128)S(1)}, f32[248,128]{1,0:T(8,128)S(1)}, u32[]{:S(2)}, u32[]{:S(2)}) collective-permute-start(f32[248,128]{1,0:T(8,128)S(1)} %get-tuple-element.36.own_left), channel_id=1, source_target_pairs={{4,0},{8,4},{12,8},{16,12},{20,16},{24,20},{28,24},{0,28},{5,1},{9... | collective-permute-start | bytes 380936 | tf_op jit(solution)/shard_map/ppermute | solution.py:472
  15.5 3.5 %collective-permute-start.4 = (f32[48,128]{1,0:T(8,128)S(1)}, f32[48,128]{1,0:T(8,128)S(1)}, u32[]{:S(2)}, u32[]{:S(2)}) collective-permute-start(f32[48,128]{1,0:T(8,128)S(1)} %get-tuple-element.46.v0), channel_id=1, source_target_pairs={{0,3},{1,2},{2,1},{3,0},{4,7},{5,6},{6,5},{7,4},{8,11},{9,10},{10,... | collective-permute-start | bytes 73736 | tf_op jit(solution)/shard_map/ppermute | solution.py:496
  15.7 3.8 %collective-permute-start.3 = (f32[48,128]{1,0:T(8,128)S(1)}, f32[48,128]{1,0:T(8,128)S(1)}, u32[]{:S(2)}, u32[]{:S(2)}) collective-permute-start(f32[48,128]{1,0:T(8,128)S(1)} %get-tuple-element.46.v0), channel_id=1, source_target_pairs={{0,2},{1,3},{2,0},{3,1},{4,6},{5,7},{6,4},{7,5},{8,10},{9,11},{10,... | collective-permute-start | bytes 73736 | tf_op jit(solution)/shard_map/ppermute | solution.py:496
  17.1 2.4 %collective-permute-start.2 = (f32[48,128]{1,0:T(8,128)S(1)}, f32[48,128]{1,0:T(8,128)S(1)}, u32[]{:S(2)}, u32[]{:S(2)}) collective-permute-start(f32[48,128]{1,0:T(8,128)S(1)} %get-tuple-element.46.v0), channel_id=1, source_target_pairs={{0,1},{1,0},{2,3},{3,2},{4,5},{5,4},{6,7},{7,6},{8,9},{9,8},{10,11... | collective-permute-start | bytes 73736 | tf_op jit(solution)/shard_map/ppermute | solution.py:496

commit v9 on v8

--- a/solution.py
+++ b/solution.py
@@ -251,7 +251,17 @@
     sweep([(x, y, coeff, z.levels, shift)], z.rows)
 
 
-def main_kernel(z, alpha, members, kappa, scale, ocean, cell, out, hot, x, coeff, y, both, shift):
+def own_columns(pair, lane):
+    pieces = []
+    for g, value in enumerate(pair):
+        pieces += [roll(value, EDGE + 64 * g), roll(value, 48 + 64 * g)]
+    return overlay(pieces, (lane >> 6) * 2 + ((lane >> 5) & 1))
+
+
+def main_kernel(
+    z, alpha, members, kappa, scale, ocean, cell, out, hot, strip_x, strip_members, strip_coeff,
+    x, coeff, y, both, shift,
+):
     forward_sweep(z, alpha, kappa, scale, ocean, coeff, x, y, shift)
     lane = lanes(z.group)
     inner = (lane >= STEPS) & (lane < z.columns - STEPS)
@@ -262,48 +272,50 @@
         both[:, pl.ds(g * 128, 128)] = high
         both[:, pl.ds(256 + g * 128, 128)] = low
     gather(z, out, 0, both[...], cell[...], lambda c: own_index(z, c), hot)
+    block = 2 * SUB
+    lane = lanes(block)
+    for t in range(z.group // block):
+        rows = [pl.ds(g * z.group + t * block, block) for g in range(2)]
+        strip_x[pl.ds(t * block, block), :] = own_columns([alpha[r, :] for r in rows], lane)
+        strip_members[pl.ds(t * block, block), :] = own_columns([members[r, :].astype(F32) for r in rows], lane)
+    lane = lanes(z.rows)
+    for k, ref in enumerate((kappa, scale, ocean)):
+        value = ref[...].astype(F32)
+        strip_coeff[k] = own_columns([value, value], lane)
 
 
 def strip_kernel(
-    z, inner, members, own_right, own_left, from_left, from_right, cell, weight,
+    z, inner, own_x, own_members, own_coeff, from_left, from_right, cell, weight,
     out, strip_members, strip_coeff, hot, coeff, x, y, outer, beside,
 ):
-
-    def parts(rows):
-        return own_right[rows, :], from_right[rows, :], from_left[rows, :], own_left[rows, :]
-
     clear_ends(x, y)
     lane = lanes(SUB)
-    part_of, side = (lane >> 4) & 3, lane >> 6
+    part_of = (lane >> 4) & 3
     for k in range(3):
-        four = parts(pl.ds(z.at_coeff + k * SUB, SUB))
+        rows = pl.ds(z.at_coeff + k * SUB, SUB)
+        right, left = from_right[rows, :], from_left[rows, :]
         for t in range(z.tiles):
-            pieces = [roll(four[p], EDGE * p + 64 * g - EDGE * t) for g in range(2) for p in range(4)]
-            strip_coeff[k, pl.ds(t * SUB, SUB), :] = overlay(pieces, lane >> 4)
+            pieces = []
+            for g in range(2):
+                pieces += [roll(right, EDGE * (1 - t) + 64 * g), roll(left, EDGE * (2 - t) + 64 * g)]
+            value = overlay(pieces, (lane >> 6) * 2 + ((lane >> 5) & 1))
+            at = pl.ds(t * SUB, SUB)
+            strip_coeff[k, at, :] = jnp.where((part_of == 1) | (part_of == 2), value, own_coeff[k, at, :])
     for q in range(z.short // SUB):
-        four = parts(pl.ds(q * SUB, SUB))
+        right, left = from_right[pl.ds(q * SUB, SUB), :], from_left[pl.ds(q * SUB, SUB), :]
         for h in range(4):
-            pieces = [roll(four[p], EDGE * (p - h)) for p in range(4)]
-            x[pl.ds(SUB + h * z.short + q * SUB, SUB), :] = overlay(pieces, part_of)
-    block = 2 * SUB
-    wide_lane = lanes(block)
-    for t in range(z.rows // block):
-        rows = pl.ds(z.at_members + t * block, block)
-        _, right, left, _ = parts(rows)
+            at = h * z.short + q * SUB
+            value = jnp.where(part_of == 1, roll(right, EDGE * (1 - h)), own_x[pl.ds(at, SUB), :])
+            x[pl.ds(SUB + at, SUB), :] = jnp.where(part_of == 2, roll(left, EDGE * (2 - h)), value)
+    for t in range(z.tiles):
+        rows = pl.ds(z.at_members + t * SUB, SUB)
+        right, left = from_right[rows, :], from_left[rows, :]
         for part in range(SUB):
-            at = part * z.rows + t * block
-            value = jnp.where(
-                (wide_lane & 32) == 0,
-                roll(right, EDGE - STEPS * part),
-                roll(left, 2 * EDGE + STEPS - STEPS * part),
+            at = pl.ds(part * z.rows + t * SUB, SUB)
+            value = jnp.where(part_of == 1, roll(right, EDGE - STEPS * part), own_members[at, :])
+            strip_members[at, :] = jnp.where(
+                part_of == 2, roll(left, 2 * EDGE + STEPS - STEPS * part), value
             )
-            for g in range(2):
-                own = members[pl.ds(g * z.group + at, block), :].astype(F32)
-                mine = (wide_lane >> 6) == g
-                inside = (wide_lane >> 4) & 3
-                value = jnp.where(mine & (inside == 0), roll(own, EDGE + 64 * g), value)
-                value = jnp.where(mine & (inside == 3), roll(own, 48 + 64 * g), value)
-            strip_members[pl.ds(at, block), :] = value
     put_coefficients(coeff, coefficients(strip_coeff[0], strip_coeff[1], strip_coeff[2], True))
     sweep([(x, y, coeff, z.levels // 2, None)], z.rows)
     unit = lanes(z.short) >> 3
@@ -470,15 +482,20 @@
     up_ring = [(i, (i + 1) % tiles) for i in range(tiles)]
     from_left = lax.ppermute(sent_right, "tile", up_ring)
     from_right = lax.ppermute(sent_left, "tile", [(b, a) for a, b in up_ring])
-    inner, own_row = call(
+    inner, own_row, own_x, own_members, own_coeff = call(
         functools.partial(main_kernel, z),
-        out_shape=(sds((z.obs_rows, 128), F32), sds((z.group, z.obs), BF16)),
+        out_shape=(
+            sds((z.obs_rows, 128), F32),
+            sds((z.group, z.obs), BF16),
+            sds((z.group, 128), F32),
+            sds((z.group, 128), F32),
+            sds((3, z.rows, 128), F32),
+        ),
         in_specs=[whole] * 6,
-        out_specs=(whole, whole),
+        out_specs=(whole,) * 5,
         scratch_shapes=[main_field, coeff, main_field, pltpu.VMEM((z.group, 512), BF16), square],
         name="main",
     )(alpha, members, kappa, norm_scale, land_sea, cell)
-    mem_weight, inner = lax.optimization_barrier((mem_weight, inner))
     factor = jnp.broadcast_to(mem_weight, (SUB, 128))
     values, strip_members, strip_coeff, beside_row = call(
         functools.partial(strip_kernel, z),
@@ -492,7 +509,7 @@
         out_specs=(whole,) * 4,
         scratch_shapes=[coeff, strip_field, strip_field, packed, pltpu.VMEM((2 * z.short, 256), BF16)],
         name="strip",
-    )(inner, members, sent_right, sent_left, from_left, from_right, cell, factor)
+    )(inner, own_x, own_members, own_coeff, from_left, from_right, cell, factor)
     others = [lax.ppermute(values, "mem", [(i, i ^ k) for i in range(holders)]) for k in range(1, holders)]
     main_c, strip_c, own_lane, beside_lane = call(
         functools.partial(ready_kernel, z),

time: 26.1 us -> 25.9 us (level)
    pallas_call x1, Pallas kernels: 3.03 us -> 2.75 us  [local(): call(functools.partial(strip_kernel, z), out_shape=(sds((3 * z.obs_rows,...]
  transfers between devices with their start and end apart: 5 -> 5, of which waited for: 3 -> 3; matrix products, arithmetic and copies ran while one was open for 0% -> 0% of each run, Pallas kernels for 16% -> 17%
where the time goes in v9:
time: 25.9 us; the launch traced here: 25.7 us
  Pallas kernels  15.1 us (58%)
  starting transfers between devices  8.05 us (31%)
  waiting for transfers between devices  1.82 us (7%)
  between operations  0.7 us (3%)
    pallas_call x1, Pallas kernels, local(): call(functools.partial(adjoint_kernel, z), out_shape=sds((z.field, z.colu...  6.38 us
    pallas_call x1, Pallas kernels, local(): call(functools.partial(main_kernel, z), out_shape=(sds((z.obs_rows, 128),...  3.41 us
    ppermute x1, starting transfers between devices, local(): from_right = lax.ppermute(sent_left, 'tile', [(b, a) for a, b in up_ring])  3.1 us
    ppermute x1, starting transfers between devices, local(): from_left = lax.ppermute(sent_right, 'tile', up_ring)  3.02 us
    pallas_call x1, Pallas kernels, local(): call(functools.partial(strip_kernel, z), out_shape=(sds((3 * z.obs_rows,...  2.75 us
    ppermute x3, starting transfers between devices, local(): lax.ppermute(values, 'mem', [(i, i ^ k) for i in range(holders)])  1.93 us
    pallas_call x1, Pallas kernels, local(): call(functools.partial(pack_kernel, z), out_shape=(payload, payload, *(sd...  1.76 us
    ppermute x3, waiting for transfers between devices, local(): lax.ppermute(values, 'mem', [(i, i ^ k) for i in range(holders)])  1.35 us
  transfers between devices with their start and end apart: 5, of which 3 were waited for; matrix products, arithmetic and copies ran while one was open for 0% of the time, Pallas kernels for 17%

profile of v9, /device:TPU:0, one launch (start us, length us, event | category | flops | bytes accessed | tf_op | source)
XLA Modules:
  0.0 25.7 jit_solution(15216417389109706993)
XLA Ops:
  0.0 1.8 %pack.1 = (f32[248,128]{1,0:T(8,128)S(1)}, f32[248,128]{1,0:T(8,128)S(1)}, f32[1024,128]{1,0:T(8,128)S(1)}, bf16[1024,128]{1,0:T(8,128)(2,1)S(1)}, f32[64,128]{1...) custom-call(f32[1024,128]{1,0:T(8,128)} %bitcast.7, ...), custom_call_target="tpu_custom_call" | custom-call | tf_op jit(solution)/shard_map/pack/pallas_call | solution.py:473
  1.8 3.0 %collective-permute-start = (f32[248,128]{1,0:T(8,128)S(1)}, f32[248,128]{1,0:T(8,128)S(1)}, u32[]{:S(2)}, u32[]{:S(2)}) collective-permute-start(f32[248,128]{1,0:T(8,128)S(1)} %get-tuple-element.30), channel_id=1, source_target_pairs={{0,4},{4,8},{8,12},{12,16},{16,20},{20,24},{24,28},{28,0},{1,5},{5... | collective-permute-start | bytes 380936 | tf_op jit(solution)/shard_map/ppermute | solution.py:483
  4.8 3.1 %collective-permute-start.1 = (f32[248,128]{1,0:T(8,128)S(1)}, f32[248,128]{1,0:T(8,128)S(1)}, u32[]{:S(2)}, u32[]{:S(2)}) collective-permute-start(f32[248,128]{1,0:T(8,128)S(1)} %get-tuple-element.31), channel_id=1, source_target_pairs={{4,0},{8,4},{12,8},{16,12},{20,16},{24,20},{28,24},{0,28},{5,1},{9... | collective-permute-start | bytes 380936 | tf_op jit(solution)/shard_map/ppermute | solution.py:484
  8.5 3.4 %main.1 = (f32[16,128]{1,0:T(8,128)S(1)}, bf16[512,2048]{1,0:T(8,128)(2,1)S(1)}, f32[512,128]{1,0:T(8,128)S(1)}, f32[512,128]{1,0:T(8,128)S(1)}, f32[3,64,128]{2,1,0:T(8,128)S(1)}) custom-call(f32[1024,128]{1,0:T(8,128)S(1)} %get-tuple-element.27.alpha, bf16[1024,128]{1,0:T(8,128)(2,1)S(1)} %get-tuple-element.28.members, ...), custom_call_target="tpu_custom_call" | custom-call | tf_op jit(solution)/shard_map/main/pallas_call | solution.py:485
  12.0 0.0 collective-permute-done.from_left
  12.0 0.5 %collective-permute-done.1.from_right = f32[248,128]{1,0:T(8,128)S(1)} collective-permute-done((f32[248,128]{1,0:T(8,128)S(1)}, f32[248,128]{1,0:T(8,128)S(1)}, u32[]{:S(2)}, u32[]{:S(2)}) %collective-permute-start.1) | collective-permute-done | bytes 127008 | tf_op jit(solution)/shard_map/ppermute | solution.py:484
  12.4 2.7 %strip.1 = (f32[48,128]{1,0:T(8,128)S(1)}, f32[512,128]{1,0:T(8,128)S(1)}, f32[3,64,128]{2,1,0:T(8,128)S(1)}, bf16[256,2048]{1,0:T(8,128)(2,1)S(1)}) custom-call(f32[16,128]{1,0:T(8,128)S(1)} %get-tuple-element.36.inner, f32[512,128]{1,0:T(8,128)S(1)} %get-tuple-element.37.own_x, f32[512,128]{1,0:T(8,128)S(1)} %get-tuple-element.38.own_members, ...), custom_call_target="tpu_custom_call" | custom-call | tf_op jit(solution)/shard_map/strip/pallas_call | solution.py:500
  15.2 0.3 %collective-permute-start.4 = (f32[48,128]{1,0:T(8,128)S(1)}, f32[48,128]{1,0:T(8,128)S(1)}, u32[]{:S(2)}, u32[]{:S(2)}) collective-permute-start(f32[48,128]{1,0:T(8,128)S(1)} %get-tuple-element.48.v0), channel_id=1, source_target_pairs={{0,3},{1,2},{2,1},{3,0},{4,7},{5,6},{6,5},{7,4},{8,11},{9,10},{10,... | collective-permute-start | bytes 73736 | tf_op jit(solution)/shard_map/ppermute | solution.py:513
  15.5 1.4 %collective-permute-start.3 = (f32[48,128]{1,0:T(8,128)S(1)}, f32[48,128]{1,0:T(8,128)S(1)}, u32[]{:S(2)}, u32[]{:S(2)}) collective-permute-start(f32[48,128]{1,0:T(8,128)S(1)} %get-tuple-element.48.v0), channel_id=1, source_target_pairs={{0,2},{1,3},{2,0},{3,1},{4,6},{5,7},{6,4},{7,5},{8,10},{9,11},{10,... | collective-permute-start | bytes 73736 | tf_op jit(solution)/shard_map/ppermute | solution.py:513
  16.9 0.3 %collective-permute-start.2 = (f32[48,128]{1,0:T(8,128)S(1)}, f32[48,128]{1,0:T(8,128)S(1)}, u32[]{:S(2)}, u32[]{:S(2)}) collective-permute-start(f32[48,128]{1,0:T(8,128)S(1)} %get-tuple-element.48.v0), channel_id=1, source_target_pairs={{0,1},{1,0},{2,3},{3,2},{4,5},{5,4},{6,7},{7,6},{8,9},{9,8},{10,11... | collective-permute-start | bytes 73736 | tf_op jit(solution)/shard_map/ppermute | solution.py:513
  17.1 0.8 %ready.1 = (f32[5,64,128]{2,1,0:T(8,128)S(1)}, f32[5,64,128]{2,1,0:T(8,128)S(1)}, bf16[256,2048]{1,0:T(8,128)(2,1)S(1)}, bf16[128,2048]{1,0:T(8,128)(2,1)S(1)}) custom-call(f32[64,128]{1,0:T(8,128)S(1)} %get-tuple-element.32.kappa, f32[64,128]{1,0:T(8,128)S(1)} %get-tuple-element.33.scale, s32[64,128]{1,0:T(8,128)S(1)} %get-tuple-element.34.ocean, ...), custom_call_target="tpu_custom_call" | custom-call | tf_op jit(solution)/shard_map/ready/pallas_call | solution.py:514
  18.0 0.7 %collective-permute-done.4.v3 = f32[48,128]{1,0:T(8,128)S(1)} collective-permute-done((f32[48,128]{1,0:T(8,128)S(1)}, f32[48,128]{1,0:T(8,128)S(1)}, u32[]{:S(2)}, u32[]{:S(2)}) %collective-permute-start.4) | collective-permute-done | bytes 24608 | tf_op jit(solution)/shard_map/ppermute | solution.py:513
  18.7 0.6 %collective-permute-done.3.v2 = f32[48,128]{1,0:T(8,128)S(1)} collective-permute-done((f32[48,128]{1,0:T(8,128)S(1)}, f32[48,128]{1,0:T(8,128)S(1)}, u32[]{:S(2)}, u32[]{:S(2)}) %collective-permute-start.3) | collective-permute-done | bytes 24608 | tf_op jit(solution)/shard_map/ppermute | solution.py:513
  19.3 0.0 collective-permute-done.2.v1
  19.3 6.4 %adjoint.1 = f32[1024,128]{1,0:T(8,128)} custom-call(f32[1024,128]{1,0:T(8,128)S(1)} %get-tuple-element.27.alpha, bf16[1024,128]{1,0:T(8,128)(2,1)S(1)} %get-tuple-element.28.members, f32[8,128]{1,0:T(8,128)S(1)} %broadcast_in_dim.2.weight, f32[16,128]{1,0:T(8,128)S(1)} %get-tuple-element.29.obs_weight, f32[248,128]{1,0:T(8,128)S(1)} %collective-permute-done.from_left, ...), custom_call_target="tpu_custom_call" | custom-call | tf_op jit(solution)/shard_map/adjoint/pallas_call | solution.py:526
  (1 shorter events, 0.0 us)
Async XLA Ops:
  1.8 10.2 %collective-permute-start = (f32[248,128]{1,0:T(8,128)S(1)}, f32[248,128]{1,0:T(8,128)S(1)}, u32[]{:S(2)}, u32[]{:S(2)}) collective-permute-start(f32[248,128]{1,0:T(8,128)S(1)} %get-tuple-element.30), channel_id=1, source_target_pairs={{0,4},{4,8},{8,12},{12,16},{16,20},{20,24},{24,28},{28,0},{1,5},{5... | collective-permute-start | bytes 380936 | tf_op jit(solution)/shard_map/ppermute | solution.py:483
  4.8 7.6 %collective-permute-start.1 = (f32[248,128]{1,0:T(8,128)S(1)}, f32[248,128]{1,0:T(8,128)S(1)}, u32[]{:S(2)}, u32[]{:S(2)}) collective-permute-start(f32[248,128]{1,0:T(8,128)S(1)} %get-tuple-element.31), channel_id=1, source_target_pairs={{4,0},{8,4},{12,8},{16,12},{20,16},{24,20},{28,24},{0,28},{5,1},{9... | collective-permute-start | bytes 380936 | tf_op jit(solution)/shard_map/ppermute | solution.py:484
  15.2 3.5 %collective-permute-start.4 = (f32[48,128]{1,0:T(8,128)S(1)}, f32[48,128]{1,0:T(8,128)S(1)}, u32[]{:S(2)}, u32[]{:S(2)}) collective-permute-start(f32[48,128]{1,0:T(8,128)S(1)} %get-tuple-element.48.v0), channel_id=1, source_target_pairs={{0,3},{1,2},{2,1},{3,0},{4,7},{5,6},{6,5},{7,4},{8,11},{9,10},{10,... | collective-permute-start | bytes 73736 | tf_op jit(solution)/shard_map/ppermute | solution.py:513
  15.5 3.8 %collective-permute-start.3 = (f32[48,128]{1,0:T(8,128)S(1)}, f32[48,128]{1,0:T(8,128)S(1)}, u32[]{:S(2)}, u32[]{:S(2)}) collective-permute-start(f32[48,128]{1,0:T(8,128)S(1)} %get-tuple-element.48.v0), channel_id=1, source_target_pairs={{0,2},{1,3},{2,0},{3,1},{4,6},{5,7},{6,4},{7,5},{8,10},{9,11},{10,... | collective-permute-start | bytes 73736 | tf_op jit(solution)/shard_map/ppermute | solution.py:513
  16.9 2.5 %collective-permute-start.2 = (f32[48,128]{1,0:T(8,128)S(1)}, f32[48,128]{1,0:T(8,128)S(1)}, u32[]{:S(2)}, u32[]{:S(2)}) collective-permute-start(f32[48,128]{1,0:T(8,128)S(1)} %get-tuple-element.48.v0), channel_id=1, source_target_pairs={{0,1},{1,0},{2,3},{3,2},{4,5},{5,4},{6,7},{7,6},{8,9},{9,8},{10,11... | collective-permute-start | bytes 73736 | tf_op jit(solution)/shard_map/ppermute | solution.py:513
